TPU v7x, 32 devices: a whole 2x2x4 slice. The times are simulated.
32 devices in a mesh: fsdp: 8 (over z, y), tp: 4 (over x, core).
Axes of the slice: x: 2, y: 2, z: 4, core: 2. Of those that a mesh axis runs over, the one named last changes fastest.
Arguments:
- tokens: bfloat16 [32768, 768], P(('fsdp', 'tp')), may hold values from -16 to 16
- segment_ids: int32 [32, 1024], P('fsdp'), may hold values from 0 to 7, never falling along the last dimension, each value on 1 to 512 neighbouring positions
- valid: int32 [32768], P(('fsdp', 'tp')), may hold values from 0 to 1, as said below
- ln1_gain: bfloat16 [768], P('fsdp'), may hold values from 0.5 to 1.5
- ln1_bias: bfloat16 [768], P('fsdp'), may hold values from -3 to 3
- w_qkv: bfloat16 [768, 3, 768], P('fsdp', None, 'tp'), may hold values from -0.21875 to 0.21875
- w_out: bfloat16 [768, 768], P('tp', 'fsdp'), may hold values from -1.75 to 1.75
- ln2_gain: bfloat16 [768], P('fsdp'), may hold values from 0.5 to 1.5
- ln2_bias: bfloat16 [768], P('fsdp'), may hold values from -3 to 3
- w_up: bfloat16 [768, 3072], P('fsdp', 'tp'), may hold values from -0.21875 to 0.21875
- w_down: bfloat16 [3072, 768], P('tp', 'fsdp'), may hold values from -0.109375 to 0.109375
- cotangent: bfloat16 [32768, 768], P(('fsdp', 'tp')), may hold values from -6 to 6
Outputs:
- layer_output: bfloat16 [32768, 768], P(('fsdp', 'tp'))
- grad_tokens: float32 [32768, 768], P(('fsdp', 'tp'))
- grad_ln1_gain: float32 [768], P(('fsdp', 'tp'))
- grad_ln1_bias: float32 [768], P(('fsdp', 'tp'))
- grad_w_qkv: float32 [768, 3, 768], P('fsdp', None, 'tp')
- grad_w_out: float32 [768, 768], P('tp', 'fsdp')
- grad_ln2_gain: float32 [768], P(('fsdp', 'tp'))
- grad_ln2_bias: float32 [768], P(('fsdp', 'tp'))
- grad_w_up: float32 [768, 3072], P('fsdp', 'tp')
- grad_w_down: float32 [3072, 768], P('tp', 'fsdp')
- rms_values: float32 [3], replicated
Inputs may be any that keep to these rules, and one draw needn't show every extreme that they name: `segment_ids`: document numbers never fall along a sequence; each document has 1 to half of 1024 tokens. The first token of every sequence is valid.
All inputs are finite; a program needn't handle non-finite values.
Results may differ from a plain program's by a relative error of at most 0.018.
Values may be sent and summed in bfloat16 or wider, within the bound.
A program may use at most 192 MiB of HBM per device.

v0:
```python
from functools import partial

import jax
import jax.numpy as jnp
from jax import lax
from jax.sharding import PartitionSpec as P

HD = 64


epsilon = 1e-05
negative = -1e30


def split_up(array, dim, size):
    before, after = (array.shape[:dim], array.shape[dim + 1 :])
    return jnp.moveaxis(array.reshape(*before, size, -1, *after), dim, 0)


def sum_at_owner(array, axis, dim):
    blocks = split_up(array, dim, lax.axis_size(axis))
    arrived = lax.all_to_all(blocks, axis, split_axis=0, concat_axis=0, tiled=True)
    return arrived.astype(jnp.float32).sum(axis=0)


def layer_norm(values, gain, shift):
    center = values - jnp.mean(values, axis=-1, keepdims=True)
    variance = jnp.mean(center * center, axis=-1, keepdims=True)
    return center * lax.rsqrt(variance + epsilon) * gain + shift


def times_transposed(left, right):
    return lax.dot_general(
        left, right, (((1,), (1,)), ((), ())), preferred_element_type=jnp.float32
    )


def inner_rows(left, right):
    return lax.dot_general(
        left, right, (((0,), (0,)), ((), ())), preferred_element_type=jnp.float32
    )


def project_rows(left, right):
    return jnp.dot(left, right, preferred_element_type=jnp.float32)


def project_back(left, right):
    return times_transposed(left, right)


def block_scores(query, key, segment, start):
    rows = start + jnp.arange(query.shape[0], dtype=jnp.int32)
    columns = jnp.arange(key.shape[0], dtype=jnp.int32)
    row_segment = lax.dynamic_slice_in_dim(segment, start, query.shape[0], 0)
    allowed = (rows[:, None] >= columns[None, :]) & (row_segment[:, None] == segment[None, :])
    scores = jnp.einsum("qhd,khd->hqk", query, key, preferred_element_type=jnp.float32) * HD ** (
        -0.5
    )
    return jnp.where(allowed[None], scores, negative)


def attend_forward(triple, segment):
    length = segment.shape[0]
    block = min(512, length)
    starts = jnp.arange(length // block, dtype=jnp.int32) * block

    def one_block(start):
        query = lax.dynamic_slice_in_dim(triple[:, 0], start, block, 0)
        scores = block_scores(query, triple[:, 1], segment, start)
        top = jnp.max(scores, axis=-1, keepdims=True)
        unnormed = jnp.exp(scores - top)
        total = jnp.sum(unnormed, axis=-1, keepdims=True)
        probs = (unnormed / total).astype(jnp.bfloat16)
        context = jnp.einsum(
            "hqk,khd->qhd", probs, triple[:, 2], preferred_element_type=jnp.float32
        )
        return (context.astype(jnp.bfloat16), (top + jnp.log(total))[..., 0])

    context, logsum = lax.map(one_block, starts)
    return (context.reshape(length, context.shape[2], context.shape[3]), logsum)


def attend_backward(triple, segment, logsum, grad_context):
    query_all = triple[:, 0]
    key = triple[:, 1]
    value = triple[:, 2]
    block = logsum.shape[-1]
    starts = jnp.arange(logsum.shape[0], dtype=jnp.int32) * block

    def one_block(carry, piece):
        grad_key, grad_value = carry
        start, block_logsum = piece
        query = lax.dynamic_slice_in_dim(query_all, start, block, 0)
        grad_block = lax.dynamic_slice_in_dim(grad_context, start, block, 0)
        scores = block_scores(query, key, segment, start)
        probs = jnp.exp(scores - block_logsum[..., None])
        grad_value = grad_value + jnp.einsum(
            "hqk,qhd->khd",
            probs.astype(jnp.bfloat16),
            grad_block,
            preferred_element_type=jnp.float32,
        )
        grad_probs = jnp.einsum(
            "qhd,khd->hqk", grad_block, value, preferred_element_type=jnp.float32
        )
        grad_scores = (
            probs * (grad_probs - jnp.sum(grad_probs * probs, axis=-1, keepdims=True))
        ).astype(jnp.bfloat16)
        grad_query = jnp.einsum(
            "hqk,khd->qhd", grad_scores, key, preferred_element_type=jnp.float32
        ) * HD ** (-0.5)
        grad_key = grad_key + jnp.einsum(
            "hqk,qhd->khd", grad_scores, query, preferred_element_type=jnp.float32
        ) * HD ** (-0.5)
        return ((grad_key, grad_value), grad_query)

    empty = jnp.zeros(key.shape, jnp.float32)
    (grad_key, grad_value), grad_query = lax.scan(one_block, (empty, empty), (starts, logsum))
    grad_query = grad_query.reshape(key.shape)
    return jnp.stack([grad_query, grad_key, grad_value], axis=1).astype(jnp.bfloat16)


def head_group():
    return 3


def sequence_forward(item):
    triple, segment = item
    heads = triple.shape[2]
    group = head_group()

    def one_group(index):
        return attend_forward(triple, segment)

    context, logsum = lax.map(one_group, jnp.arange(heads // group, dtype=jnp.int32))
    return (jnp.moveaxis(context, 0, 1).reshape(triple.shape[0], heads * HD), logsum)


def sequence_backward(item):
    triple, segment, logsum, grad_context = item
    heads = triple.shape[2]
    group = head_group()

    def one_group(pair):
        index, group_logsum = pair
        return attend_backward(triple, segment, group_logsum, grad_context)

    grads = lax.map(one_group, (jnp.arange(heads // group, dtype=jnp.int32), logsum))
    return jnp.moveaxis(grads, 0, 2).reshape(triple.shape[0], 3 * heads * HD)


def attention_forward(whole, qkv_weight, segments):
    count, length = segments.shape
    heads = qkv_weight.shape[2] // HD
    flat = qkv_weight.reshape(qkv_weight.shape[0], -1)
    triples = jnp.dot(whole, flat, preferred_element_type=jnp.float32).astype(jnp.bfloat16)
    triples = triples.reshape(count, length, 3, heads, HD)
    context, logsum = lax.map(sequence_forward, (triples, segments))
    return (context.reshape(count * length, heads * HD), triples, logsum)


def attention_backward(triples, segments, logsum, grad_context):
    count, length = segments.shape
    heads = triples.shape[3]
    grad_seq = grad_context.reshape(count, length, heads, HD)
    grads = lax.map(sequence_backward, (triples, segments, logsum, grad_seq))
    return grads.reshape(count * length, 3 * heads * HD)


def local(
    tokens,
    segment_ids,
    valid,
    ln1_gain,
    ln1_bias,
    w_qkv,
    w_out,
    ln2_gain,
    ln2_bias,
    w_up,
    w_down,
    cotangent,
):
    local_rows, width = tokens.shape
    gathered = (
        lax.all_gather(ln1_gain, "fsdp", axis=0, tiled=True),
        lax.all_gather(ln1_bias, "fsdp", axis=0, tiled=True),
        lax.all_gather(w_qkv, "fsdp", axis=0, tiled=True),
        lax.all_gather(w_out, "fsdp", axis=1, tiled=True),
        lax.all_gather(ln2_gain, "fsdp", axis=0, tiled=True),
        lax.all_gather(ln2_bias, "fsdp", axis=0, tiled=True),
        lax.all_gather(w_up, "fsdp", axis=0, tiled=True),
        lax.all_gather(w_down, "fsdp", axis=1, tiled=True),
    )
    gain_one = gathered[0].astype(jnp.float32)
    shift_one = gathered[1].astype(jnp.float32)
    gain_two = gathered[4].astype(jnp.float32)
    shift_two = gathered[5].astype(jnp.float32)
    matrices = (gathered[2], gathered[3], gathered[6], gathered[7])
    resid_in = tokens.astype(jnp.float32)
    normed_one = layer_norm(resid_in, gain_one, shift_one).astype(jnp.bfloat16)
    whole_one = lax.all_gather(normed_one, "tp", axis=0, tiled=True)
    context, triples, logsum = attention_forward(whole_one, matrices[0], segment_ids)
    branch_attn = lax.psum_scatter(
        project_rows(context, matrices[1]).astype(jnp.bfloat16),
        "tp",
        scatter_dimension=0,
        tiled=True,
    ).astype(jnp.float32)
    middle = resid_in + branch_attn
    normed_two = layer_norm(middle, gain_two, shift_two).astype(jnp.bfloat16)
    whole_two = lax.all_gather(normed_two, "tp", axis=0, tiled=True)
    upper = jnp.dot(whole_two, matrices[2], preferred_element_type=jnp.float32)
    active = jax.nn.gelu(upper, approximate=True).astype(jnp.bfloat16)
    branch_mlp = lax.psum_scatter(
        project_rows(active, matrices[3]).astype(jnp.bfloat16),
        "tp",
        scatter_dimension=0,
        tiled=True,
    ).astype(jnp.float32)
    output = middle + branch_mlp
    weight_rows = valid.astype(jnp.float32)[:, None]
    sums = jnp.stack(
        [
            jnp.sum(weight_rows * output * output),
            jnp.sum(weight_rows * branch_attn * branch_attn),
            jnp.sum(weight_rows * branch_mlp * branch_mlp),
        ]
    )
    valid_count = jnp.sum(valid).astype(jnp.float32)
    again = (
        lax.all_gather(ln1_gain, "fsdp", axis=0, tiled=True),
        lax.all_gather(w_qkv, "fsdp", axis=0, tiled=True),
        lax.all_gather(w_out, "fsdp", axis=1, tiled=True),
        lax.all_gather(ln2_gain, "fsdp", axis=0, tiled=True),
        lax.all_gather(w_up, "fsdp", axis=0, tiled=True),
        lax.all_gather(w_down, "fsdp", axis=1, tiled=True),
    )
    gain_one = again[0].astype(jnp.float32)
    gain_two = again[3].astype(jnp.float32)
    matrices = (again[1], again[2], again[4], again[5])
    grad_branch = lax.all_gather(cotangent, "tp", axis=0, tiled=True)
    grad_active = times_transposed(grad_branch, matrices[3])
    gelu_back = jax.vjp(partial(jax.nn.gelu, approximate=True), upper)[1]
    grad_upper = gelu_back(grad_active)[0].astype(jnp.bfloat16)
    grad_down = inner_rows(active, grad_branch)
    grad_up = inner_rows(whole_two, grad_upper)
    grad_normed_two = lax.psum_scatter(
        project_back(grad_upper, matrices[2]).astype(jnp.bfloat16),
        "tp",
        scatter_dimension=0,
        tiled=True,
    ).astype(jnp.float32)
    norm_back_two = jax.vjp(layer_norm, middle, gain_two, shift_two)[1]
    grad_middle, grad_gain_two, grad_shift_two = norm_back_two(grad_normed_two)
    grad_middle = grad_middle + cotangent.astype(jnp.float32)
    grad_attn = grad_middle.astype(jnp.bfloat16)
    grad_attn_whole = lax.all_gather(grad_attn, "tp", axis=0, tiled=True)
    grad_context = times_transposed(grad_attn_whole, matrices[1]).astype(jnp.bfloat16)
    grad_outw = inner_rows(context, grad_attn_whole)
    grad_triples = attention_backward(triples, segment_ids, logsum, grad_context)
    qkv_flat = matrices[0].reshape(width, -1)
    grad_qkv = inner_rows(whole_one, grad_triples).reshape(matrices[0].shape)
    grad_normed_one = lax.psum_scatter(
        project_back(grad_triples, qkv_flat).astype(jnp.bfloat16),
        "tp",
        scatter_dimension=0,
        tiled=True,
    ).astype(jnp.float32)
    norm_back_one = jax.vjp(layer_norm, resid_in, gain_one, shift_one)[1]
    grad_input, grad_gain_one, grad_shift_one = norm_back_one(grad_normed_one)
    grad_tokens = grad_middle + grad_input
    grad_qkv, grad_outw, grad_up, grad_down = (
        sum_at_owner(grad_qkv.astype(jnp.bfloat16), "fsdp", 0),
        sum_at_owner(grad_outw.astype(jnp.bfloat16), "fsdp", 1),
        sum_at_owner(grad_up.astype(jnp.bfloat16), "fsdp", 0),
        sum_at_owner(grad_down.astype(jnp.bfloat16), "fsdp", 1),
    )
    norm_grads = jnp.stack([grad_gain_one, grad_shift_one, grad_gain_two, grad_shift_two])
    norm_total, sums_total, count_total = lax.psum((norm_grads, sums, valid_count), ("fsdp", "tp"))
    share = width // (lax.axis_size("fsdp") * lax.axis_size("tp"))
    owner = lax.axis_index("fsdp") * lax.axis_size("tp") + lax.axis_index("tp")
    norm_share = lax.dynamic_slice_in_dim(norm_total, owner * share, share, 1)
    spread = jnp.sqrt(sums_total / (count_total * width))
    return (
        output.astype(jnp.bfloat16),
        grad_tokens,
        norm_share[0],
        norm_share[1],
        grad_qkv,
        grad_outw,
        norm_share[2],
        norm_share[3],
        grad_up,
        grad_down,
        spread,
    )


def solution(mesh):
    placed = (
        P(("fsdp", "tp"), None),
        P("fsdp", None),
        P(("fsdp", "tp")),
        P("fsdp"),
        P("fsdp"),
        P("fsdp", None, "tp"),
        P("tp", "fsdp"),
        P("fsdp"),
        P("fsdp"),
        P("fsdp", "tp"),
        P("tp", "fsdp"),
        P(("fsdp", "tp"), None),
    )
    return jax.shard_map(
        local,
        mesh=mesh,
        in_specs=placed,
        out_specs=(
            P(("fsdp", "tp"), None),
            P(("fsdp", "tp"), None),
            P(("fsdp", "tp")),
            P(("fsdp", "tp")),
            P("fsdp", None, "tp"),
            P("tp", "fsdp"),
            P(("fsdp", "tp")),
            P(("fsdp", "tp")),
            P("fsdp", "tp"),
            P("tp", "fsdp"),
            P(),
        ),
        check_vma=False,
    )
```

profile of v0, /device:TPU:0, one launch (start us, length us, event | category | flops | bytes accessed | tf_op | source)
XLA Modules:
  0.0 970.5 jit_solution(11403954243379681484)
XLA Ops:
  13.4 23.9 %all-reduce.5 = (bf16[768]{0:T(1024)(128)(2,1)S(1)}, bf16[768]{0:T(1024)(128)(2,1)S(1)}, bf16[768]{0:T(1024)(128)(2,1)}, bf16[768]{0:T(1024)(128)(2,1)}) all-reduce(bf16[768]{0:T(1024)(128)(2,1)S(1)} %dynamic-update-slice.1, bf16[768]{0:T(1024)(128)(2,1)S(1)} %dynamic-update-slice, ...), channel_id=1, replica_groups=mesh['fsdp'=8,'tp'=4] {'fsdp'}, use_global_device_ids=true, to_apply=%add.1 | all-reduce | flops 3072 | bytes 12288
  44.5 35.2 %all_gather.45 = bf16[768,3,192]{2,1,0:T(4,128)(2,1)S(1)} all-gather(bf16[96,3,192]{2,1,0:T(4,128)(2,1)S(1)} %copy.44), channel_id=1, replica_groups=mesh['fsdp'=8,'tp'=4] {'fsdp'}, dimensions={0}, use_global_device_ids=true | all-gather | bytes 995328 | tf_op jit(solution)/shard_map/all_gather | solution.py:189
  80.6 33.6 %all_gather.46 = bf16[192,768]{0,1:T(8,128)(2,1)} all-gather(bf16[192,96]{0,1:T(8,128)(2,1)S(1)} %copy.48), channel_id=1, replica_groups=mesh['fsdp'=8,'tp'=4] {'fsdp'}, dimensions={1}, use_global_device_ids=true | all-gather | bytes 331776 | tf_op jit(solution)/shard_map/all_gather | solution.py:190
  114.2 8.3 convolution_convert_fusion.4
  122.5 8.8 reshape.280
  131.4 6.1 copy.46
  137.5 91.7 %while.68 = (s32[]{:T(128)}, bf16[4,1024,192]{1,2,0:T(8,128)(2,1)}, f32[4,1,2,3,512]{4,3,2,1,0:T(4,128)}, bf16[4,1024,3,3,64]{1,4,3,2,0:T(8,128)(2,1)}, s32[4,10...) while((s32[]{:T(128)}, bf16[4,1024,192]{1,2,0:T(8,128)(2,1)}, ...), condition=%wide.region_7.8_spmd, body=%wide.region_2.7_spmd.sunk | while | flops 423197696 | bytes 27767164 | solution.py:159
  139.6 18.7 %while.71 = (s32[]{:T(128)}, bf16[2,512,3,64]{1,3,2,0:T(8,128)(2,1)S(1)}, f32[2,3,512]{2,1,0:T(4,128)S(1)}, s32[2]{0:T(128)S(1)}, s32[1024]{0:T(1024)S(1)}, /*in...) while((s32[]{:T(128)}, bf16[2,512,3,64]{1,3,2,0:T(8,128)(2,1)S(1)}, ...), condition=%wide.region_6.6_spmd, body=%wide.region_3.5_spmd.sunk | while | flops 423197696 | bytes 23011496 | solution.py:80
  162.5 18.7 %while.71 = (s32[]{:T(128)}, bf16[2,512,3,64]{1,3,2,0:T(8,128)(2,1)S(1)}, f32[2,3,512]{2,1,0:T(4,128)S(1)}, s32[2]{0:T(128)S(1)}, s32[1024]{0:T(1024)S(1)}, /*in...) while((s32[]{:T(128)}, bf16[2,512,3,64]{1,3,2,0:T(8,128)(2,1)S(1)}, ...), condition=%wide.region_6.6_spmd, body=%wide.region_3.5_spmd.sunk | while | flops 423197696 | bytes 23011496 | solution.py:80
  185.5 18.7 %while.71 = (s32[]{:T(128)}, bf16[2,512,3,64]{1,3,2,0:T(8,128)(2,1)S(1)}, f32[2,3,512]{2,1,0:T(4,128)S(1)}, s32[2]{0:T(128)S(1)}, s32[1024]{0:T(1024)S(1)}, /*in...) while((s32[]{:T(128)}, bf16[2,512,3,64]{1,3,2,0:T(8,128)(2,1)S(1)}, ...), condition=%wide.region_6.6_spmd, body=%wide.region_3.5_spmd.sunk | while | flops 423197696 | bytes 23011496 | solution.py:80
  208.4 18.7 %while.71 = (s32[]{:T(128)}, bf16[2,512,3,64]{1,3,2,0:T(8,128)(2,1)S(1)}, f32[2,3,512]{2,1,0:T(4,128)S(1)}, s32[2]{0:T(128)S(1)}, s32[1024]{0:T(1024)S(1)}, /*in...) while((s32[]{:T(128)}, bf16[2,512,3,64]{1,3,2,0:T(8,128)(2,1)S(1)}, ...), condition=%wide.region_6.6_spmd, body=%wide.region_3.5_spmd.sunk | while | flops 423197696 | bytes 23011496 | solution.py:80
  232.0 4.5 convolution_convert_fusion.1
  239.2 55.9 %reduce-scatter.5.cloned.1.call-done = bf16[1024,768]{1,0:T(8,128)(2,1)} async-done(((bf16[4096,768]{1,0:T(8,128)(2,1)}), bf16[1024,768]{1,0:T(8,128)(2,1)}) %reduce-scatter.5.cloned.1.call-update) | async-done | bytes 1572880 | tf_op jit(solution)/shard_map/reduce_scatter | solution.py:205
  299.9 28.6 %all-gather.15.cloned.1.call-done = bf16[4096,768]{1,0:T(8,128)(2,1)} async-done(((bf16[1024,768]{1,0:T(8,128)(2,1)}), bf16[4096,768]{1,0:T(8,128)(2,1)}) %all-gather.15.cloned.1.call-update) | async-done | bytes 6291472 | tf_op jit(solution)/shard_map/all_gather | solution.py:243
  328.4 10.1 %fusion.83 = f32[4096,768]{1,0:T(8,128)} fusion(bf16[4096,768]{1,0:T(8,128)(2,1)} %all-gather.15.cloned.1.call-done, bf16[768,768]{0,1:T(8,128)(2,1)} %all-gather.13.cloned.1.call-done), kind=kOutput, calls=%fused_computation.159 | convolution fusion | flops 4831838208 | bytes 20054016 | tf_op jit(solution)/shard_map/dot_general | solution.py:33
  338.6 33.7 %all-gather.11.cloned.1.call-done = bf16[768,768]{1,0:T(8,128)(2,1)} async-done(((bf16[96,768]{1,0:T(8,128)(2,1)}), bf16[768,768]{1,0:T(8,128)(2,1)}) %all-gather.11.cloned.1.call-update) | async-done | bytes 1179664 | tf_op jit(solution)/shard_map/all_gather | solution.py:193
  372.3 47.0 %all-gather.9.cloned.1.call-done = bf16[4096,768]{1,0:T(8,128)(2,1)} async-done(((bf16[1024,768]{1,0:T(8,128)(2,1)}), bf16[4096,768]{1,0:T(8,128)(2,1)}) %all-gather.9.cloned.1.call-update) | async-done | bytes 6291472 | tf_op jit(solution)/shard_map/all_gather | solution.py:213
  419.3 21.0 %fusion.50 = (bf16[4096,768]{1,0:T(8,128)(2,1)S(1)}, f32[4096,768]{1,0:T(8,128)}) fusion(f32[4096,768]{1,0:T(8,128)} %fusion.83, bf16[4096,768]{1,0:T(8,128)(2,1)} %all-gather.9.cloned.1.call-done, bf16[768,768]{1,0:T(8,128)(2,1)} %all-gather.11.cloned.1.call-done), kind=kOutput, calls=%fused_computation.78 | convolution fusion | flops 4894752768 | bytes 38928384 | tf_op jit(solution)/shard_map/dot_general | solution.py:214
  440.3 2.7 copy-done.34
  443.0 7.0 convolution_convert_fusion.2
  450.3 12.5 %convolution_convert_fusion.3 = bf16[4096,768]{1,0:T(8,128)(2,1)} fusion(bf16[768,768]{0,1:T(8,128)(2,1)} %all-gather.13.cloned.1.call-done, f32[4096,768]{1,0:T(8,128)} %get-tuple-element.381), kind=kOutput, calls=%fused_computation.83 | convolution fusion | flops 4863295488 | bytes 20054016 | tf_op jit(solution)/shard_map/dot_general | solution.py:45
  464.9 43.7 %reduce-scatter.9.cloned.1.call-done = bf16[1024,768]{1,0:T(8,128)(2,1)} async-done(((bf16[4096,768]{1,0:T(8,128)(2,1)}), bf16[1024,768]{1,0:T(8,128)(2,1)}) %reduce-scatter.9.cloned.1.call-update) | async-done | bytes 1572880 | tf_op jit(solution)/shard_map/reduce_scatter | solution.py:249
  508.6 60.8 %reduce-scatter.7.cloned.1.call-done = bf16[1024,768]{1,0:T(8,128)(2,1)} async-done(((bf16[4096,768]{1,0:T(8,128)(2,1)}), bf16[1024,768]{1,0:T(8,128)(2,1)}) %reduce-scatter.7.cloned.1.call-update) | async-done | bytes 1572880 | tf_op jit(solution)/shard_map/reduce_scatter | solution.py:216
  569.4 6.4 fusion.66
  580.9 46.3 %all-gather.17.cloned.1.call-done = bf16[4096,768]{1,0:T(8,128)(2,1)} async-done(((bf16[1024,768]{1,0:T(8,128)(2,1)}), bf16[4096,768]{1,0:T(8,128)(2,1)}) %all-gather.17.cloned.1.call-update) | async-done | bytes 6291472 | tf_op jit(solution)/shard_map/all_gather | solution.py:259
  627.2 5.0 convolution_convert_fusion.5
  634.2 135.9 %while.70 = (s32[]{:T(128)}, bf16[4,1024,576]{1,2,0:T(8,128)(2,1)}, f32[4,1,2,3,512]{4,3,2,1,0:T(4,128)}, bf16[4,1024,3,3,64]{1,4,3,2,0:T(8,128)(2,1)}, bf16[4,1...) while((s32[]{:T(128)}, bf16[4,1024,576]{1,2,0:T(8,128)(2,1)}, ...), condition=%wide.region_19.20_spmd, body=%wide.region_15.19_spmd.sunk | while | flops 1034451968 | bytes 81621544 | solution.py:167
  637.9 27.7 %while.72 = (s32[]{:T(128)}, f32[1024,3,64]{0,2,1:T(8,128)S(1)}, f32[1024,3,64]{0,2,1:T(8,128)S(1)}, bf16[2,512,3,64]{1,3,2,0:T(8,128)(2,1)S(1)}, s32[2]{0:T(128...) while((s32[]{:T(128)}, f32[1024,3,64]{0,2,1:T(8,128)S(1)}, ...), condition=%wide.region_18.18_spmd.clone, body=%wide.region_16.17_spmd.clone.sunk | while | flops 1032879104 | bytes 54849764 | solution.py:119
  671.9 27.7 %while.72 = (s32[]{:T(128)}, f32[1024,3,64]{0,2,1:T(8,128)S(1)}, f32[1024,3,64]{0,2,1:T(8,128)S(1)}, bf16[2,512,3,64]{1,3,2,0:T(8,128)(2,1)S(1)}, s32[2]{0:T(128...) while((s32[]{:T(128)}, f32[1024,3,64]{0,2,1:T(8,128)S(1)}, ...), condition=%wide.region_18.18_spmd.clone, body=%wide.region_16.17_spmd.clone.sunk | while | flops 1032879104 | bytes 54849764 | solution.py:119
  679.3 2.6 multiply_reduce_fusion.3
  705.8 27.7 %while.72 = (s32[]{:T(128)}, f32[1024,3,64]{0,2,1:T(8,128)S(1)}, f32[1024,3,64]{0,2,1:T(8,128)S(1)}, bf16[2,512,3,64]{1,3,2,0:T(8,128)(2,1)S(1)}, s32[2]{0:T(128...) while((s32[]{:T(128)}, f32[1024,3,64]{0,2,1:T(8,128)S(1)}, ...), condition=%wide.region_18.18_spmd.clone, body=%wide.region_16.17_spmd.clone.sunk | while | flops 1032879104 | bytes 54849764 | solution.py:119
  713.3 2.6 multiply_reduce_fusion.3
  739.8 27.7 %while.72 = (s32[]{:T(128)}, f32[1024,3,64]{0,2,1:T(8,128)S(1)}, f32[1024,3,64]{0,2,1:T(8,128)S(1)}, bf16[2,512,3,64]{1,3,2,0:T(8,128)(2,1)S(1)}, s32[2]{0:T(128...) while((s32[]{:T(128)}, f32[1024,3,64]{0,2,1:T(8,128)S(1)}, ...), condition=%wide.region_18.18_spmd.clone, body=%wide.region_16.17_spmd.clone.sunk | while | flops 1032879104 | bytes 54849764 | solution.py:119
  770.1 3.0 copy.58
  775.3 7.2 convolution_convert_fusion
  782.5 12.6 %convolution_convert_fusion.6 = bf16[768,768]{0,1:T(8,128)(2,1)} fusion(bf16[4096,768]{1,0:T(8,128)(2,1)} %all-gather.15.cloned.1.call-done, f32[4096,768]{1,0:T(8,128)} %get-tuple-element.381), kind=kOutput, calls=%fused_computation.133 | convolution fusion | flops 4860739584 | bytes 20054016 | tf_op jit(solution)/shard_map/dot_general | solution.py:39
  795.1 5.5 all-to-all-start.3
  800.6 10.8 %convolution_convert_fusion.7 = bf16[768,768]{1,0:T(8,128)(2,1)} fusion(bf16[4096,768]{1,0:T(8,128)(2,1)} %all-gather.9.cloned.1.call-done, bf16[4096,768]{1,0:T(8,128)(2,1)} %copy-done.34), kind=kOutput, calls=%fused_computation.134 | convolution fusion | flops 4832428032 | bytes 13762560 | tf_op jit(solution)/shard_map/dot_general | solution.py:39
  811.5 18.1 %all-to-all-done.3 = bf16[8,768,96]{1,2,0:T(8,128)(2,1)S(1)} async-done(((bf16[8,768,96]{1,2,0:T(8,128)(2,1)}), bf16[8,768,96]{1,2,0:T(8,128)(2,1)S(1)}, u32[]{:S(2)}, u32[]{:S(2)}) %all-to-all-start.3) | async-done | bytes 1179680 | tf_op jit(solution)/shard_map/all_to_all | solution.py:22
  829.6 4.2 all-to-all-start.2
  833.9 4.2 convolution_convert_fusion.8
  839.3 22.9 %all-to-all-done.2 = bf16[8,96,768]{2,1,0:T(8,128)(2,1)} async-done(((bf16[8,96,768]{2,1,0:T(8,128)(2,1)}), bf16[8,96,768]{2,1,0:T(8,128)(2,1)}, u32[]{:S(2)}, u32[]{:S(2)}) %all-to-all-start.2) | async-done | bytes 1179680 | tf_op jit(solution)/shard_map/all_to_all | solution.py:22
  862.2 3.7 all-to-all-start.1
  865.9 8.9 fusion.76
  878.6 6.1 all-to-all-start
  891.3 21.8 %all-to-all-done = bf16[8,96,3,192]{1,3,2,0:T(8,128)(2,1)} async-done(((bf16[8,96,3,192]{1,3,2,0:T(8,128)(2,1)}), bf16[8,96,3,192]{1,3,2,0:T(8,128)(2,1)}, u32[]{:S(2)}, u32[]{:S(2)}) %all-to-all-start) | async-done | bytes 884768 | tf_op jit(solution)/shard_map/all_to_all | solution.py:22
  919.8 37.1 %all-reduce.4 = (f32[4,768]{1,0:T(4,128)S(1)}, f32[3]{0:T(128)S(1)}, f32[]{:T(128)}) all-reduce(f32[4,768]{1,0:T(4,128)S(1)} %pad_maximum_fusion.1, f32[3]{0:T(128)S(1)} %pad_maximum_fusion.2, f32[]{:T(128)S(6)} %convert_element_type.156), channel_id=1, replica_groups=mesh['fsdp'=8,'tp'=4] {'fsdp','tp'}, use_global_device_ids=true, to_apply=%region_27.28 | all-reduce | flops 3076 | bytes 24608 | tf_op jit(solution)/shard_map/psum | solution.py:281
  958.8 4.4 add_add_fusion.2
  (414 shorter events, 243.8 us)
Async XLA Ops:
  8.0 34.4 %copy-start = (bf16[1024,768]{1,0:T(8,128)(2,1)S(1)}, bf16[1024,768]{1,0:T(8,128)(2,1)}, u32[]{:S(2)}) copy-start(bf16[1024,768]{1,0:T(8,128)(2,1)} %param.20) | copy-start | bytes 4718596
  8.0 106.2 %all-gather.7.cloned.1.call-start = ((), (), s32[]{:S(2)}) async-start(), calls=%async_computation.8 | async-start | bytes 7864320 | tf_op jit(solution)/shard_map/all_gather | solution.py:203
  37.4 4.4 copy-start.19
  39.1 2.7 copy-start.16
  39.1 5.1 copy-start.23
  39.1 5.3 copy-start.18
  44.2 250.9 %reduce-scatter.5.cloned.1.call-start = ((), (), s32[]{:S(2)}) async-start(), calls=%async_computation.9 | async-start | bytes 7864320 | tf_op jit(solution)/shard_map/reduce_scatter | solution.py:205
  80.6 41.9 %copy-start.14 = (bf16[768,3,192]{0,2,1:T(8,128)(2,1)}, bf16[768,3,192]{0,2,1:T(8,128)(2,1)S(1)}, u32[]{:S(2)}) copy-start(bf16[768,3,192]{0,2,1:T(8,128)(2,1)S(1)} %copy.45) | copy-start | bytes 2654212
  229.2 2.8 copy-start.13
  236.5 2.0 copy-start.32
  236.5 2.0 copy-start.31
  236.5 58.5 %copy-start.1 = (bf16[1024,768]{1,0:T(8,128)(2,1)S(1)}, bf16[1024,768]{1,0:T(8,128)(2,1)}, u32[]{:S(2)}) copy-start(bf16[1024,768]{1,0:T(8,128)(2,1)} %param.20) | copy-start | bytes 4718596
  236.6 63.3 %all-gather.13.cloned.1.call-start = ((), (), s32[]{:S(2)}) async-start(), calls=%async_computation.12 | async-start | bytes 1327104 | tf_op jit(solution)/shard_map/all_gather | solution.py:194
  237.1 91.3 %all-gather.15.cloned.1.call-start = ((), (), s32[]{:S(2)}) async-start(), calls=%async_computation.14 | async-start | bytes 7864320 | tf_op jit(solution)/shard_map/all_gather | solution.py:243
  237.7 134.6 %all-gather.11.cloned.1.call-start = ((), (), s32[]{:S(2)}) async-start(), calls=%async_computation.11 | async-start | bytes 1327104 | tf_op jit(solution)/shard_map/all_gather | solution.py:193
  238.3 181.0 %all-gather.9.cloned.1.call-start = ((), (), s32[]{:S(2)}) async-start(), calls=%async_computation.10 | async-start | bytes 7864320 | tf_op jit(solution)/shard_map/all_gather | solution.py:213
  295.0 2.0 copy-start.3
  295.0 2.8 copy-start.30
  299.8 208.8 %reduce-scatter.9.cloned.1.call-start = ((), (), s32[]{:S(2)}) async-start(), calls=%async_computation.15 | async-start | bytes 7864320 | tf_op jit(solution)/shard_map/reduce_scatter | solution.py:249
  419.3 23.8 %copy-start.33 = (bf16[768,768]{1,0:T(8,128)(2,1)S(1)}, bf16[768,768]{1,0:T(8,128)(2,1)}, u32[]{:S(2)}) copy-start(bf16[768,768]{1,0:T(8,128)(2,1)} %all-gather.11.cloned.1.call-done) | copy-start | bytes 3538948
  440.3 2.7 copy-start.34
  450.1 119.3 %reduce-scatter.7.cloned.1.call-start = ((), (), s32[]{:S(2)}) async-start(), calls=%async_computation.13 | async-start | bytes 7864320 | tf_op jit(solution)/shard_map/reduce_scatter | solution.py:216
  462.8 164.3 %all-gather.17.cloned.1.call-start = ((), (), s32[]{:S(2)}) async-start(), calls=%async_computation.16 | async-start | bytes 7864320 | tf_op jit(solution)/shard_map/all_gather | solution.py:259
  569.4 6.5 copy-start.11
  575.9 3.3 copy-start.6
  580.8 334.7 %reduce-scatter.11.cloned.1.call-start = ((), (), s32[]{:S(2)}) async-start(), calls=%async_computation.17 | async-start | bytes 7864320 | tf_op jit(solution)/shard_map/reduce_scatter | solution.py:265
  634.2 2.1 copy-start.9
  666.4 1.8 copy-start.10
  668.2 2.1 copy-start.9
  700.4 1.8 copy-start.10
  702.2 2.1 copy-start.9
  736.1 2.1 copy-start.9
  770.1 5.2 copy-start.15
  773.1 2.2 copy-start.12
  795.1 34.5 %all-to-all-start.3 = ((bf16[8,768,96]{1,2,0:T(8,128)(2,1)}), bf16[8,768,96]{1,2,0:T(8,128)(2,1)S(1)}, u32[]{:S(2)}, u32[]{:S(2)}) async-start(bf16[8,768,96]{1,2,0:T(8,128)(2,1)} %bitcast.32), calls=%async_computation.7 | async-start | bytes 2359296 | tf_op jit(solution)/shard_map/all_to_all | solution.py:22
  800.6 33.3 %copy-start.8 = (bf16[4,24,8,1024]{3,2,0,1:T(8,128)(2,1)S(1)}, bf16[4,24,8,1024]{3,2,0,1:T(8,128)(2,1)}, u32[]{:S(2)}) copy-start(bf16[4,24,8,1024]{3,2,0,1:T(8,128)(2,1)} %copy-done.7) | copy-start | bytes 4718596
  829.6 32.6 %all-to-all-start.2 = ((bf16[8,96,768]{2,1,0:T(8,128)(2,1)}), bf16[8,96,768]{2,1,0:T(8,128)(2,1)}, u32[]{:S(2)}, u32[]{:S(2)}) async-start(bf16[8,96,768]{2,1,0:T(8,128)(2,1)} %bitcast.191), calls=%async_computation.6 | async-start | bytes 2359296 | tf_op jit(solution)/shard_map/all_to_all | solution.py:22
  862.2 16.4 %all-to-all-start.1 = ((bf16[8,192,96]{2,1,0:T(8,128)(2,1)}), bf16[8,192,96]{2,1,0:T(8,128)(2,1)S(1)}, u32[]{:S(2)}, u32[]{:S(2)}) async-start(bf16[8,192,96]{2,1,0:T(8,128)(2,1)} %bitcast.130), calls=%async_computation.5 | async-start | bytes 786432 | tf_op jit(solution)/shard_map/all_to_all | solution.py:22
  878.5 10.0 %copy-start.29 = (f32[768]{0:T(1024)S(1)}, f32[768]{0:T(1024)}, u32[]{:S(2)}) copy-start(f32[768]{0:T(1024)} %get-tuple-element.290) | copy-start | bytes 9220
  878.6 10.0 %copy-start.28 = (f32[768]{0:T(1024)S(1)}, f32[768]{0:T(1024)}, u32[]{:S(2)}) copy-start(f32[768]{0:T(1024)} %get-tuple-element.295) | copy-start | bytes 9220
  878.6 34.5 %all-to-all-start = ((bf16[8,96,3,192]{1,3,2,0:T(8,128)(2,1)}), bf16[8,96,3,192]{1,3,2,0:T(8,128)(2,1)}, u32[]{:S(2)}, u32[]{:S(2)}) async-start(bf16[8,96,3,192]{1,3,2,0:T(8,128)(2,1)} %copy.52), calls=%async_computation.4 | async-start | bytes 2359296 | tf_op jit(solution)/shard_map/all_to_all | solution.py:22
  884.7 30.8 %copy-start.2 = (bf16[1024,768]{1,0:T(8,128)(2,1)S(1)}, bf16[1024,768]{1,0:T(8,128)(2,1)}, u32[]{:S(2)}) copy-start(bf16[1024,768]{1,0:T(8,128)(2,1)} %param.20) | copy-start | bytes 4718596
  884.7 30.8 %copy-start.17 = (f32[1024]{0:T(1024)S(1)}, f32[1024]{0:T(1024)}, u32[]{:S(2)}) copy-start(f32[1024]{0:T(1024)} %copy-done.16) | copy-start | bytes 12292
  884.7 30.8 %copy-start.20 = (f32[768]{0:T(1024)S(1)}, f32[768]{0:T(1024)}, u32[]{:S(2)}) copy-start(f32[768]{0:T(1024)} %copy-done.19) | copy-start | bytes 9220
  888.5 29.4 %copy-start.25 = (f32[1024]{0:T(1024)S(1)}, f32[1024]{0:T(1024)}, u32[]{:S(2)}) copy-start(f32[1024]{0:T(1024)} %copy-done.24) | copy-start | bytes 12292
  888.5 29.4 %copy-start.22 = (f32[1024]{0:T(1024)S(1)}, f32[1024]{0:T(1024)}, u32[]{:S(2)}) copy-start(f32[1024]{0:T(1024)} %copy-done.21) | copy-start | bytes 12292
  915.5 43.3 %copy-start.27 = (f32[1024]{0:T(1024)S(1)}, f32[1024]{0:T(1024)}, u32[]{:S(2)}) copy-start(f32[1024]{0:T(1024)} %copy-done.26) | copy-start | bytes 12292
  915.5 2.4 copy-start.5
  (7 other events, 9.3 us)
Sparse Core Ops, SparseCore 0:
  44.3 43.6 all-gather.6
  236.7 58.3 reduce-scatter.4
  450.2 58.3 reduce-scatter.8
  511.0 58.3 reduce-scatter.6
Sparse Core Ops, SparseCore 1:
  239.5 41.2 all-gather.12
  282.2 46.2 all-gather.14
  330.7 41.5 all-gather.10
  374.5 44.7 all-gather.8
  580.9 46.2 all-gather.16
  782.6 58.2 reduce-scatter.10
where the time goes:
time: 978 us; the launch traced here: 970 us
  waiting for transfers between devices  381 us (39%)
  matrix products  203 us (21%)
  blocking collectives  130 us (13%)
  local copies, waits for them, and re-layouts  99.8 us (10%)
  other arithmetic  87.3 us (9%)
  loops' own time  31.5 us (3%)
  starting transfers between devices  20.4 us (2%)
  between operations  18.1 us (2%)
    all_to_all x4, waiting for transfers between devices, sum_at_owner(): lax.all_to_all(blocks, axis, split_axis=0, concat_axis=0, tiled=True)  62.8 us
    reduce_scatter x1, waiting for transfers between devices, local(): lax.psum_scatter(project_rows(active, matrices[3]).astype(jnp.bfloat16),...  60.8 us
    reduce_scatter x1, waiting for transfers between devices, local(): lax.psum_scatter(project_rows(context, matrices[1]).astype(jnp.bfloat16),...  55.9 us
    all_gather x1, waiting for transfers between devices, local(): whole_two = lax.all_gather(normed_two, 'tp', axis=0, tiled=True)  47 us
    all_gather x1, waiting for transfers between devices, local(): grad_attn_whole = lax.all_gather(grad_attn, 'tp', axis=0, tiled=True)  46.3 us
    reduce_scatter x1, waiting for transfers between devices, local(): lax.psum_scatter(project_back(grad_upper, matrices[2]).astype(jnp.bfloat1...  43.7 us
    psum x1, blocking collectives, local(): lax.psum((norm_grads, sums, valid_count), ('fsdp', 'tp'))  37.1 us
    dot_general x4, matrix products, inner_rows(): lax.dot_general(left, right, (((0,), (0,)), ((), ())), preferred_element_...  36.5 us
  transfers between devices with their start and end apart: 14, of which 10 were waited for; matrix products, arithmetic and copies ran while one was open for 8% of the time, Pallas kernels for 0%

commit v1 on v0

v1 whole, which is shorter than its diff:
```python
from functools import partial

import jax
import jax.numpy as jnp
from jax import lax
from jax.experimental import pallas as pl
from jax.experimental.pallas import tpu as pltpu
from jax.sharding import PartitionSpec as P

HD = 64
BQ = 256
EPS = 1e-05
BIG = -1e30
F32 = jnp.float32
BF = jnp.bfloat16
NN = (((1,), (0,)), ((), ()))
NT = (((1,), (1,)), ((), ()))
TN = (((0,), (0,)), ((), ()))
MESH = pl.DeviceIdType.MESH
C0 = 0.7978845608
C1 = 0.7978845608 * 0.044715


def dot(a, b, dims=NN):
    return lax.dot_general(a, b, dims, preferred_element_type=F32)


def remote(src, dst, send, recv, device):
    return pltpu.make_async_remote_copy(
        src_ref=src, dst_ref=dst, send_sem=send, recv_sem=recv,
        device_id=device, device_id_type=MESH,
    )


class Place:
    def __init__(self, inner):
        f = lax.axis_index("fsdp")
        t = lax.axis_index("tp")
        g = f // inner
        self.low = f % inner
        self.inner = inner
        self.z, self.y, self.x, self.c = g // 2, g % 2, t // 2, t % 2

    def device(self, z, y, x, c):
        return ((z * 2 + y) * self.inner + self.low, x * 2 + c)

    def core(self):
        return self.device(self.z, self.y, self.x, 1 - self.c)

    def xn(self):
        return self.device(self.z, self.y, 1 - self.x, self.c)

    def yn(self):
        return self.device(self.z, 1 - self.y, self.x, self.c)

    def zn(self, d):
        return self.device((self.z + d) % 4, self.y, self.x, self.c)

    def zp(self, d):
        return self.device((self.z - d + 4) % 4, self.y, self.x, self.c)


def barrier(inner):
    p = Place(inner)
    sem = pltpu.get_barrier_semaphore()
    for dev in (p.core(), p.xn(), p.yn(), p.zn(1), p.zn(2), p.zn(3)):
        pl.semaphore_signal(sem, inc=1, device_id=dev, device_id_type=MESH)
    pl.semaphore_wait(sem, 6)


class Gather:
    def __init__(self, inner, buf, row0, rows, send, recv):
        self.inner, self.buf, self.row0, self.rows = inner, buf, row0, rows
        self.send, self.recv = send, recv

    def own(self, x, c, z, y):
        return self.buf.at[x, c, z, y, pl.ds(self.row0, self.rows)]

    def group(self, x, c, y, half=None):
        start, size = self.row0, self.rows
        if half is not None:
            size = self.rows // 2
            start = self.row0 + half * size
        return self.buf.at[x, c, :, y, pl.ds(start, size)]

    def parts(self, slot):
        p = Place(self.inner)
        x, c, z, y = p.x, p.c, p.z, p.y
        if slot < 3:
            d = slot + 1
            return self.own(x, c, z, y), self.own(x, c, (z - d + 4) % 4, y), p.zn(d)
        if slot == 3:
            return self.group(x, c, y), self.group(1 - x, c, y), p.xn()
        if slot == 4:
            return self.group(x, c, y), self.group(x, c, 1 - y), p.yn()
        if slot == 5:
            return self.group(1 - x, c, y, 0), self.group(1 - x, c, 1 - y, 0), p.yn()
        if slot == 6:
            return self.group(x, c, 1 - y, 1), self.group(1 - x, c, 1 - y, 1), p.xn()
        xx = x if slot in (7, 9) else 1 - x
        yy = y if slot in (7, 8) else 1 - y
        return self.group(xx, c, yy), self.group(xx, 1 - c, yy), p.core()

    def start(self, *slots):
        for slot in slots:
            mine, _, dev = self.parts(slot)
            remote(mine, mine, self.send.at[slot], self.recv.at[slot], dev).start()

    def arrive(self, *slots):
        for slot in slots:
            _, theirs, dev = self.parts(slot)
            remote(theirs, theirs, self.send.at[slot], self.recv.at[slot], dev).wait_recv()

    def left(self, *slots):
        for slot in slots:
            mine, _, dev = self.parts(slot)
            remote(mine, mine, self.send.at[slot], self.recv.at[slot], dev).wait_send()

    def s1(self):
        self.start(0, 1, 2)

    def s2(self):
        self.arrive(0, 1, 2)
        self.start(3, 4, 7)

    def s3(self):
        self.arrive(3)
        self.start(5, 8)
        self.arrive(4)
        self.start(6, 9)

    def s4(self):
        self.arrive(5, 6)
        self.start(10)

    def s5(self):
        self.arrive(7, 8, 9, 10)

    def s6(self):
        self.left(*range(11))


class Scatter:
    def __init__(self, inner, buf, rows, slots, send, recv, credit, out):
        self.inner, self.buf, self.rows = inner, buf, rows
        self.slots, self.send, self.recv = slots, send, recv
        self.credit, self.out = credit, out

    def parts(self, slot):
        p = Place(self.inner)
        x, c, z, y = p.x, p.c, p.z, p.y
        buf, half = self.buf, self.rows // 2
        r1, ra, rb, rx, ry, rz = self.slots
        whole, cut = pl.ds(0, self.rows), pl.ds(0, half)
        if slot == 0:
            return buf.at[:, 1 - c], r1.at[:, :, :, whole], p.core()
        if slot == 1:
            return buf.at[1 - x, c, :, 1 - y, pl.ds(0, half)], ra.at[:, cut], p.yn()
        if slot == 2:
            return buf.at[1 - x, c, :, 1 - y, pl.ds(half, half)], rb.at[:, cut], p.xn()
        if slot == 3:
            return buf.at[1 - x, c, :, y], rx.at[:, whole], p.xn()
        if slot == 4:
            return buf.at[x, c, :, 1 - y], ry.at[:, whole], p.yn()
        d = slot - 4
        return buf.at[x, c, (z + d) % 4, y], rz.at[d - 1, whole], p.zn(d)

    def start(self, *slots):
        for slot in slots:
            src, dst, dev = self.parts(slot)
            remote(src, dst, self.send.at[slot], self.recv.at[slot], dev).start()

    def arrive(self, *slots):
        for slot in slots:
            _, dst, dev = self.parts(slot)
            remote(dst, dst, self.send.at[slot], self.recv.at[slot], dev).wait_recv()

    def left(self):
        for slot in range(8):
            src, dst, dev = self.parts(slot)
            remote(src, dst, self.send.at[slot], self.recv.at[slot], dev).wait_send()

    def take_credit(self):
        for i in range(6):
            pl.semaphore_wait(self.credit.at[i], 1)

    def give_credit(self):
        p = Place(self.inner)
        for i, dev in enumerate((p.core(), p.xn(), p.yn(), p.zp(1), p.zp(2), p.zp(3))):
            pl.semaphore_signal(self.credit.at[i], inc=1, device_id=dev, device_id_type=MESH)

    def s1(self):
        self.start(0)

    def add_core(self, x, y):
        c = Place(self.inner).c
        r1 = self.slots[0]

        @pl.loop(0, 4)
        def _(z):
            got = r1[x, z, y, 0 : self.rows].astype(F32)
            self.buf[x, c, z, y] = (self.buf[x, c, z, y].astype(F32) + got).astype(BF)

    def s2(self):
        p = Place(self.inner)
        x, y = p.x, p.y
        self.arrive(0)
        self.add_core(1 - x, 1 - y)
        self.start(1, 2)
        self.add_core(1 - x, y)
        self.add_core(x, 1 - y)
        self.add_core(x, y)

    def s3(self):
        p = Place(self.inner)
        x, y, c = p.x, p.y, p.c
        buf, half = self.buf, self.rows // 2
        _, ra, rb, _, _, _ = self.slots
        self.arrive(1)

        @pl.loop(0, 4)
        def _(z):
            one = buf[1 - x, c, z, y, 0:half].astype(F32) + ra[z, 0:half].astype(F32)
            buf[1 - x, c, z, y, 0:half] = one.astype(BF)

        self.start(3)
        self.arrive(2)

        @pl.loop(0, 4)
        def _(z):
            two = buf[x, c, z, 1 - y, half : 2 * half].astype(F32) + rb[z, 0:half].astype(F32)
            buf[x, c, z, 1 - y, half : 2 * half] = two.astype(BF)

        self.start(4)

    def s4(self):
        p = Place(self.inner)
        x, y, c = p.x, p.y, p.c
        buf, rows = self.buf, self.rows
        _, _, _, rx, ry, _ = self.slots
        self.arrive(3, 4)

        @pl.loop(0, 4)
        def _(z):
            one = rx[z, 0:rows].astype(F32) + ry[z, 0:rows].astype(F32)
            buf[x, c, z, y] = (buf[x, c, z, y].astype(F32) + one).astype(BF)

        self.start(5, 6, 7)

    def s5(self):
        p = Place(self.inner)
        rows = self.rows
        rz = self.slots[5]
        self.arrive(5, 6, 7)
        total = self.buf[p.x, p.c, p.z, p.y].astype(F32)
        for d in range(3):
            total = total + rz[d, 0:rows].astype(F32)
        self.out[...] = total
        self.left()


class Total:
    def __init__(self, inner, ref, got, send, recv):
        self.inner, self.ref, self.got, self.send, self.recv = inner, ref, got, send, recv

    def copy(self, slot):
        p = Place(self.inner)
        dev = (p.core, p.xn, p.yn)[slot]() if slot < 3 else p.zn(slot - 2)
        stage = min(slot, 3)
        return remote(self.ref.at[stage], self.got.at[slot], self.send.at[slot], self.recv.at[slot], dev)

    def run(self, stage):
        slots = (stage,) if stage < 3 else (3, 4, 5)
        for slot in slots:
            self.copy(slot).start()

    def take(self, stage):
        slots = (stage,) if stage < 3 else (3, 4, 5)
        total = self.ref[stage]
        for slot in slots:
            self.copy(slot).wait_recv()
            total = total + self.got[slot]
        self.ref[stage + 1] = total

    def left(self):
        for slot in range(6):
            self.copy(slot).wait_send()


def head_parts(t_ref, k2_ref, t, h, qs, kr):
    if h < 2:
        return t_ref[t, qs, 0:128], t_ref[t, kr, 128:256], t_ref[t, kr, 256:384]
    return t_ref[t, qs, 384:512], k2_ref[kr, :], t_ref[t, kr, 512:640]


def lanes():
    return lax.broadcasted_iota(jnp.int32, (1, 128), 1)


def roll_key(t_ref, k2_ref, t):
    k2_ref[...] = pltpu.roll(t_ref[t, :, 384:512].astype(F32), 64, 1).astype(BF)


def below(transposed):
    r = lax.broadcasted_iota(jnp.int32, (BQ, BQ), 0)
    c = lax.broadcasted_iota(jnp.int32, (BQ, BQ), 1)
    return r <= c if transposed else r >= c


def attend(t_ref, l_ref, kx_ref, k2_ref, c_ref, t, length):
    lane = lanes()
    low = lane < 64
    roll_key(t_ref, k2_ref, t)
    for i in range(length // BQ):
        first = max(0, i * BQ - length // 2)
        width = (i + 1) * BQ - first
        qs, kr = slice(i * BQ, (i + 1) * BQ), slice(first, first + width)
        kx = kx_ref[kr, :]
        doc = kx_ref[qs, :].astype(F32)
        qx = jnp.where(lane < 8, BIG * (1.0 - doc), 0.0).astype(BF)
        marks = qx
        outs = []
        for h in range(3):
            q, k, v = head_parts(t_ref, k2_ref, t, h, qs, kr)
            keep = jnp.logical_not(low) if h == 1 else low
            q = jnp.where(keep, q * BF(HD ** -0.5), BF(0))
            s = dot(jnp.concatenate([q, qx], 1), jnp.concatenate([k, kx], 1), NT)
            edge = jnp.where(below(False), s[:, width - BQ :], BIG)
            s = edge if width == BQ else jnp.concatenate([s[:, : width - BQ], edge], 1)
            top = jnp.max(s, axis=1, keepdims=True)
            p = jnp.exp(s - top).astype(BF)
            both = dot(p, jnp.concatenate([v, jnp.ones((width, 128), BF)], 1))
            total = both[:, 128:256]
            outs.append(both[:, :128] / total)
            rest = -(top + jnp.log(total))
            for n in range(3):
                piece = rest.astype(BF)
                marks = jnp.where(lane == 8 + 16 * h + n, piece, marks)
                rest = rest - piece.astype(F32)
        l_ref[t, qs, :] = marks
        c_ref[t, qs, 0:128] = jnp.where(low, outs[0], outs[1]).astype(BF)
        c_ref[t, qs, 128:256] = jnp.where(low, outs[2], 0.0).astype(BF)


def attend_back(t_ref, l_ref, kx_ref, k2_ref, c_ref, do_ref, sums, t, length):
    lane = lanes()
    low = lane < 64
    dk_ref, dv_ref, dk2_ref, dv2_ref = sums
    roll_key(t_ref, k2_ref, t)
    for ref in sums:
        ref[...] = jnp.zeros_like(ref)
    for i in range(length // BQ):
        first = max(0, i * BQ - length // 2)
        width = (i + 1) * BQ - first
        qs, kr = slice(i * BQ, (i + 1) * BQ), slice(first, first + width)
        marks = l_ref[t, qs, :]
        kx = kx_ref[kr, :]
        minus = jnp.full((width, 128), -1.0, BF)
        grads = []
        for h in range(3):
            q, k, v = head_parts(t_ref, k2_ref, t, h, qs, kr)
            keep = jnp.logical_not(low) if h == 1 else low
            side = slice(0, 128) if h < 2 else slice(128, 256)
            q = jnp.where(keep, q * BF(HD ** -0.5), BF(0))
            do = jnp.where(keep, do_ref[t, qs, side], BF(0))
            km = jnp.where(keep, k, BF(0))
            dd = (do.astype(F32) * c_ref[t, qs, side].astype(F32)).astype(BF)
            mine = (lane < 8) | ((lane >= 8 + 16 * h) & (lane < 24 + 16 * h))
            qe = jnp.concatenate([q, jnp.where(mine, marks, BF(0))], 1)
            s = dot(jnp.concatenate([k, kx], 1), qe, NT)
            dp = dot(jnp.concatenate([v, minus], 1), jnp.concatenate([do, dd], 1), NT)
            edge = jnp.where(below(True), s[width - BQ :], BIG)
            s = edge if width == BQ else jnp.concatenate([s[: width - BQ], edge], 0)
            p = jnp.exp(s)
            ds = (p * dp).astype(BF)
            grads.append(dot(ds, km, TN))
            gv, gk = dot(p.astype(BF), do), dot(ds, q)
            if h < 2:
                dk_ref[kr, :] += gk
                dv_ref[kr, :] += gv
            else:
                dk2_ref[kr, :] += gk
                dv2_ref[kr, :] += gv
        t_ref[t, qs, 0:128] = ((grads[0] + grads[1]) * HD ** -0.5).astype(BF)
        t_ref[t, qs, 384:512] = jnp.where(low, (grads[2] * HD ** -0.5).astype(BF), t_ref[t, qs, 384:512])
    t_ref[t, :, 128:256] = dk_ref[...].astype(BF)
    t_ref[t, :, 256:384] = dv_ref[...].astype(BF)
    t_ref[t, :, 384:512] = jnp.where(low, t_ref[t, :, 384:512], pltpu.roll(dk2_ref[...], 64, 1).astype(BF))
    t_ref[t, :, 512:640] = dv2_ref[...].astype(BF)


def stats(v):
    mean = jnp.mean(v, axis=-1, keepdims=True)
    center = v - mean
    scale = lax.rsqrt(jnp.mean(center * center, axis=-1, keepdims=True) + EPS)
    return center * scale, scale


def norm_back(v, q, gain):
    n, scale = stats(v)
    e = q * gain
    back = scale * (e - jnp.mean(e, -1, keepdims=True) - n * jnp.mean(e * n, -1, keepdims=True))
    return back, jnp.sum(q * n, 0, keepdims=True), jnp.sum(q, 0, keepdims=True)


def kernel(
    inner, length,
    tok, cot, seg, valid, wq_in, wo_in, wm_in,
    lo_out, gt_out, gq_out, go_out, gm_out, ar_out,
    bq, bo, bm0, bm1, bm2,
    n1, tt, cc, ll, kx, k2, mid, n2, acc, gn, act, gu, val, par,
    dk, dv, dk2, dv2,
    m_sets, q_set, ar, ar_got,
    ag_send, ag_recv, rs_send, rs_recv, credit, ar_send, ar_recv, local_sem,
):
    width = tok.shape[1]
    bm = (bm0, bm1, bm2)
    blocks = [(bq, 0, 32), (bq, 32, 32), (bq, 64, 32), (bo, 0, 96)] + [(b, 0, 192) for b in bm]
    gathers = [Gather(inner, b, r0, rows, ag_send.at[k], ag_recv.at[k]) for k, (b, r0, rows) in enumerate(blocks)]
    here = Place(inner)

    def fills():
        at = (here.x, here.c, here.z, here.y)
        pairs = [(wq_in, bq), (wo_in, bo)] + [(wm_in.at[j], bm[j]) for j in range(3)]
        return [pltpu.make_async_copy(src, b.at[at], local_sem.at[k]) for k, (src, b) in enumerate(pairs)]

    for one in fills():
        one.start()
    barrier(inner)
    for one in fills():
        one.wait()

    for g in gathers:
        g.s1()
    for g in gathers:
        g.s2()
        g.s3()
        g.s4()
    for g in gathers:
        g.s5()
        g.s6()

    def rows_of(i, size):
        return pl.ds(pl.multiple_of(i * size, size), size)

    def weight(buf, t, r0, rows, columns):
        return buf[t // 2, t % 2, :, :, r0 : r0 + rows, columns].reshape(8 * rows, -1)

    par[...] = bq[0, 0, :, :, :, 512:640].reshape(width, 128).astype(F32).T
    me_t = lax.axis_index("tp")
    row = seg[pl.ds(me_t, 1), :].astype(F32)
    lane_id = lax.broadcasted_iota(jnp.int32, (128, length), 0)
    marks = jnp.where(row == lane_id.astype(F32), 1.0, 0.0)
    marks = jnp.where(lane_id < 8, marks, 0.0)
    low4 = lane_id % 16
    ones = (lane_id >= 8) & (lane_id < 56) & (low4 >= 8) & (low4 < 11)
    marks = jnp.where(ones, 1.0, marks)
    marks = jnp.where(lane_id == 64, valid[...].astype(F32), marks)
    columns = marks.T
    val[...] = columns[:, 64:65]
    kx[...] = jnp.where(lanes() < 64, columns, 0.0).astype(BF)
    ar[0] = jnp.zeros_like(ar.at[0])
    ar[0, 7:8, 0:128] = jnp.broadcast_to(jnp.sum(valid[...].astype(F32), axis=1, keepdims=True), (1, 128))

    @pl.loop(0, length // 256)
    def _(i):
        s = rows_of(i, 256)
        n, _ = stats(tok[s, :].astype(F32))
        n1[s, :] = (n * par[64:65, :] + par[65:66, :]).astype(BF)

    @pl.loop(0, 4)
    def _(t):
        w = weight(bq, t, 0, 96, slice(0, 640))

        @pl.loop(0, length // 512)
        def _(i):
            s = rows_of(i, 512)
            tt[t, s, :] = dot(n1[s, :], w).astype(BF)

        attend(tt, ll, kx, k2, cc, t, length)

    @pl.loop(0, length // 256)
    def _(i):
        s = rows_of(i, 256)
        branch = jnp.zeros((256, width), F32)
        for t in range(4):
            branch = branch + dot(cc[t, s, :], weight(bo, t, 0, 96, slice(0, 256)), NT)
        v = tok[s, :].astype(F32) + branch
        mid[s, :] = v
        ar[0, 5:6, :] += jnp.sum(val[s, :] * (branch * branch), 0, keepdims=True)
        n, _ = stats(v)
        n2[s, :] = (n * par[66:67, :] + par[67:68, :]).astype(BF)

    for j in range(3):
        b = bm[j]

        @pl.loop(0, 4)
        def _(t):
            up = weight(b, t, 0, 96, slice(0, 256))
            down = weight(b, t, 96, 96, slice(0, 256))

            @pl.loop(0, length // 512)
            def _(i):
                s = rows_of(i, 512)
                v = dot(n2[s, :], up)
                ga = dot(cot[s, :], down)
                v2 = v * v
                th = jnp.tanh(v * (C0 + C1 * v2))
                h = 0.5 + 0.5 * th
                act[t, s, :] = (v * h).astype(BF)
                slope = h + (0.5 * v) * (1.0 - th * th) * (C0 + (3.0 * C1) * v2)
                gu[t, s, :] = (ga * slope).astype(BF)

        def cat(ref, s):
            return jnp.concatenate([ref[t, s, :] for t in range(4)], 1)

        def wcat(r0):
            return jnp.concatenate([weight(b, t, r0, 96, slice(0, 256)) for t in range(4)], 1)

        @pl.loop(0, length // 256)
        def _(i):
            s = rows_of(i, 256)
            one = dot(cat(act, s), wcat(96), NT)
            two = dot(cat(gu, s), wcat(0), NT)
            if j == 0:
                acc[s, :] = one
                gn[s, :] = two
            else:
                acc[s, :] += one
                gn[s, :] += two

        @pl.loop(0, 4)
        def _(t):
            gup = dot(n2[...], gu[t], TN).astype(BF)
            b[t // 2, t % 2, :, :, 0:96, :] = gup.reshape(4, 2, 96, 256)
            gdown = dot(cot[...], act[t], TN).astype(BF)
            b[t // 2, t % 2, :, :, 96:192, :] = gdown.reshape(4, 2, 96, 256)

    @pl.loop(0, length // 256)
    def _(i):
        s = rows_of(i, 256)
        v = mid[s, :]
        mlp = acc[s, :]
        out = v + mlp
        weight_rows = val[s, :]
        ar[0, 4:5, :] += jnp.sum(weight_rows * (out * out), 0, keepdims=True)
        ar[0, 6:7, :] += jnp.sum(weight_rows * (mlp * mlp), 0, keepdims=True)
        low_out = out.astype(BF)
        for k in range(width // 256):
            gu[k, s, :] = low_out[:, 256 * k : 256 * k + 256]
        back, g_gain, g_bias = norm_back(v, gn[s, :], par[66:67, :])
        ar[0, 2:3, :] += g_gain
        ar[0, 3:4, :] += g_bias
        grad = cot[s, :].astype(F32) + back
        mid[s, :] = grad
        n2[s, :] = grad.astype(BF)

    def store_low():
        return [
            pltpu.make_async_copy(gu.at[k], lo_out.at[:, pl.ds(256 * k, 256)], local_sem.at[k])
            for k in range(width // 256)
        ]

    for one in store_low():
        one.start()

    @pl.loop(0, 4)
    def _(t):
        w = weight(bo, t, 0, 96, slice(0, 256))
        act[t] = dot(n2[...], w).astype(BF)
        bo[t // 2, t % 2] = dot(n2[...], cc[t], TN).astype(BF).reshape(4, 2, 96, 256)

    @pl.loop(0, 4)
    def _(t):
        attend_back(tt, ll, kx, k2, cc, act, (dk, dv, dk2, dv2), t, length)

    @pl.loop(0, length // 256)
    def _(i):
        s = rows_of(i, 256)
        total = jnp.zeros((256, width), F32)
        for t in range(4):
            total = total + dot(tt[t, s, :], weight(bq, t, 0, 96, slice(0, 640)), NT)
        back, g_gain, g_bias = norm_back(tok[s, :].astype(F32), total, par[64:65, :])
        ar[0, 0:1, :] += g_gain
        ar[0, 1:2, :] += g_bias
        acc[s, :] = mid[s, :] + back

    def store_grad():
        return pltpu.make_async_copy(acc, gt_out, local_sem.at[4])

    store_grad().start()

    @pl.loop(0, 4)
    def _(t):
        bq[t // 2, t % 2] = dot(n1[...], tt[t], TN).astype(BF).reshape(4, 2, 96, 640)

    sets = [m_sets[0:6], m_sets[6:12]]
    plan = [(bm0, 192, sets[0], gm_out.at[0]), (bm1, 192, sets[1], gm_out.at[1]),
            (bm2, 192, sets[0], gm_out.at[2]), (bo, 96, sets[1], go_out), (bq, 96, q_set, gq_out)]
    scatters = [
        Scatter(inner, b, rows, slots, rs_send.at[k], rs_recv.at[k], credit.at[k], out)
        for k, (b, rows, slots, out) in enumerate(plan)
    ]
    for k, s in enumerate(scatters):
        if k in (2, 3):
            scatters[k - 2].take_credit()
        s.s1()
        s.s2()
        s.s3()
        s.s4()
        s.s5()
        if k in (0, 1):
            s.give_credit()
    total = Total(inner, ar, ar_got, ar_send, ar_recv)
    for stage in range(4):
        total.run(stage)
        total.take(stage)
    total.left()
    ar_out[...] = ar[4]
    for one in store_low():
        one.wait()
    store_grad().wait()


def scatter_slots(rows, columns):
    return [
        pltpu.VMEM((2, 4, 2, rows, columns), BF),
        pltpu.VMEM((4, rows // 2, columns), BF),
        pltpu.VMEM((4, rows // 2, columns), BF),
        pltpu.VMEM((4, rows, columns), BF),
        pltpu.VMEM((4, rows, columns), BF),
        pltpu.VMEM((3, rows, columns), BF),
    ]


def layer(inner, tokens, cotangent, segments, valid, wq, wo, wm):
    length, width = tokens.shape
    block = lambda rows, columns: pltpu.VMEM((2, 2, 4, 2, rows, columns), BF)
    scratch = [
        block(96, 640), block(96, 256), block(192, 256), block(192, 256), block(192, 256),
        pltpu.VMEM((length, width), BF),
        pltpu.VMEM((4, length, 640), BF),
        pltpu.VMEM((4, length, 256), BF),
        pltpu.VMEM((4, length, 128), BF),
        pltpu.VMEM((length, 128), BF),
        pltpu.VMEM((length, 128), BF),
        pltpu.VMEM((length, width), F32),
        pltpu.VMEM((length, width), BF),
        pltpu.VMEM((length, width), F32),
        pltpu.VMEM((length, width), F32),
        pltpu.VMEM((4, length, 256), BF),
        pltpu.VMEM((4, length, 256), BF),
        pltpu.VMEM((length, 1), F32),
        pltpu.VMEM((128, width), F32),
    ]
    scratch += [pltpu.VMEM((length, 128), F32)] * 4
    scratch += [scatter_slots(192, 256) + scatter_slots(192, 256), scatter_slots(96, 640)]
    scratch += [
        pltpu.VMEM((5, 8, width), F32),
        pltpu.VMEM((6, 8, width), F32),
        pltpu.SemaphoreType.DMA((7, 11)),
        pltpu.SemaphoreType.DMA((7, 11)),
        pltpu.SemaphoreType.DMA((5, 8)),
        pltpu.SemaphoreType.DMA((5, 8)),
        pltpu.SemaphoreType.REGULAR((2, 6)),
        pltpu.SemaphoreType.DMA((6,)),
        pltpu.SemaphoreType.DMA((6,)),
        pltpu.SemaphoreType.DMA((5,)),
    ]
    vmem, anywhere = pl.BlockSpec(memory_space=pltpu.VMEM), pl.BlockSpec(memory_space=pl.ANY)
    return pl.pallas_call(
        partial(kernel, inner, length),
        out_shape=(
            jax.ShapeDtypeStruct((length, width), BF),
            jax.ShapeDtypeStruct((length, width), F32),
            jax.ShapeDtypeStruct((96, 640), F32),
            jax.ShapeDtypeStruct((96, 256), F32),
            jax.ShapeDtypeStruct((3, 192, 256), F32),
            jax.ShapeDtypeStruct((8, width), F32),
        ),
        in_specs=[vmem] * 4 + [anywhere] * 3,
        out_specs=(anywhere, anywhere, vmem, vmem, vmem, vmem),
        scratch_shapes=scratch,
        compiler_params=pltpu.CompilerParams(
            collective_id=0, has_side_effects=True, vmem_limit_bytes=63 * 2**20
        ),
    )(tokens, cotangent, segments, valid, wq, wo, wm)


def local(
    tokens, segment_ids, valid, ln1_gain, ln1_bias, w_qkv, w_out, ln2_gain, ln2_bias, w_up, w_down, cotangent
):
    length, width = tokens.shape
    holders = lax.axis_size("fsdp")
    inner = holders // 8
    groups = [[g * inner + i for i in range(inner)] for g in range(8)]

    def widen(block):
        if inner == 1:
            return block
        return lax.all_gather(block, "fsdp", axis_index_groups=groups, axis=0, tiled=True)

    def narrow(block):
        if inner == 1:
            return block
        return lax.psum_scatter(
            block, "fsdp", scatter_dimension=0, axis_index_groups=groups, tiled=True
        )

    rows = w_up.shape[0]
    heads = w_qkv.reshape(rows, 3, 3, HD)
    pairs = heads[:, :, 0:2].reshape(rows, 3 * 2 * HD)
    odd = heads[:, :, 2].reshape(rows, 3 * HD)
    params = jnp.stack([ln1_gain, ln1_bias, ln2_gain, ln2_bias], axis=1)
    wq = widen(jnp.concatenate([pairs, odd, params, jnp.zeros((rows, 60), BF)], axis=1))
    wo = widen(jnp.pad(w_out.T, ((0, 0), (0, 64))))
    up = widen(w_up).reshape(rows * inner, 3, 256)
    down = widen(w_down.T).reshape(rows * inner, 3, 256)
    wm = jnp.concatenate([up, down], axis=0).transpose(1, 0, 2)

    low, grad_tokens, gq, go, gm, sums = layer(
        inner, tokens, cotangent, segment_ids, valid.reshape(1, length), wq, wo, wm
    )

    gq = narrow(gq[:, : 9 * HD])
    pair = gq[:, : 6 * HD].reshape(rows, 3, 2 * HD)
    one = gq[:, 6 * HD : 9 * HD].reshape(rows, 3, HD)
    grad_qkv = jnp.concatenate([pair, one], axis=2)
    grad_out = narrow(go[:, : 3 * HD]).T
    gm = gm.transpose(1, 0, 2).reshape(192, 768)
    grad_up = narrow(gm[:96])
    grad_down = narrow(gm[96:]).T
    if inner > 1:
        sums = lax.psum(sums, "fsdp", axis_index_groups=groups)
    share = width // (holders * lax.axis_size("tp"))
    owner = lax.axis_index("fsdp") * lax.axis_size("tp") + lax.axis_index("tp")
    mine = lax.dynamic_slice_in_dim(sums[0:4], owner * share, share, 1)
    spread = jnp.sqrt(jnp.sum(sums[4:7], axis=1) / (sums[7, 0] * width))
    return (
        low, grad_tokens, mine[0], mine[1], grad_qkv, grad_out, mine[2], mine[3], grad_up, grad_down, spread
    )


def solution(mesh):
    both = ("fsdp", "tp")
    return jax.shard_map(
        local,
        mesh=mesh,
        in_specs=(
            P(both, None), P("fsdp", None), P(both), P("fsdp"), P("fsdp"), P("fsdp", None, "tp"),
            P("tp", "fsdp"), P("fsdp"), P("fsdp"), P("fsdp", "tp"), P("tp", "fsdp"), P(both, None),
        ),
        out_specs=(
            P(both, None), P(both, None), P(both), P(both), P("fsdp", None, "tp"), P("tp", "fsdp"),
            P(both), P(both), P("fsdp", "tp"), P("tp", "fsdp"), P(),
        ),
        check_vma=False,
    )
```

time: 978 us -> 380 us (0.39)
  waiting for transfers between devices: 381 us -> 0 us
  Pallas kernels: 0 us -> 359 us
  matrix products: 203 us -> 0 us
  blocking collectives: 130 us -> 0 us
  other arithmetic: 87.3 us -> 1.48 us
  local copies, waits for them, and re-layouts: 99.8 us -> 18 us
  loops' own time: 31.5 us -> 0 us
  starting transfers between devices: 20.4 us -> 0 us
  between operations: 18.1 us -> 1.44 us
    pallas_call x0 -> x1, Pallas kernels: none -> 359 us  [layer(): pl.pallas_call(partial(kernel, inner, length), out_shape=(jax.ShapeDtypeS...]
    dot_general x68 -> x0, matrix products: 203 us -> none  [the longest x4 36.5 us: inner_rows(): lax.dot_general(left, right, (((0,), (0,)), ((), ())), preferred_element_...]
    reduce_scatter x4 -> x0, waiting for transfers between devices: 160 us -> none  [the longest x1 60.8 us: local(): lax.psum_scatter(project_rows(active, matrices[3]).astype(jnp.bfloat16),...]
    all_gather x6 -> x0, waiting for transfers between devices: 156 us -> none  [the longest x1 47 us: local(): whole_two = lax.all_gather(normed_two, 'tp', axis=0, tiled=True)]
    all_gather x2 -> x0, blocking collectives: 68.8 us -> none  [the longest x1 35.2 us: local(): lax.all_gather(w_qkv, 'fsdp', axis=0, tiled=True)]
    all_to_all x4 -> x0, waiting for transfers between devices: 62.8 us -> none  [sum_at_owner(): lax.all_to_all(blocks, axis, split_axis=0, concat_axis=0, tiled=True)]
    reduce_sum x21 -> x1, other arithmetic: 40.5 us -> 0.12 us  [local(): spread = jnp.sqrt(jnp.sum(sums[4:7], axis=1) / (sums[7, 0] * width))]
    psum x1 -> x0, blocking collectives: 37.1 us -> none  [local(): lax.psum((norm_grads, sums, valid_count), ('fsdp', 'tp'))]
  transfers between devices with their start and end apart: 14 -> 0, of which waited for: 10 -> 0; matrix products, arithmetic and copies ran while one was open for 8% -> 0% of each run, Pallas kernels for 0% -> 0%
where the time goes in v1:
time: 380 us; the launch traced here: 379 us
  Pallas kernels  359 us (94%)
  local copies, waits for them, and re-layouts  18 us (5%)
    pallas_call x1, Pallas kernels, layer(): pl.pallas_call(partial(kernel, inner, length), out_shape=(jax.ShapeDtypeS...  359 us
    unnamed x21, local copies, waits for them, and re-layouts  7.69 us

profile of v1, /device:TPU:0, one launch (start us, length us, event | category | flops | bytes accessed | tf_op | source)
XLA Modules:
  0.0 379.4 jit_solution(192374982977786937)
XLA Ops:
  0.6 0.0 copy-start.3
  0.7 0.0 copy-start.4
  0.7 1.1 copy.33
  1.8 0.1 copy.34
  1.9 0.1 copy.35
  2.0 0.8 copy.36
  2.8 0.8 copy.37
  3.6 0.8 copy.38
  4.4 0.8 copy.39
  5.1 0.8 concatenate.9.wq_in
  5.9 0.9 copy.40
  6.8 0.6 pad.4.wo_in
  7.4 0.0 copy-done.3
  7.4 0.0 copy-done.4
  7.5 0.7 maximum_bitcast_fusion.wm_in
  8.2 358.5 %shard_map.203 = (bf16[1024,768]{1,0:T(8,128)(2,1)}, f32[1024,768]{1,0:T(8,128)}, f32[96,640]{1,0:T(8,128)}, f32[96,256]{1,0:T(8,128)}, f32[3,192,256]{2,1,0:T(8,128)}, /*index=5*/f32[8,768]{1,0:T(8,128)}) custom-call(bf16[1024,768]{1,0:T(8,128)(2,1)} %tok.1, bf16[1024,768]{1,0:T(8,128)(2,1)} %cot.1, s32[4,1024]{1,0:T(4,128)} %seg.1, s32[1,1024]{1,0:T(1,128)} %bitcast.50, ...), custom_call_target="tpu_custom_call" | custom-call | tf_op jit(solution)/shard_map/pallas_call | solution.py:671
  366.7 0.0 copy-start.5
  366.7 0.8 slice.53
  367.5 0.1 constant_dynamic-slice_fusion
  367.6 0.5 slice_bitcast_fusion.3
  368.1 0.0 copy-start.2
  368.1 1.0 slice.57
  369.1 0.1 copy.43
  369.2 0.1 copy.44
  369.3 0.9 slice.56
  370.2 0.1 reshape.53
  370.3 0.1 pad_maximum_fusion
  370.4 0.0 copy-start.6
  370.4 0.0 copy-start.1
  370.4 0.8 copy.47
  371.2 0.0 copy-done.5
  371.2 0.7 copy.48
  372.0 0.0 copy-done.2
  372.0 0.7 copy.51
  372.7 0.7 copy.52
  373.5 0.0 copy-done.6
  373.5 0.1 slice_reduce_fusion
  373.6 0.5 slice.66
  374.8 0.5 divide_sqrt_fusion
  375.3 0.0 copy-done.1
  375.3 0.0 copy-start
  375.3 1.1 copy.57
  376.4 1.3 copy-done
  377.8 1.7 copy.58
  (6 shorter events, 0.1 us)
Async XLA Ops:
  0.6 6.8 %copy-start.3 = (bf16[768,96]{0,1:T(8,128)(2,1)S(1)}, bf16[768,96]{0,1:T(8,128)(2,1)}, u32[]{:S(2)}) copy-start(bf16[768,96]{0,1:T(8,128)(2,1)} %param.22) | copy-start | bytes 442372
  0.7 6.8 %copy-start.4 = (bf16[96,768]{1,0:T(8,128)(2,1)S(1)}, bf16[96,768]{1,0:T(8,128)(2,1)}, u32[]{:S(2)}) copy-start(bf16[96,768]{1,0:T(8,128)(2,1)} %param.21) | copy-start | bytes 442372
  366.7 4.5 %copy-start.5 = (f32[96,256]{1,0:T(8,128)S(1)}, f32[96,256]{1,0:T(8,128)}, u32[]{:S(2)}) copy-start(f32[96,256]{1,0:T(8,128)} %get-tuple-element.21) | copy-start | bytes 294916
  368.1 3.8 %copy-start.2 = (f32[3,192,256]{2,1,0:T(8,128)S(1)}, f32[3,192,256]{2,1,0:T(8,128)}, u32[]{:S(2)}) copy-start(f32[3,192,256]{2,1,0:T(8,128)} %get-tuple-element.22) | copy-start | bytes 1769476
  370.4 3.1 copy-start.6
  370.4 4.9 %copy-start.1 = (bf16[1024,768]{1,0:T(8,128)(2,1)S(1)}, bf16[1024,768]{1,0:T(8,128)(2,1)}, u32[]{:S(2)}) copy-start(bf16[1024,768]{1,0:T(8,128)(2,1)} %get-tuple-element.64) | copy-start | bytes 4718596
  375.3 2.5 copy-start

commit v2 on v1

--- a/solution.py
+++ b/solution.py
@@ -141,29 +141,32 @@
 
 
 class Scatter:
-    def __init__(self, inner, buf, rows, slots, send, recv, credit, out):
+    def __init__(self, inner, buf, rows, col0, cols, slots, send, recv, credit, out):
         self.inner, self.buf, self.rows = inner, buf, rows
+        self.cols = slice(col0, col0 + cols)
         self.slots, self.send, self.recv = slots, send, recv
         self.credit, self.out = credit, out
 
     def parts(self, slot):
         p = Place(self.inner)
         x, c, z, y = p.x, p.c, p.z, p.y
-        buf, half = self.buf, self.rows // 2
+        half = self.rows // 2
+        cols = self.cols
         r1, ra, rb, rx, ry, rz = self.slots
-        whole, cut = pl.ds(0, self.rows), pl.ds(0, half)
+        rows, cut, rest = slice(0, self.rows), slice(0, half), slice(half, self.rows)
+        buf = self.buf
         if slot == 0:
-            return buf.at[:, 1 - c], r1.at[:, :, :, whole], p.core()
+            return buf.at[:, 1 - c, :, :, :, cols], r1.at[:, :, :, rows], p.core()
         if slot == 1:
-            return buf.at[1 - x, c, :, 1 - y, pl.ds(0, half)], ra.at[:, cut], p.yn()
+            return buf.at[1 - x, c, :, 1 - y, cut, cols], ra.at[:, cut], p.yn()
         if slot == 2:
-            return buf.at[1 - x, c, :, 1 - y, pl.ds(half, half)], rb.at[:, cut], p.xn()
+            return buf.at[1 - x, c, :, 1 - y, rest, cols], rb.at[:, cut], p.xn()
         if slot == 3:
-            return buf.at[1 - x, c, :, y], rx.at[:, whole], p.xn()
+            return buf.at[1 - x, c, :, y, rows, cols], rx.at[:, rows], p.xn()
         if slot == 4:
-            return buf.at[x, c, :, 1 - y], ry.at[:, whole], p.yn()
+            return buf.at[x, c, :, 1 - y, rows, cols], ry.at[:, rows], p.yn()
         d = slot - 4
-        return buf.at[x, c, (z + d) % 4, y], rz.at[d - 1, whole], p.zn(d)
+        return buf.at[x, c, (z + d) % 4, y, rows, cols], rz.at[d - 1, rows], p.zn(d)
 
     def start(self, *slots):
         for slot in slots:
@@ -192,69 +195,54 @@
     def s1(self):
         self.start(0)
 
-    def add_core(self, x, y):
+    def add(self, x, y, rows, *others):
         c = Place(self.inner).c
-        r1 = self.slots[0]
 
         @pl.loop(0, 4)
         def _(z):
-            got = r1[x, z, y, 0 : self.rows].astype(F32)
-            self.buf[x, c, z, y] = (self.buf[x, c, z, y].astype(F32) + got).astype(BF)
+            total = self.buf[x, c, z, y, rows, self.cols].astype(F32)
+            for other in others:
+                total = total + other(z).astype(F32)
+            self.buf[x, c, z, y, rows, self.cols] = total.astype(BF)
 
     def s2(self):
         p = Place(self.inner)
-        x, y = p.x, p.y
+        rows = slice(0, self.rows)
+        r1 = self.slots[0]
         self.arrive(0)
-        self.add_core(1 - x, 1 - y)
-        self.start(1, 2)
-        self.add_core(1 - x, y)
-        self.add_core(x, 1 - y)
-        self.add_core(x, y)
+        for x, y in ((1 - p.x, 1 - p.y), (1 - p.x, p.y), (p.x, 1 - p.y), (p.x, p.y)):
+            self.add(x, y, rows, lambda z: r1[x, z, y, rows])
+            if x is not p.x and y is not p.y:
+                self.start(1, 2)
 
     def s3(self):
         p = Place(self.inner)
-        x, y, c = p.x, p.y, p.c
-        buf, half = self.buf, self.rows // 2
-        _, ra, rb, _, _, _ = self.slots
+        half = self.rows // 2
+        cut, rest = slice(0, half), slice(half, self.rows)
+        ra, rb = self.slots[1:3]
         self.arrive(1)
-
-        @pl.loop(0, 4)
-        def _(z):
-            one = buf[1 - x, c, z, y, 0:half].astype(F32) + ra[z, 0:half].astype(F32)
-            buf[1 - x, c, z, y, 0:half] = one.astype(BF)
-
+        self.add(1 - p.x, p.y, cut, lambda z: ra[z, cut])
         self.start(3)
         self.arrive(2)
-
-        @pl.loop(0, 4)
-        def _(z):
-            two = buf[x, c, z, 1 - y, half : 2 * half].astype(F32) + rb[z, 0:half].astype(F32)
-            buf[x, c, z, 1 - y, half : 2 * half] = two.astype(BF)
-
+        self.add(p.x, 1 - p.y, rest, lambda z: rb[z, cut])
         self.start(4)
 
     def s4(self):
         p = Place(self.inner)
-        x, y, c = p.x, p.y, p.c
-        buf, rows = self.buf, self.rows
-        _, _, _, rx, ry, _ = self.slots
+        rows = slice(0, self.rows)
+        rx, ry = self.slots[3:5]
         self.arrive(3, 4)
-
-        @pl.loop(0, 4)
-        def _(z):
-            one = rx[z, 0:rows].astype(F32) + ry[z, 0:rows].astype(F32)
-            buf[x, c, z, y] = (buf[x, c, z, y].astype(F32) + one).astype(BF)
-
+        self.add(p.x, p.y, rows, lambda z: rx[z, rows], lambda z: ry[z, rows])
         self.start(5, 6, 7)
 
     def s5(self):
         p = Place(self.inner)
-        rows = self.rows
+        rows = slice(0, self.rows)
         rz = self.slots[5]
         self.arrive(5, 6, 7)
-        total = self.buf[p.x, p.c, p.z, p.y].astype(F32)
+        total = self.buf[p.x, p.c, p.z, p.y, rows, self.cols].astype(F32)
         for d in range(3):
-            total = total + rz[d, 0:rows].astype(F32)
+            total = total + rz[d, rows].astype(F32)
         self.out[...] = total
         self.left()
 
@@ -342,11 +330,13 @@
         c_ref[t, qs, 128:256] = jnp.where(low, outs[2], 0.0).astype(BF)
 
 
-def attend_back(t_ref, l_ref, kx_ref, k2_ref, c_ref, do_ref, sums, t, length):
+def attend_back(t_ref, l_ref, kx_ref, k2_ref, c_ref, do_ref, sums, heads, t, length):
     lane = lanes()
     low = lane < 64
-    dk_ref, dv_ref, dk2_ref, dv2_ref = sums
-    roll_key(t_ref, k2_ref, t)
+    dk_ref, dv_ref = sums
+    odd = heads == (2,)
+    if odd:
+        roll_key(t_ref, k2_ref, t)
     for ref in sums:
         ref[...] = jnp.zeros_like(ref)
     for i in range(length // BQ):
@@ -356,11 +346,11 @@
         marks = l_ref[t, qs, :]
         kx = kx_ref[kr, :]
         minus = jnp.full((width, 128), -1.0, BF)
-        grads = []
-        for h in range(3):
+        grad = None
+        for h in heads:
             q, k, v = head_parts(t_ref, k2_ref, t, h, qs, kr)
             keep = jnp.logical_not(low) if h == 1 else low
-            side = slice(0, 128) if h < 2 else slice(128, 256)
+            side = slice(128, 256) if odd else slice(0, 128)
             q = jnp.where(keep, q * BF(HD ** -0.5), BF(0))
             do = jnp.where(keep, do_ref[t, qs, side], BF(0))
             km = jnp.where(keep, k, BF(0))
@@ -373,20 +363,22 @@
             s = edge if width == BQ else jnp.concatenate([s[: width - BQ], edge], 0)
             p = jnp.exp(s)
             ds = (p * dp).astype(BF)
-            grads.append(dot(ds, km, TN))
-            gv, gk = dot(p.astype(BF), do), dot(ds, q)
-            if h < 2:
-                dk_ref[kr, :] += gk
-                dv_ref[kr, :] += gv
-            else:
-                dk2_ref[kr, :] += gk
-                dv2_ref[kr, :] += gv
-        t_ref[t, qs, 0:128] = ((grads[0] + grads[1]) * HD ** -0.5).astype(BF)
-        t_ref[t, qs, 384:512] = jnp.where(low, (grads[2] * HD ** -0.5).astype(BF), t_ref[t, qs, 384:512])
-    t_ref[t, :, 128:256] = dk_ref[...].astype(BF)
-    t_ref[t, :, 256:384] = dv_ref[...].astype(BF)
-    t_ref[t, :, 384:512] = jnp.where(low, t_ref[t, :, 384:512], pltpu.roll(dk2_ref[...], 64, 1).astype(BF))
-    t_ref[t, :, 512:640] = dv2_ref[...].astype(BF)
+            gq = dot(ds, km, TN)
+            grad = gq if grad is None else grad + gq
+            dv_ref[kr, :] += dot(p.astype(BF), do)
+            dk_ref[kr, :] += dot(ds, q)
+        grad = (grad * HD ** -0.5).astype(BF)
+        if odd:
+            t_ref[t, qs, 384:512] = jnp.where(low, grad, t_ref[t, qs, 384:512])
+        else:
+            t_ref[t, qs, 0:128] = grad
+    if odd:
+        moved = pltpu.roll(dk_ref[...], 64, 1).astype(BF)
+        t_ref[t, :, 384:512] = jnp.where(low, t_ref[t, :, 384:512], moved)
+        t_ref[t, :, 512:640] = dv_ref[...].astype(BF)
+    else:
+        t_ref[t, :, 128:256] = dk_ref[...].astype(BF)
+        t_ref[t, :, 256:384] = dv_ref[...].astype(BF)
 
 
 def stats(v):
@@ -409,7 +401,7 @@
     lo_out, gt_out, gq_out, go_out, gm_out, ar_out,
     bq, bo, bm0, bm1, bm2,
     n1, tt, cc, ll, kx, k2, mid, n2, acc, gn, act, gu, val, par,
-    dk, dv, dk2, dv2,
+    dk, dv,
     m_sets, q_set, ar, ar_got,
     ag_send, ag_recv, rs_send, rs_recv, credit, ar_send, ar_recv, local_sem,
 ):
@@ -424,29 +416,38 @@
         pairs = [(wq_in, bq), (wo_in, bo)] + [(wm_in.at[j], bm[j]) for j in range(3)]
         return [pltpu.make_async_copy(src, b.at[at], local_sem.at[k]) for k, (src, b) in enumerate(pairs)]
 
+    scatters = []
+    sets = [m_sets[0:6], m_sets[6:12]]
+    plan = [(bm0, 192, 0, 256, sets[0], gm_out.at[0]), (bm1, 192, 0, 256, sets[1], gm_out.at[1]),
+            (bm2, 192, 0, 256, sets[0], gm_out.at[2]), (bo, 96, 0, 256, sets[1], go_out),
+            (bq, 96, 0, 384, q_set, gq_out.at[:, 0:384]), (bq, 96, 384, 256, sets[0], gq_out.at[:, 384:640])]
+    for k, (b, rows, col0, cols, slots, out) in enumerate(plan):
+        cred = credit.at[min(k, 2)]
+        scatters.append(Scatter(inner, b, rows, col0, cols, slots, rs_send.at[k], rs_recv.at[k], cred, out))
+    m_sum, o_sum, qa_sum, qb_sum = scatters[0:3], scatters[3], scatters[4], scatters[5]
+    q_in, o_in, m_in = gathers[0:3], gathers[3], gathers[4:7]
+    total = Total(inner, ar, ar_got, ar_send, ar_recv)
+
+    def after(t, last, *steps):
+        @pl.when(t == last)
+        def _():
+            for step in steps:
+                step()
+
+    def rows_of(i, size):
+        return pl.ds(pl.multiple_of(i * size, size), size)
+
+    def weight(buf, t, r0, rows, columns):
+        return buf[t // 2, t % 2, :, :, r0 : r0 + rows, columns].reshape(8 * rows, -1)
+
     for one in fills():
         one.start()
     barrier(inner)
     for one in fills():
         one.wait()
-
-    for g in gathers:
+    for g in q_in:
         g.s1()
-    for g in gathers:
-        g.s2()
-        g.s3()
-        g.s4()
-    for g in gathers:
-        g.s5()
-        g.s6()
-
-    def rows_of(i, size):
-        return pl.ds(pl.multiple_of(i * size, size), size)
-
-    def weight(buf, t, r0, rows, columns):
-        return buf[t // 2, t % 2, :, :, r0 : r0 + rows, columns].reshape(8 * rows, -1)
-
-    par[...] = bq[0, 0, :, :, :, 512:640].reshape(width, 128).astype(F32).T
+
     me_t = lax.axis_index("tp")
     row = seg[pl.ds(me_t, 1), :].astype(F32)
     lane_id = lax.broadcasted_iota(jnp.int32, (128, length), 0)
@@ -465,8 +466,31 @@
     @pl.loop(0, length // 256)
     def _(i):
         s = rows_of(i, 256)
-        n, _ = stats(tok[s, :].astype(F32))
-        n1[s, :] = (n * par[64:65, :] + par[65:66, :]).astype(BF)
+        mid[s, :] = stats(tok[s, :].astype(F32))[0]
+
+    q_in[0].s2()
+    o_in.s1()
+    q_in[1].s2()
+    q_in[0].s3()
+    m_in[0].s1()
+    q_in[2].s2()
+    q_in[1].s3()
+    q_in[0].s4()
+    q_in[2].s3()
+    q_in[1].s4()
+    o_in.s2()
+    m_in[1].s1()
+    q_in[2].s4()
+    for g in q_in:
+        g.s5()
+    m_in[0].s2()
+
+    par[...] = bq[0, 0, :, :, :, 512:640].reshape(width, 128).astype(F32).T
+
+    @pl.loop(0, length // 256)
+    def _(i):
+        s = rows_of(i, 256)
+        n1[s, :] = (mid[s, :] * par[64:65, :] + par[65:66, :]).astype(BF)
 
     @pl.loop(0, 4)
     def _(t):
@@ -478,6 +502,10 @@
             tt[t, s, :] = dot(n1[s, :], w).astype(BF)
 
         attend(tt, ll, kx, k2, cc, t, length)
+        after(t, 0, o_in.s3, m_in[2].s1)
+        after(t, 1, m_in[1].s2, o_in.s4)
+        after(t, 2, m_in[0].s3, o_in.s5)
+        after(t, 3, m_in[2].s2, m_in[0].s4)
 
     @pl.loop(0, length // 256)
     def _(i):
@@ -491,8 +519,12 @@
         n, _ = stats(v)
         n2[s, :] = (n * par[66:67, :] + par[67:68, :]).astype(BF)
 
+    m_in[1].s3()
+    m_in[0].s5()
+
     for j in range(3):
         b = bm[j]
+        before = m_sum[j - 1] if j > 0 else None
 
         @pl.loop(0, 4)
         def _(t):
@@ -511,6 +543,15 @@
                 slope = h + (0.5 * v) * (1.0 - th * th) * (C0 + (3.0 * C1) * v2)
                 gu[t, s, :] = (ga * slope).astype(BF)
 
+            if j > 0:
+                after(t, 1, before.s2)
+
+        if j == 0:
+            m_in[2].s3()
+            m_in[1].s4()
+        else:
+            before.s3()
+
         def cat(ref, s):
             return jnp.concatenate([ref[t, s, :] for t in range(4)], 1)
 
@@ -529,12 +570,28 @@
                 acc[s, :] += one
                 gn[s, :] += two
 
+        m_in[j].s6()
+        if j == 0:
+            m_in[2].s4()
+            m_in[1].s5()
+        else:
+            before.s4()
+
         @pl.loop(0, 4)
         def _(t):
             gup = dot(n2[...], gu[t], TN).astype(BF)
             b[t // 2, t % 2, :, :, 0:96, :] = gup.reshape(4, 2, 96, 256)
             gdown = dot(cot[...], act[t], TN).astype(BF)
             b[t // 2, t % 2, :, :, 96:192, :] = gdown.reshape(4, 2, 96, 256)
+
+        if j == 2:
+            m_sum[0].take_credit()
+        m_sum[j].s1()
+        if j == 0:
+            m_in[2].s5()
+        else:
+            before.s5()
+            before.give_credit()
 
     @pl.loop(0, length // 256)
     def _(i):
@@ -563,6 +620,8 @@
 
     for one in store_low():
         one.start()
+    m_sum[2].s2()
+    o_in.s6()
 
     @pl.loop(0, 4)
     def _(t):
@@ -570,17 +629,63 @@
         act[t] = dot(n2[...], w).astype(BF)
         bo[t // 2, t % 2] = dot(n2[...], cc[t], TN).astype(BF).reshape(4, 2, 96, 256)
 
+    m_sum[1].take_credit()
+    o_sum.s1()
+    m_sum[2].s3()
+
     @pl.loop(0, 4)
     def _(t):
-        attend_back(tt, ll, kx, k2, cc, act, (dk, dv, dk2, dv2), t, length)
+        attend_back(tt, ll, kx, k2, cc, act, (dk, dv), (0, 1), t, length)
+        after(t, 0, o_sum.s2, m_sum[2].s4)
+        after(t, 1, o_sum.s3, m_sum[2].s5, m_sum[2].give_credit)
+        after(t, 2, o_sum.s4)
+        after(t, 3, o_sum.s5)
+
+    for g in q_in:
+        g.s6()
 
     @pl.loop(0, length // 256)
     def _(i):
         s = rows_of(i, 256)
-        total = jnp.zeros((256, width), F32)
+        part = jnp.zeros((256, width), F32)
         for t in range(4):
-            total = total + dot(tt[t, s, :], weight(bq, t, 0, 96, slice(0, 640)), NT)
-        back, g_gain, g_bias = norm_back(tok[s, :].astype(F32), total, par[64:65, :])
+            part = part + dot(tt[t, s, 0:384], weight(bq, t, 0, 96, slice(0, 384)), NT)
+        gn[s, :] = part
+
+    @pl.loop(0, 4)
+    def _(t):
+        bq[t // 2, t % 2, :, :, :, 0:384] = dot(n1[...], tt[t, :, 0:384], TN).astype(BF).reshape(4, 2, 96, 384)
+
+    qa_sum.s1()
+
+    @pl.loop(0, 4)
+    def _(t):
+        attend_back(tt, ll, kx, k2, cc, act, (dk, dv), (2,), t, length)
+        after(t, 0, qa_sum.s2)
+        after(t, 1, qa_sum.s3)
+        after(t, 3, qa_sum.s4)
+
+    @pl.loop(0, length // 256)
+    def _(i):
+        s = rows_of(i, 256)
+        part = gn[s, :]
+        for t in range(4):
+            part = part + dot(tt[t, s, 384:640], weight(bq, t, 0, 96, slice(384, 640)), NT)
+        gn[s, :] = part
+
+    @pl.loop(0, 4)
+    def _(t):
+        bq[t // 2, t % 2, :, :, :, 384:640] = dot(n1[...], tt[t, :, 384:640], TN).astype(BF).reshape(4, 2, 96, 256)
+
+    m_sum[2].take_credit()
+    qb_sum.s1()
+    qa_sum.s5()
+    qb_sum.s2()
+
+    @pl.loop(0, length // 256)
+    def _(i):
+        s = rows_of(i, 256)
+        back, g_gain, g_bias = norm_back(tok[s, :].astype(F32), gn[s, :], par[64:65, :])
         ar[0, 0:1, :] += g_gain
         ar[0, 1:2, :] += g_bias
         acc[s, :] = mid[s, :] + back
@@ -589,32 +694,17 @@
         return pltpu.make_async_copy(acc, gt_out, local_sem.at[4])
 
     store_grad().start()
-
-    @pl.loop(0, 4)
-    def _(t):
-        bq[t // 2, t % 2] = dot(n1[...], tt[t], TN).astype(BF).reshape(4, 2, 96, 640)
-
-    sets = [m_sets[0:6], m_sets[6:12]]
-    plan = [(bm0, 192, sets[0], gm_out.at[0]), (bm1, 192, sets[1], gm_out.at[1]),
-            (bm2, 192, sets[0], gm_out.at[2]), (bo, 96, sets[1], go_out), (bq, 96, q_set, gq_out)]
-    scatters = [
-        Scatter(inner, b, rows, slots, rs_send.at[k], rs_recv.at[k], credit.at[k], out)
-        for k, (b, rows, slots, out) in enumerate(plan)
-    ]
-    for k, s in enumerate(scatters):
-        if k in (2, 3):
-            scatters[k - 2].take_credit()
-        s.s1()
-        s.s2()
-        s.s3()
-        s.s4()
-        s.s5()
-        if k in (0, 1):
-            s.give_credit()
-    total = Total(inner, ar, ar_got, ar_send, ar_recv)
-    for stage in range(4):
-        total.run(stage)
-        total.take(stage)
+    total.run(0)
+    qb_sum.s3()
+    total.take(0)
+    total.run(1)
+    total.take(1)
+    total.run(2)
+    qb_sum.s4()
+    total.take(2)
+    total.run(3)
+    qb_sum.s5()
+    total.take(3)
     total.left()
     ar_out[...] = ar[4]
     for one in store_low():
@@ -653,16 +743,16 @@
         pltpu.VMEM((length, 1), F32),
         pltpu.VMEM((128, width), F32),
     ]
-    scratch += [pltpu.VMEM((length, 128), F32)] * 4
-    scratch += [scatter_slots(192, 256) + scatter_slots(192, 256), scatter_slots(96, 640)]
+    scratch += [pltpu.VMEM((length, 128), F32)] * 2
+    scratch += [scatter_slots(192, 256) + scatter_slots(192, 256), scatter_slots(96, 384)]
     scratch += [
         pltpu.VMEM((5, 8, width), F32),
         pltpu.VMEM((6, 8, width), F32),
         pltpu.SemaphoreType.DMA((7, 11)),
         pltpu.SemaphoreType.DMA((7, 11)),
-        pltpu.SemaphoreType.DMA((5, 8)),
-        pltpu.SemaphoreType.DMA((5, 8)),
-        pltpu.SemaphoreType.REGULAR((2, 6)),
+        pltpu.SemaphoreType.DMA((6, 8)),
+        pltpu.SemaphoreType.DMA((6, 8)),
+        pltpu.SemaphoreType.REGULAR((3, 6)),
         pltpu.SemaphoreType.DMA((6,)),
         pltpu.SemaphoreType.DMA((6,)),
         pltpu.SemaphoreType.DMA((5,)),

time: 380 us -> 245 us (0.64)
  Pallas kernels: 359 us -> 223 us
    pallas_call x1, Pallas kernels: 359 us -> 223 us  [layer(): pl.pallas_call(partial(kernel, inner, length), out_shape=(jax.ShapeDtypeS...]
where the time goes in v2:
time: 245 us; the launch traced here: 244 us
  Pallas kernels  223 us (91%)
  local copies, waits for them, and re-layouts  18 us (7%)
    pallas_call x1, Pallas kernels, layer(): pl.pallas_call(partial(kernel, inner, length), out_shape=(jax.ShapeDtypeS...  223 us
    unnamed x21, local copies, waits for them, and re-layouts  7.69 us

profile of v2, /device:TPU:0, one launch (start us, length us, event | category | flops | bytes accessed | tf_op | source)
XLA Modules:
  0.0 244.2 jit_solution(13833099356422554420)
XLA Ops:
  0.6 0.0 copy-start.3
  0.7 0.0 copy-start.4
  0.7 1.1 copy.33
  1.8 0.1 copy.34
  1.9 0.1 copy.35
  2.0 0.8 copy.36
  2.8 0.8 copy.37
  3.6 0.8 copy.38
  4.4 0.8 copy.39
  5.1 0.8 concatenate.9.wq_in
  5.9 0.9 copy.40
  6.8 0.6 pad.4.wo_in
  7.4 0.0 copy-done.3
  7.4 0.0 copy-done.4
  7.5 0.7 maximum_bitcast_fusion.wm_in
  8.2 223.3 %shard_map.203 = (bf16[1024,768]{1,0:T(8,128)(2,1)}, f32[1024,768]{1,0:T(8,128)}, f32[96,640]{1,0:T(8,128)}, f32[96,256]{1,0:T(8,128)}, f32[3,192,256]{2,1,0:T(8,128)}, /*index=5*/f32[8,768]{1,0:T(8,128)}) custom-call(bf16[1024,768]{1,0:T(8,128)(2,1)} %tok.1, bf16[1024,768]{1,0:T(8,128)(2,1)} %cot.1, s32[4,1024]{1,0:T(4,128)} %seg.1, s32[1,1024]{1,0:T(1,128)} %bitcast.50, ...), custom_call_target="tpu_custom_call" | custom-call | tf_op jit(solution)/shard_map/pallas_call | solution.py:761
  231.5 0.0 copy-start.5
  231.5 0.8 slice.53
  232.3 0.1 constant_dynamic-slice_fusion
  232.3 0.5 slice_bitcast_fusion.3
  232.9 0.0 copy-start.2
  232.9 1.0 slice.57
  233.8 0.1 copy.43
  233.9 0.1 copy.44
  234.1 0.9 slice.56
  235.0 0.1 reshape.53
  235.0 0.1 pad_maximum_fusion
  235.2 0.0 copy-start.6
  235.2 0.0 copy-start.1
  235.2 0.8 copy.47
  235.9 0.0 copy-done.5
  236.0 0.7 copy.48
  236.7 0.0 copy-done.2
  236.7 0.7 copy.51
  237.5 0.7 copy.52
  238.2 0.0 copy-done.6
  238.2 0.1 slice_reduce_fusion
  238.3 0.5 slice.66
  239.5 0.5 divide_sqrt_fusion
  240.0 0.0 copy-done.1
  240.0 0.0 copy-start
  240.0 1.1 copy.57
  241.2 1.3 copy-done
  242.5 1.7 copy.58
  (6 shorter events, 0.1 us)
Async XLA Ops:
  0.6 6.8 %copy-start.3 = (bf16[768,96]{0,1:T(8,128)(2,1)S(1)}, bf16[768,96]{0,1:T(8,128)(2,1)}, u32[]{:S(2)}) copy-start(bf16[768,96]{0,1:T(8,128)(2,1)} %param.22) | copy-start | bytes 442372
  0.7 6.8 %copy-start.4 = (bf16[96,768]{1,0:T(8,128)(2,1)S(1)}, bf16[96,768]{1,0:T(8,128)(2,1)}, u32[]{:S(2)}) copy-start(bf16[96,768]{1,0:T(8,128)(2,1)} %param.21) | copy-start | bytes 442372
  231.5 4.5 %copy-start.5 = (f32[96,256]{1,0:T(8,128)S(1)}, f32[96,256]{1,0:T(8,128)}, u32[]{:S(2)}) copy-start(f32[96,256]{1,0:T(8,128)} %get-tuple-element.21) | copy-start | bytes 294916
  232.9 3.8 %copy-start.2 = (f32[3,192,256]{2,1,0:T(8,128)S(1)}, f32[3,192,256]{2,1,0:T(8,128)}, u32[]{:S(2)}) copy-start(f32[3,192,256]{2,1,0:T(8,128)} %get-tuple-element.22) | copy-start | bytes 1769476
  235.2 3.1 %copy-start.6 = (f32[8,768]{1,0:T(8,128)S(1)}, f32[8,768]{1,0:T(8,128)}, u32[]{:S(2)}) copy-start(f32[8,768]{1,0:T(8,128)} %get-tuple-element.19) | copy-start | bytes 73732
  235.2 4.9 %copy-start.1 = (bf16[1024,768]{1,0:T(8,128)(2,1)S(1)}, bf16[1024,768]{1,0:T(8,128)(2,1)}, u32[]{:S(2)}) copy-start(bf16[1024,768]{1,0:T(8,128)(2,1)} %get-tuple-element.64) | copy-start | bytes 4718596
  240.0 2.5 %copy-start = (f32[1024,768]{1,0:T(8,128)S(1)}, f32[1024,768]{1,0:T(8,128)}, u32[]{:S(2)}) copy-start(f32[1024,768]{1,0:T(8,128)} %get-tuple-element.65) | copy-start | bytes 9437188

commit v3 on v2

v3 whole, which is shorter than its diff:
```python
from functools import partial

import jax
import jax.numpy as jnp
from jax import lax
from jax.experimental import pallas as pl
from jax.experimental.pallas import tpu as pltpu
from jax.sharding import PartitionSpec as P

HD = 64
BQ = 256
EPS = 1e-05
BIG = -1e30
F32 = jnp.float32
BF = jnp.bfloat16
NN = (((1,), (0,)), ((), ()))
NT = (((1,), (1,)), ((), ()))
TN = (((0,), (0,)), ((), ()))
MESH = pl.DeviceIdType.MESH
C0 = 0.7978845608
C1 = 0.7978845608 * 0.044715


def dot(a, b, dims=NN):
    return lax.dot_general(a, b, dims, preferred_element_type=F32)


def phase(body):
    return body


def remote(src, dst, send, recv, device):
    return pltpu.make_async_remote_copy(
        src_ref=src, dst_ref=dst, send_sem=send, recv_sem=recv,
        device_id=device, device_id_type=MESH,
    )


class Place:
    def __init__(self, inner):
        f = lax.axis_index("fsdp")
        t = lax.axis_index("tp")
        g = f // inner
        self.low = f % inner
        self.inner = inner
        self.z, self.y, self.x, self.c = g // 2, g % 2, t // 2, t % 2

    def device(self, z, y, x, c):
        return ((z * 2 + y) * self.inner + self.low, x * 2 + c)

    def core(self):
        return self.device(self.z, self.y, self.x, 1 - self.c)

    def xn(self):
        return self.device(self.z, self.y, 1 - self.x, self.c)

    def yn(self):
        return self.device(self.z, 1 - self.y, self.x, self.c)

    def cube(self, n):
        y, x, c = (self.y + n // 4) % 2, (self.x + n // 2) % 2, (self.c + n) % 2
        return self.device(self.z, y, x, c)

    def zn(self, d):
        return self.device((self.z + d) % 4, self.y, self.x, self.c)

    def zp(self, d):
        return self.device((self.z - d + 4) % 4, self.y, self.x, self.c)


def greet(inner):
    p = Place(inner)
    sem = pltpu.get_barrier_semaphore()
    for dev in [p.cube(n) for n in range(1, 8)] + [p.zn(d) for d in range(1, 4)]:
        pl.semaphore_signal(sem, inc=1, device_id=dev, device_id_type=MESH)


def met(inner):
    pl.semaphore_wait(pltpu.get_barrier_semaphore(), 10)


class Gather:
    def __init__(self, name, inner, buf, row0, rows, send, recv):
        self.name = name
        self.inner, self.buf, self.row0, self.rows = inner, buf, row0, rows
        self.send, self.recv = send, recv

    def own(self, x, c, z, y):
        return self.buf.at[x, c, z, y, pl.ds(self.row0, self.rows)]

    def group(self, x, c, y, half=None):
        start, size = self.row0, self.rows
        if half is not None:
            size = self.rows // 2
            start = self.row0 + half * size
        return self.buf.at[x, c, :, y, pl.ds(start, size)]

    def parts(self, slot):
        p = Place(self.inner)
        x, c, z, y = p.x, p.c, p.z, p.y
        if slot < 3:
            d = slot + 1
            return self.own(x, c, z, y), self.own(x, c, (z - d + 4) % 4, y), p.zn(d)
        if slot == 3:
            return self.group(x, c, y), self.group(1 - x, c, y), p.xn()
        if slot == 4:
            return self.group(x, c, y), self.group(x, c, 1 - y), p.yn()
        if slot == 5:
            return self.group(1 - x, c, y, 0), self.group(1 - x, c, 1 - y, 0), p.yn()
        if slot == 6:
            return self.group(x, c, 1 - y, 1), self.group(1 - x, c, 1 - y, 1), p.xn()
        xx = x if slot in (7, 9) else 1 - x
        yy = y if slot in (7, 8) else 1 - y
        return self.group(xx, c, yy), self.group(xx, 1 - c, yy), p.core()

    def start(self, *slots):
        for slot in slots:
            mine, _, dev = self.parts(slot)
            remote(mine, mine, self.send.at[slot], self.recv.at[slot], dev).start()

    def arrive(self, *slots):
        for slot in slots:
            _, theirs, dev = self.parts(slot)
            remote(theirs, theirs, self.send.at[slot], self.recv.at[slot], dev).wait_recv()

    def left(self, *slots):
        for slot in slots:
            mine, _, dev = self.parts(slot)
            remote(mine, mine, self.send.at[slot], self.recv.at[slot], dev).wait_send()

    def s1(self):
        self.start(0, 1, 2)

    def s2(self):
        self.arrive(0, 1, 2)
        self.start(3, 4, 7)

    def s3(self):
        self.arrive(4)
        self.start(6, 9)
        self.arrive(3)
        self.start(5, 8)

    def s4(self):
        self.arrive(5, 6)
        self.start(10)

    def near(self):
        self.arrive(7, 9)

    def far(self):
        self.arrive(8, 10)

    def s5(self):
        self.near()
        self.far()

    def s6(self):
        self.left(*range(11))


class Scatter:
    def __init__(self, name, inner, buf, rows, col0, cols, slots, send, recv, credit, out):
        self.name = name
        self.inner, self.buf, self.rows = inner, buf, rows
        self.half = (rows // 2 + 15) // 16 * 16
        self.cols = slice(col0, col0 + cols)
        self.slots, self.send, self.recv = slots, send, recv
        self.credit, self.out = credit, out

    def parts(self, slot):
        p = Place(self.inner)
        x, c, z, y = p.x, p.c, p.z, p.y
        half = self.half
        cols = self.cols
        r1, ra, rb, rx, ry, rz = self.slots
        rows, cut, rest = slice(0, self.rows), slice(0, half), slice(half, self.rows)
        buf = self.buf
        if slot == 0:
            return buf.at[:, 1 - c, :, :, rows, cols], r1.at[:, :, :, rows], p.core()
        if slot == 1:
            return buf.at[1 - x, c, :, 1 - y, cut, cols], ra.at[:, cut], p.yn()
        if slot == 2:
            return buf.at[1 - x, c, :, 1 - y, rest, cols], rb.at[:, slice(0, self.rows - half)], p.xn()
        if slot == 3:
            return buf.at[1 - x, c, :, y, rows, cols], rx.at[:, rows], p.xn()
        if slot == 4:
            return buf.at[x, c, :, 1 - y, rows, cols], ry.at[:, rows], p.yn()
        d = slot - 4
        return buf.at[x, c, (z + d) % 4, y, rows, cols], rz.at[d - 1, rows], p.zn(d)

    def start(self, *slots):
        for slot in slots:
            src, dst, dev = self.parts(slot)
            remote(src, dst, self.send.at[slot], self.recv.at[slot], dev).start()

    def arrive(self, *slots):
        for slot in slots:
            _, dst, dev = self.parts(slot)
            remote(dst, dst, self.send.at[slot], self.recv.at[slot], dev).wait_recv()

    def left(self):
        for slot in range(8):
            src, dst, dev = self.parts(slot)
            remote(src, dst, self.send.at[slot], self.recv.at[slot], dev).wait_send()

    def take_credit(self):
        for i in range(6):
            pl.semaphore_wait(self.credit.at[i], 1)

    def give_credit(self):
        p = Place(self.inner)
        for i, dev in enumerate((p.core(), p.xn(), p.yn(), p.zp(1), p.zp(2), p.zp(3))):
            pl.semaphore_signal(self.credit.at[i], inc=1, device_id=dev, device_id_type=MESH)

    def s1(self):
        self.start(0)

    def add(self, x, y, rows, *others):
        c = Place(self.inner).c

        @pl.loop(0, 4)
        def _(z):
            total = self.buf[x, c, z, y, rows, self.cols].astype(F32)
            for other in others:
                total = total + other(z).astype(F32)
            self.buf[x, c, z, y, rows, self.cols] = total.astype(BF)

    def s2(self):
        p = Place(self.inner)
        rows = slice(0, self.rows)
        r1 = self.slots[0]
        self.arrive(0)
        for x, y in ((1 - p.x, 1 - p.y), (1 - p.x, p.y), (p.x, 1 - p.y), (p.x, p.y)):
            self.add(x, y, rows, lambda z: r1[x, z, y, rows])
            if x is not p.x and y is not p.y:
                self.start(1, 2)

    def s3(self):
        p = Place(self.inner)
        half = self.half
        cut, rest = slice(0, half), slice(half, self.rows)
        ra, rb = self.slots[1:3]
        self.arrive(1)
        self.add(1 - p.x, p.y, cut, lambda z: ra[z, cut])
        self.start(3)
        self.arrive(2)
        self.add(p.x, 1 - p.y, rest, lambda z: rb[z, 0 : self.rows - half])
        self.start(4)

    def s4(self):
        p = Place(self.inner)
        rows = slice(0, self.rows)
        rx, ry = self.slots[3:5]
        self.arrive(3, 4)
        self.add(p.x, p.y, rows, lambda z: rx[z, rows], lambda z: ry[z, rows])
        self.start(5, 6, 7)

    def s5(self):
        p = Place(self.inner)
        rows = slice(0, self.rows)
        rz = self.slots[5]
        self.arrive(5, 6, 7)
        total = self.buf[p.x, p.c, p.z, p.y, rows, self.cols].astype(F32)
        for d in range(3):
            total = total + rz[d, rows].astype(F32)
        self.out(total)
        self.left()


class Total:
    def __init__(self, inner, ref, got, send, recv):
        self.inner, self.ref, self.got, self.send, self.recv = inner, ref, got, send, recv

    def copy(self, slot):
        p = Place(self.inner)
        dev = p.cube(slot + 1) if slot < 7 else p.zn(slot - 6)
        stage = 0 if slot < 7 else 1
        return remote(self.ref.at[stage], self.got.at[slot], self.send.at[slot], self.recv.at[slot], dev)

    def slots(self, stage):
        return range(7) if stage == 0 else range(7, 10)

    def run(self, stage):
        for slot in self.slots(stage):
            self.copy(slot).start()

    def take(self, stage):
        total = self.ref[stage]
        for slot in self.slots(stage):
            self.copy(slot).wait_recv()
            total = total + self.got[slot]
        self.ref[stage + 1] = total

    def left(self):
        for slot in range(10):
            self.copy(slot).wait_send()


def head_parts(t_ref, k2_ref, t, h, qs, kr):
    if h < 2:
        return t_ref[t, qs, 0:128], t_ref[t, kr, 128:256], t_ref[t, kr, 256:384]
    return t_ref[t, qs, 384:512], k2_ref[kr, :], t_ref[t, kr, 512:640]


def lanes():
    return lax.broadcasted_iota(jnp.int32, (1, 128), 1)


def roll_key(t_ref, k2_ref, t):
    k2_ref[...] = pltpu.roll(t_ref[t, :, 384:512].astype(F32), 64, 1).astype(BF)


def below(transposed):
    r = lax.broadcasted_iota(jnp.int32, (BQ, BQ), 0)
    c = lax.broadcasted_iota(jnp.int32, (BQ, BQ), 1)
    return r <= c if transposed else r >= c


def attend(t_ref, l_ref, kx_ref, k2_ref, c_ref, t, length):
    lane = lanes()
    low = lane < 64
    roll_key(t_ref, k2_ref, t)
    for i in range(length // BQ):
        first = max(0, i * BQ - length // 2)
        width = (i + 1) * BQ - first
        qs, kr = slice(i * BQ, (i + 1) * BQ), slice(first, first + width)
        kx = kx_ref[kr, :]
        doc = kx_ref[qs, :].astype(F32)
        qx = jnp.where(lane < 8, BIG * (1.0 - doc), 0.0).astype(BF)
        marks = qx
        outs = []
        for h in range(3):
            q, k, v = head_parts(t_ref, k2_ref, t, h, qs, kr)
            keep = jnp.logical_not(low) if h == 1 else low
            q = jnp.where(keep, q * BF(HD ** -0.5), BF(0))
            s = dot(jnp.concatenate([q, qx], 1), jnp.concatenate([k, kx], 1), NT)
            edge = jnp.where(below(False), s[:, width - BQ :], BIG)
            s = edge if width == BQ else jnp.concatenate([s[:, : width - BQ], edge], 1)
            top = jnp.max(s, axis=1, keepdims=True)
            p = jnp.exp(s - top).astype(BF)
            both = dot(p, jnp.concatenate([v, jnp.ones((width, 128), BF)], 1))
            total = both[:, 128:256]
            outs.append(both[:, :128] / total)
            rest = -(top + jnp.log(total))
            for n in range(3):
                piece = rest.astype(BF)
                marks = jnp.where(lane == 8 + 16 * h + n, piece, marks)
                rest = rest - piece.astype(F32)
        l_ref[t, qs, :] = marks
        c_ref[t, qs, 0:128] = jnp.where(low, outs[0], outs[1]).astype(BF)
        c_ref[t, qs, 128:256] = jnp.where(low, outs[2], 0.0).astype(BF)


def attend_back(t_ref, l_ref, kx_ref, k2_ref, c_ref, do_ref, sums, heads, t, length):
    lane = lanes()
    low = lane < 64
    dk_ref, dv_ref = sums
    odd = heads == (2,)
    if odd:
        roll_key(t_ref, k2_ref, t)
    for ref in sums:
        ref[...] = jnp.zeros_like(ref)
    for i in range(length // BQ):
        first = max(0, i * BQ - length // 2)
        width = (i + 1) * BQ - first
        qs, kr = slice(i * BQ, (i + 1) * BQ), slice(first, first + width)
        marks = l_ref[t, qs, :]
        kx = kx_ref[kr, :]
        minus = jnp.full((width, 128), -1.0, BF)
        grad = None
        for h in heads:
            q, k, v = head_parts(t_ref, k2_ref, t, h, qs, kr)
            keep = jnp.logical_not(low) if h == 1 else low
            side = slice(128, 256) if odd else slice(0, 128)
            q = jnp.where(keep, q * BF(HD ** -0.5), BF(0))
            do = jnp.where(keep, do_ref[t, qs, side], BF(0))
            km = jnp.where(keep, k, BF(0))
            dd = (do.astype(F32) * c_ref[t, qs, side].astype(F32)).astype(BF)
            mine = (lane < 8) | ((lane >= 8 + 16 * h) & (lane < 24 + 16 * h))
            qe = jnp.concatenate([q, jnp.where(mine, marks, BF(0))], 1)
            s = dot(jnp.concatenate([k, kx], 1), qe, NT)
            dp = dot(jnp.concatenate([v, minus], 1), jnp.concatenate([do, dd], 1), NT)
            edge = jnp.where(below(True), s[width - BQ :], BIG)
            s = edge if width == BQ else jnp.concatenate([s[: width - BQ], edge], 0)
            p = jnp.exp(s)
            ds = (p * dp).astype(BF)
            gq = dot(ds, km, TN)
            grad = gq if grad is None else grad + gq
            dv_ref[kr, :] += dot(p.astype(BF), do)
            dk_ref[kr, :] += dot(ds, q)
        grad = (grad * HD ** -0.5).astype(BF)
        if odd:
            t_ref[t, qs, 384:512] = jnp.where(low, grad, t_ref[t, qs, 384:512])
        else:
            t_ref[t, qs, 0:128] = grad
    if odd:
        moved = pltpu.roll(dk_ref[...], 64, 1).astype(BF)
        t_ref[t, :, 384:512] = jnp.where(low, t_ref[t, :, 384:512], moved)
        t_ref[t, :, 512:640] = dv_ref[...].astype(BF)
    else:
        t_ref[t, :, 128:256] = dk_ref[...].astype(BF)
        t_ref[t, :, 256:384] = dv_ref[...].astype(BF)


def stats(v):
    mean = jnp.mean(v, axis=-1, keepdims=True)
    center = v - mean
    scale = lax.rsqrt(jnp.mean(center * center, axis=-1, keepdims=True) + EPS)
    return center * scale, scale


def norm_back(v, q, gain):
    n, scale = stats(v)
    e = q * gain
    back = scale * (e - jnp.mean(e, -1, keepdims=True) - n * jnp.mean(e * n, -1, keepdims=True))
    return back, jnp.sum(q * n, 0, keepdims=True), jnp.sum(q, 0, keepdims=True)


def kernel(
    inner, length,
    tok_in, cot_in, seg, valid, wq_in, wo_in, up_in, down_in, par_in,
    lo_out, gt_out, gq_out, go_out, gup_out, gdown_out, *rest,
):
    small_outs = rest[: 1 if inner > 1 else 5]
    (
        bq, bo, bm0, bm1, bm2,
        tok, cot, n1, tt, cc, ll, kx, k2, mid, n2, acc, gn, act, gu, val, par,
        dk, dv,
        m_sets, ar, ar_got,
        ag_send, ag_recv, rs_send, rs_recv, credit, ar_send, ar_recv, local_sem, own_sem,
    ) = rest[len(small_outs) :]
    width = tok.shape[1]
    bm = (bm0, bm1, bm2)
    blocks = [(bq, 0, 32), (bq, 32, 32), (bq, 64, 32), (bo, 0, 96)]
    blocks += [(b, r0, 96) for b in bm for r0 in (0, 96)]
    gathers = [
        Gather(f"gather{k}", inner, b, r0, rows, ag_send.at[k], ag_recv.at[k])
        for k, (b, r0, rows) in enumerate(blocks)
    ]
    here = Place(inner)
    mine = (here.x, here.c, here.z, here.y)

    def put_mlp(j):
        def put(total):
            gup_out[:, 256 * j : 256 * j + 256] = total[0:96]
            gdown_out[:, 256 * j : 256 * j + 256] = total[96:192]

        return put

    def put_out(total):
        go_out[...] = total.T[0 : 3 * HD]

    def put_pair(total):
        gq_out[0, :, 0:128] = total[0:96, 0:128]
        gq_out[1, :, 0:128] = total[0:96, 128:256]
        gq_out[2, 0:48, 0:128] = total[96:144, 0:128]
        gq_out[2, 48:96, 0:128] = total[96:144, 128:256]

    def put_odd(total):
        gq_out[0, :, 128:192] = total[:, 0:64]
        gq_out[1, :, 128:192] = total[:, 64:128]
        gq_out[2, :, 128:192] = total[:, 128:192]

    sets = [m_sets[0:6], m_sets[6:12], m_sets[12:18]]
    plan = [
        (bm0, 192, 0, 256, sets[0], put_mlp(0)), (bm1, 192, 0, 256, sets[1], put_mlp(1)),
        (bm2, 192, 0, 256, sets[2], put_mlp(2)), (bo, 96, 0, 256, sets[0], put_out),
        (bm0, 144, 0, 256, sets[1], put_pair), (bm1, 96, 0, 256, sets[2], put_odd),
    ]
    scatters = [
        Scatter(
            f"scatter{k}", inner, b, rows, col0, cols, slots,
            rs_send.at[k], rs_recv.at[k], credit.at[min(k, 2)], out,
        )
        for k, (b, rows, col0, cols, slots, out) in enumerate(plan)
    ]
    m_sum, o_sum, qa_sum, qb_sum = scatters[0:3], scatters[3], scatters[4], scatters[5]
    q_in, o_in, m_in = gathers[0:3], gathers[3], gathers[4:10]
    total = Total(inner, ar, ar_got, ar_send, ar_recv)

    def after(t, last, *steps):
        @pl.when(t == last)
        def _():
            for step in steps:
                step()

    def rows_of(i, size):
        return pl.ds(pl.multiple_of(i * size, size), size)

    def weight(buf, t, r0, rows, columns):
        return buf[t // 2, t % 2, :, :, r0 : r0 + rows, columns].reshape(8 * rows, -1)

    def cat(ref, s):
        return jnp.concatenate([ref[t, s, :] for t in range(4)], 1)

    def own_copies():
        copies = []
        for j in range(3):
            cols = pl.ds(256 * j, 256)
            copies.append((up_in.at[:, cols], bm[j].at[(*mine, pl.ds(0, 96))]))
            copies.append((down_in.at[:, cols], bm[j].at[(*mine, pl.ds(96, 96))]))
        copies += [(tok_in, tok), (cot_in, cot)]
        return [pltpu.make_async_copy(src, dst, own_sem.at[k]) for k, (src, dst) in enumerate(copies)]

    @phase
    def entry():
        for one in own_copies():
            one.start()
        greet(inner)
        q, k, v = (wq_in[n] for n in range(3))
        for n, one in enumerate((q, k, v)):
            bq[(*mine, slice(None), slice(128 * n, 128 * n + 128))] = one[:, 0:128]
        odd = [one[:, 128:192].astype(F32) for one in (q, k, v)]
        bq[(*mine, slice(None), slice(384, 512))] = jnp.concatenate(odd[0:2], 1).astype(BF)
        params = jnp.concatenate([par_in[...], jnp.zeros((124, 96), F32)], 0).T[:, 0:64]
        bq[(*mine, slice(None), slice(512, 640))] = jnp.concatenate([odd[2], params], 1).astype(BF)
        met(inner)

    @phase
    def document_marks():
        me_t = lax.axis_index("tp")
        row = seg[pl.ds(me_t, 1), :].astype(F32)
        lane_id = lax.broadcasted_iota(jnp.int32, (128, length), 0)
        marks = jnp.where(row == lane_id.astype(F32), 1.0, 0.0)
        marks = jnp.where(lane_id < 8, marks, 0.0)
        low4 = lane_id % 16
        ones = (lane_id >= 8) & (lane_id < 56) & (low4 >= 8) & (low4 < 11)
        marks = jnp.where(ones, 1.0, marks)
        marks = jnp.where(lane_id == 64, valid[...].astype(F32), marks)
        columns = marks.T
        val[...] = columns[:, 64:65]
        kx[...] = jnp.where(lanes() < 64, columns, 0.0).astype(BF)
        ar[0] = jnp.zeros_like(ar.at[0])
        count = jnp.sum(valid[...].astype(F32), axis=1, keepdims=True)
        ar[0, 7:8, 0:128] = jnp.broadcast_to(count, (1, 128))
        wide = jnp.concatenate([wo_in[...].astype(F32), jnp.zeros((64, 96), F32)], 0)
        bo[mine] = wide.T.astype(BF)

    @phase
    def first_norm_statistics():
        @pl.loop(0, length // 256)
        def _(i):
            s = rows_of(i, 256)
            mid[s, :] = stats(tok[s, :].astype(F32))[0]

    @phase
    def first_norm():
        par[...] = bq[here.x, here.c, :, :, :, 512:640].reshape(width, 128).astype(F32).T

        @pl.loop(0, length // 256)
        def _(i):
            s = rows_of(i, 256)
            n1[s, :] = (mid[s, :] * par[64:65, :] + par[65:66, :]).astype(BF)

    @phase
    def attention():
        @pl.loop(0, 4)
        def _(n):
            x, c = (here.x + n // 2) % 2, (here.c + n % 2) % 2
            t = 2 * x + c
            w = bq[x, c].reshape(width, 640)

            @pl.loop(0, length // 512)
            def _(i):
                s = rows_of(i, 512)
                tt[t, s, :] = dot(n1[s, :], w).astype(BF)

            after(n, 0, m_in[1].s1)
            after(n, 1, o_in.s3, m_in[1].s2, m_in[3].s1)
            after(n, 2, o_in.s4)
            after(n, 3, m_in[0].s4, m_in[2].s2, m_in[5].s1)
            attend(tt, ll, kx, k2, cc, t, length)
            after(n, 0, *[g.s4 for g in q_in], *[g.near for g in q_in], m_in[0].s2, m_in[2].s1)
            after(n, 1, m_in[0].s3, m_in[4].s1)
            after(n, 2, *[g.far for g in q_in], m_in[1].s3)
            after(n, 3, o_in.s5, m_in[3].s2, m_in[1].s4)

    @phase
    def out_projection():
        @pl.loop(0, length // 256)
        def _(i):
            s = rows_of(i, 256)
            branch = jnp.zeros((256, width), F32)
            for t in range(4):
                branch = branch + dot(cc[t, s, :], weight(bo, t, 0, 96, slice(0, 256)), NT)
            v = tok[s, :].astype(F32) + branch
            mid[s, :] = v
            ar[0, 5:6, :] += jnp.sum(val[s, :] * (branch * branch), 0, keepdims=True)
            n, _ = stats(v)
            n2[s, :] = (n * par[66:67, :] + par[67:68, :]).astype(BF)

    def mlp_hidden(j, *steps):
        b = bm[j]

        @phase
        def hidden():
            @pl.loop(0, 4)
            def _(t):
                up = weight(b, t, 0, 96, slice(0, 256))
                down = weight(b, t, 96, 96, slice(0, 256))

                for i in range(length // 512):
                    s = slice(512 * i, 512 * i + 512)
                    v = dot(n2[s, :], up)
                    ga = dot(cot[s, :], down)
                    v2 = v * v
                    th = jnp.tanh(v * (C0 + C1 * v2))
                    h = 0.5 + 0.5 * th
                    act[t, s, :] = (v * h).astype(BF)
                    slope = h + (0.5 * v) * (1.0 - th * th) * (C0 + (3.0 * C1) * v2)
                    gu[t, s, :] = (ga * slope).astype(BF)

                for k, step in enumerate(steps):
                    after(t, k, *step)

        hidden()

    def mlp_sums(j, *steps):
        b = bm[j]

        def wcat(r0):
            return jnp.concatenate([weight(b, t, r0, 96, slice(0, 256)) for t in range(4)], 1)

        @phase
        def sums():
            @pl.loop(0, length // 256)
            def _(i):
                s = rows_of(i, 256)
                one = dot(cat(act, s), wcat(96), NT)
                two = dot(cat(gu, s), wcat(0), NT)
                if j == 0:
                    acc[s, :] = one
                    gn[s, :] = two
                else:
                    acc[s, :] += one
                    gn[s, :] += two
                for k, step in enumerate(steps):
                    after(i, k, *step)

        sums()

    def mlp_weight_grads(j):
        b = bm[j]

        @phase
        def weight_grads():
            @pl.loop(0, 4)
            def _(t):
                gup = dot(n2[...], gu[t], TN).astype(BF)
                b[t // 2, t % 2, :, :, 0:96, :] = gup.reshape(4, 2, 96, 256)
                gdown = dot(cot[...], act[t], TN).astype(BF)
                b[t // 2, t % 2, :, :, 96:192, :] = gdown.reshape(4, 2, 96, 256)

        weight_grads()

    def store_low():
        return [
            pltpu.make_async_copy(gu.at[k], lo_out.at[:, pl.ds(256 * k, 256)], local_sem.at[k])
            for k in range(width // 256)
        ]

    @phase
    def second_norm_back():
        @pl.loop(0, length // 256)
        def _(i):
            s = rows_of(i, 256)
            v = mid[s, :]
            mlp = acc[s, :]
            out = v + mlp
            weight_rows = val[s, :]
            ar[0, 4:5, :] += jnp.sum(weight_rows * (out * out), 0, keepdims=True)
            ar[0, 6:7, :] += jnp.sum(weight_rows * (mlp * mlp), 0, keepdims=True)
            low_out = out.astype(BF)
            for k in range(width // 256):
                gu[k, s, :] = low_out[:, 256 * k : 256 * k + 256]
            back, g_gain, g_bias = norm_back(v, gn[s, :], par[66:67, :])
            ar[0, 2:3, :] += g_gain
            ar[0, 3:4, :] += g_bias
            grad = cot[s, :].astype(F32) + back
            mid[s, :] = grad
            n2[s, :] = grad.astype(BF)

        for one in store_low():
            one.start()

    @phase
    def out_projection_back():
        @pl.loop(0, 4)
        def _(t):
            w = weight(bo, t, 0, 96, slice(0, 256))
            act[t] = dot(n2[...], w).astype(BF)
            bo[t // 2, t % 2] = dot(n2[...], cc[t], TN).astype(BF).reshape(4, 2, 96, 256)

    @phase
    def pair_attention_back():
        @pl.loop(0, 4)
        def _(t):
            attend_back(tt, ll, kx, k2, cc, act, (dk, dv), (0, 1), t, length)
            after(t, 0, o_sum.s2, m_sum[2].s3)
            after(t, 1, m_sum[1].s5, m_sum[1].give_credit, o_sum.s3)
            after(t, 2, m_sum[2].s4)
            after(t, 3, o_sum.s4)

    @phase
    def pair_weight_grads():
        @pl.loop(0, 4)
        def _(t):
            grad = dot(n1[...], tt[t, :, 0:384], TN).astype(BF)
            x, c = t // 2, t % 2
            bm0[x, c, :, :, 0:96, :] = grad[:, 0:256].reshape(4, 2, 96, 256)
            third = grad[:, 256:384].reshape(4, 2, 96, 128)
            bm0[x, c, :, :, 96:144, 0:128] = third[:, :, 0:48]
            bm0[x, c, :, :, 96:144, 128:256] = third[:, :, 48:96]

    @phase
    def odd_weight_grads():
        @pl.loop(0, 4)
        def _(t):
            grad = dot(n1[...], tt[t, :, 384:640], TN).astype(BF)
            bm1[t // 2, t % 2, :, :, 0:96, :] = grad.reshape(4, 2, 96, 256)

    @phase
    def odd_attention_back():
        @pl.loop(0, 4)
        def _(t):
            attend_back(tt, ll, kx, k2, cc, act, (dk, dv), (2,), t, length)
            after(t, 0, qa_sum.s2, o_sum.s5)
            after(t, 1, m_sum[2].s5, m_sum[2].give_credit)
            after(t, 2, qa_sum.s3)

    def store_grad():
        return pltpu.make_async_copy(acc, gt_out, local_sem.at[4])

    @phase
    def first_norm_back():
        @pl.loop(0, length // 256)
        def _(i):
            s = rows_of(i, 256)
            grad = jnp.zeros((256, width), F32)
            for t in range(4):
                grad = grad + dot(tt[t, s, :], weight(bq, t, 0, 96, slice(0, 640)), NT)
            back, g_gain, g_bias = norm_back(tok[s, :].astype(F32), grad, par[64:65, :])
            ar[0, 0:1, :] += g_gain
            ar[0, 1:2, :] += g_bias
            acc[s, :] = mid[s, :] + back
            after(i, 0, qb_sum.s2)
            after(i, 1, qa_sum.s4)
            after(i, 2, qb_sum.s3)

        store_grad().start()

    @phase
    def small_results():
        sums = ar[2]
        if inner > 1:
            small_outs[0][...] = sums
            return
        share = width // 32
        owner = lax.axis_index("fsdp") * 4 + lax.axis_index("tp")
        moved = pltpu.roll(sums, width - owner * share, 1)
        for k in range(4):
            small_outs[k][...] = moved[k, 0:share]
        square = jnp.sum(sums[4:7], axis=1, keepdims=True) / (sums[7:8, 0:1] * width)
        rms = jnp.sqrt(jnp.broadcast_to(square, (3, 128)))
        lane = lanes()
        row = jnp.where(lane == 0, rms[0:1], jnp.where(lane == 1, rms[1:2], rms[2:3]))
        small_outs[4][...] = row[0, 0:3]

    entry()
    for g in q_in:
        g.s1()
    document_marks()
    own = own_copies()
    for one in own:
        one.wait()
    first_norm_statistics()
    q_in[0].s2()
    q_in[1].s2()
    q_in[0].s3()
    q_in[2].s2()
    o_in.s1()
    q_in[1].s3()
    m_in[0].s1()
    q_in[2].s3()
    first_norm()
    o_in.s2()
    attention()
    out_projection()
    m_in[0].s5()
    m_in[1].s5()

    mlp_hidden(0, (m_in[2].s3,), (m_in[4].s2,), (m_in[3].s3,))
    mlp_sums(0, (m_in[2].s4, m_in[5].s2), (m_in[4].s3,), (m_in[3].s4,))
    m_in[0].s6()
    m_in[1].s6()
    mlp_weight_grads(0)
    m_in[5].s3()
    m_sum[0].s1()
    m_in[2].s5()
    m_in[3].s5()

    mlp_hidden(1, (m_in[4].s4,), (), (m_sum[0].s2,))
    m_in[5].s4()
    mlp_sums(1)
    m_sum[0].s3()
    m_in[2].s6()
    m_in[3].s6()
    m_in[4].s5()
    m_in[5].s5()
    mlp_weight_grads(1)
    m_sum[1].s1()

    mlp_hidden(2, (), (), (m_sum[1].s2,))
    m_sum[0].s4()
    mlp_sums(2)
    m_sum[1].s3()
    m_in[4].s6()
    m_in[5].s6()
    mlp_weight_grads(2)
    m_sum[2].s1()

    second_norm_back()
    m_sum[2].s2()
    m_sum[0].s5()
    m_sum[0].give_credit()
    o_in.s6()
    out_projection_back()
    m_sum[1].s4()
    m_sum[0].take_credit()
    o_sum.s1()
    pair_attention_back()
    pair_weight_grads()
    m_sum[1].take_credit()
    qa_sum.s1()
    odd_attention_back()
    odd_weight_grads()
    m_sum[2].take_credit()
    qb_sum.s1()
    for g in q_in:
        g.s6()
    first_norm_back()
    total.run(0)
    total.take(0)
    total.run(1)
    qb_sum.s4()
    qa_sum.s5()
    total.take(1)
    total.left()
    small_results()
    for one in store_low():
        one.wait()
    store_grad().wait()
    qb_sum.s5()


def scatter_slots(rows, columns):
    return [
        pltpu.VMEM((2, 4, 2, rows, columns), BF),
        pltpu.VMEM((4, (rows // 2 + 15) // 16 * 16, columns), BF),
        pltpu.VMEM((4, rows // 2, columns), BF),
        pltpu.VMEM((4, rows, columns), BF),
        pltpu.VMEM((4, rows, columns), BF),
        pltpu.VMEM((3, rows, columns), BF),
    ]


def layer(inner, tokens, cotangent, segments, valid, wq, wo, up, down, params):
    length, width = tokens.shape
    block = lambda rows, columns: pltpu.VMEM((2, 2, 4, 2, rows, columns), BF)
    scratch = [
        block(96, 640), block(96, 256), block(192, 256), block(192, 256), block(192, 256),
        pltpu.VMEM((length, width), BF),
        pltpu.VMEM((length, width), BF),
        pltpu.VMEM((length, width), BF),
        pltpu.VMEM((4, length, 640), BF),
        pltpu.VMEM((4, length, 256), BF),
        pltpu.VMEM((4, length, 128), BF),
        pltpu.VMEM((length, 128), BF),
        pltpu.VMEM((length, 128), BF),
        pltpu.VMEM((length, width), F32),
        pltpu.VMEM((length, width), BF),
        pltpu.VMEM((length, width), F32),
        pltpu.VMEM((length, width), F32),
        pltpu.VMEM((4, length, 256), BF),
        pltpu.VMEM((4, length, 256), BF),
        pltpu.VMEM((length, 1), F32),
        pltpu.VMEM((128, width), F32),
    ]
    scratch += [pltpu.VMEM((length, 128), F32)] * 2
    scratch += [scatter_slots(192, 256) * 3]
    scratch += [
        pltpu.VMEM((3, 8, width), F32),
        pltpu.VMEM((10, 8, width), F32),
        pltpu.SemaphoreType.DMA((10, 11)),
        pltpu.SemaphoreType.DMA((10, 11)),
        pltpu.SemaphoreType.DMA((6, 8)),
        pltpu.SemaphoreType.DMA((6, 8)),
        pltpu.SemaphoreType.REGULAR((3, 6)),
        pltpu.SemaphoreType.DMA((10,)),
        pltpu.SemaphoreType.DMA((10,)),
        pltpu.SemaphoreType.DMA((5,)),
        pltpu.SemaphoreType.DMA((8,)),
    ]
    vmem, anywhere = pl.BlockSpec(memory_space=pltpu.VMEM), pl.BlockSpec(memory_space=pl.ANY)
    small = [(8, width)] if inner > 1 else [(width // 32,)] * 4 + [(3,)]
    shapes = [(3, 96, 3 * HD), (3 * HD, 96), (96, width), (96, width)] + small
    return pl.pallas_call(
        partial(kernel, inner, length),
        out_shape=[
            jax.ShapeDtypeStruct((length, width), BF),
            jax.ShapeDtypeStruct((length, width), F32),
        ]
        + [jax.ShapeDtypeStruct(shape, F32) for shape in shapes],
        in_specs=[anywhere, anywhere, vmem, vmem, vmem, vmem, anywhere, anywhere, vmem],
        out_specs=[anywhere, anywhere] + [vmem] * len(shapes),
        scratch_shapes=scratch,
        compiler_params=pltpu.CompilerParams(
            collective_id=0, has_side_effects=True, vmem_limit_bytes=63 * 2**20
        ),
    )(tokens, cotangent, segments, valid, wq, wo, up, down, params)


def hand_over(arrays):
    count = len(arrays)
    pieces = []
    for k, a in enumerate(arrays):
        step = 256 if a.ndim == 2 and a.shape[0] % 256 == 0 else a.shape[0]
        pieces += [(k, start, step) for start in range(0, a.shape[0], step)]

    def body(*refs):
        came, went, held = refs[:count], refs[count : 2 * count], refs[2 * count : 3 * count]
        sems = refs[-1]

        def copy(n, into):
            k, start, step = pieces[n]
            part = (lambda ref: ref.at[pl.ds(start, step)]) if step < came[k].shape[0] else (lambda ref: ref)
            if into:
                return pltpu.make_async_copy(part(came[k]), part(held[k]), sems.at[0, n])
            return pltpu.make_async_copy(part(held[k]), part(went[k]), sems.at[1, n])

        for n in range(len(pieces)):
            copy(n, True).start()
        for n in range(len(pieces)):
            copy(n, True).wait()
            copy(n, False).start()
        for n in range(len(pieces)):
            copy(n, False).wait()

    anywhere = pl.BlockSpec(memory_space=pltpu.HBM)
    return pl.pallas_call(
        body,
        out_shape=[jax.ShapeDtypeStruct(a.shape, a.dtype) for a in arrays],
        in_specs=[anywhere] * count,
        out_specs=[anywhere] * count,
        scratch_shapes=[pltpu.VMEM(a.shape, a.dtype) for a in arrays]
        + [pltpu.SemaphoreType.DMA((2, len(pieces)))],
        compiler_params=pltpu.CompilerParams(vmem_limit_bytes=63 * 2**20),
    )(*arrays)


def local(
    tokens, segment_ids, valid, ln1_gain, ln1_bias, w_qkv, w_out, ln2_gain, ln2_bias, w_up, w_down, cotangent
):
    length, width = tokens.shape
    holders = lax.axis_size("fsdp")
    inner = holders // 8
    groups = [[g * inner + i for i in range(inner)] for g in range(8)]

    def widen(block, axis=0):
        if inner == 1:
            return block
        return lax.all_gather(block, "fsdp", axis_index_groups=groups, axis=axis, tiled=True)

    def narrow(block, axis=0):
        if inner == 1:
            return block
        return lax.psum_scatter(
            block, "fsdp", scatter_dimension=axis, axis_index_groups=groups, tiled=True
        )

    params = widen(jnp.stack([ln1_gain, ln1_bias, ln2_gain, ln2_bias]), 1).astype(F32)
    results = layer(
        inner, tokens, cotangent, segment_ids, valid.reshape(1, length),
        widen(w_qkv.transpose(1, 0, 2), 1), widen(w_out, 1), widen(w_up), widen(w_down.T), params,
    )
    low, grad_tokens, gq, go, gup, gdown, *small = hand_over(results)
    if inner > 1:
        sums = lax.psum(small[0], "fsdp", axis_index_groups=groups)
        share = width // (holders * lax.axis_size("tp"))
        owner = lax.axis_index("fsdp") * lax.axis_size("tp") + lax.axis_index("tp")
        mine = lax.dynamic_slice_in_dim(sums[0:4], owner * share, share, 1)
        spread = jnp.sqrt(jnp.sum(sums[4:7], axis=1) / (sums[7, 0] * width))
        small = (mine[0], mine[1], mine[2], mine[3], spread)
    return (
        low, grad_tokens, small[0], small[1], narrow(gq, 1).transpose(1, 0, 2), narrow(go, 1),
        small[2], small[3], narrow(gup), narrow(gdown).T, small[4],
    )


def solution(mesh):
    both = ("fsdp", "tp")
    return jax.shard_map(
        local,
        mesh=mesh,
        in_specs=(
            P(both, None), P("fsdp", None), P(both), P("fsdp"), P("fsdp"), P("fsdp", None, "tp"),
            P("tp", "fsdp"), P("fsdp"), P("fsdp"), P("fsdp", "tp"), P("tp", "fsdp"), P(both, None),
        ),
        out_specs=(
            P(both, None), P(both, None), P(both), P(both), P("fsdp", None, "tp"), P("tp", "fsdp"),
            P(both), P(both), P("fsdp", "tp"), P("tp", "fsdp"), P(),
        ),
        check_vma=False,
    )
```

time: 245 us -> 187 us (0.76)
  Pallas kernels: 223 us -> 184 us
  local copies, waits for them, and re-layouts: 18 us -> 0 us
    pallas_call x1 -> x2, Pallas kernels: 223 us -> 184 us  [the longest x1 179 us: layer(): pl.pallas_call(partial(kernel, inner, length), out_shape=[jax.ShapeDtypeS...]
    unnamed x21 -> x0, local copies, waits for them, and re-layouts: 7.69 us -> none
    slice x9 -> x0, local copies, waits for them, and re-layouts: 4.74 us -> none  [the longest x2 1.05 us: local(): one = gq[:, 6 * HD:9 * HD].reshape(rows, 3, HD)]
    another operation x5 -> x0, local copies, waits for them, and re-layouts: 3.19 us -> none  [the longest x4 3.1 us: local(): params = jnp.stack([ln1_gain, ln1_bias, ln2_gain, ln2_bias], axis=1)]
where the time goes in v3:
time: 187 us; the launch traced here: 186 us
  Pallas kernels  184 us (98%)
    pallas_call x1, Pallas kernels, layer(): pl.pallas_call(partial(kernel, inner, length), out_shape=[jax.ShapeDtypeS...  179 us
    pallas_call x1, Pallas kernels, hand_over(): pl.pallas_call(body, out_shape=[jax.ShapeDtypeStruct(a.shape, a.dtype) fo...  5.04 us

profile of v3, /device:TPU:0, one launch (start us, length us, event | category | flops | bytes accessed | tf_op | source)
XLA Modules:
  0.0 186.3 jit_solution(13476979919562640399)
XLA Ops:
  0.6 1.3 maximum_convert_fusion.par_in
  1.9 179.1 %shard_map.203 = (bf16[1024,768]{1,0:T(8,128)(2,1)}, f32[1024,768]{1,0:T(8,128)}, f32[3,96,192]{2,1,0:T(8,128)}, f32[192,96]{1,0:T(8,128)}, f32[96,768]{1,0:T(8,...) custom-call(bf16[1024,768]{1,0:T(8,128)(2,1)} %tok_in.1, ...), custom_call_target="tpu_custom_call" | custom-call | tf_op jit(solution)/shard_map/pallas_call | solution.py:908
  181.0 5.0 %shard_map.204 = (bf16[1024,768]{1,0:T(8,128)(2,1)}, f32[1024,768]{1,0:T(8,128)}, f32[3,96,192]{2,1,0:T(8,128)}, f32[192,96]{1,0:T(8,128)}, f32[96,768]{1,0:T(8,...) custom-call(bf16[1024,768]{1,0:T(8,128)(2,1)} %get-tuple-element.33., ...), custom_call_target="tpu_custom_call" | custom-call | tf_op jit(solution)/shard_map/pallas_call | solution.py:951

commit v4 on v3

--- a/solution.py
+++ b/solution.py
@@ -160,34 +160,43 @@
 
 
 class Scatter:
-    def __init__(self, name, inner, buf, rows, col0, cols, slots, send, recv, credit, out):
+    def __init__(self, name, inner, buf, block, slots, place, send, recv, credit, out):
         self.name = name
-        self.inner, self.buf, self.rows = inner, buf, rows
-        self.half = (rows // 2 + 15) // 16 * 16
-        self.cols = slice(col0, col0 + cols)
-        self.slots, self.send, self.recv = slots, send, recv
+        self.inner, self.buf, self.slots = inner, buf, slots
+        self.row0, self.rows, self.col0, columns = block
+        self.half = (self.rows // 2 + 15) // 16 * 16
+        row, upper, lower, col = place
+        self.land = (
+            slice(row, row + self.rows), slice(upper, upper + self.half),
+            slice(lower, lower + self.rows - self.half), slice(col, col + columns),
+        )
+        self.cols = slice(self.col0, self.col0 + columns)
+        self.send, self.recv = send, recv
         self.credit, self.out = credit, out
 
     def parts(self, slot):
         p = Place(self.inner)
         x, c, z, y = p.x, p.c, p.z, p.y
-        half = self.half
-        cols = self.cols
+        buf, cols = self.buf, self.cols
         r1, ra, rb, rx, ry, rz = self.slots
-        rows, cut, rest = slice(0, self.rows), slice(0, half), slice(half, self.rows)
-        buf = self.buf
+        rows, upper, lower = self.spans()
+        land, land_a, land_b, land_cols = self.land
         if slot == 0:
-            return buf.at[:, 1 - c, :, :, rows, cols], r1.at[:, :, :, rows], p.core()
+            return buf.at[:, 1 - c, :, :, rows, cols], r1.at[:, :, :, land, land_cols], p.core()
         if slot == 1:
-            return buf.at[1 - x, c, :, 1 - y, cut, cols], ra.at[:, cut], p.yn()
+            return buf.at[1 - x, c, :, 1 - y, upper, cols], ra.at[:, land_a, land_cols], p.yn()
         if slot == 2:
-            return buf.at[1 - x, c, :, 1 - y, rest, cols], rb.at[:, slice(0, self.rows - half)], p.xn()
+            return buf.at[1 - x, c, :, 1 - y, lower, cols], rb.at[:, land_b, land_cols], p.xn()
         if slot == 3:
-            return buf.at[1 - x, c, :, y, rows, cols], rx.at[:, rows], p.xn()
+            return buf.at[1 - x, c, :, y, rows, cols], rx.at[:, land, land_cols], p.xn()
         if slot == 4:
-            return buf.at[x, c, :, 1 - y, rows, cols], ry.at[:, rows], p.yn()
+            return buf.at[x, c, :, 1 - y, rows, cols], ry.at[:, land, land_cols], p.yn()
         d = slot - 4
-        return buf.at[x, c, (z + d) % 4, y, rows, cols], rz.at[d - 1, rows], p.zn(d)
+        return buf.at[x, c, (z + d) % 4, y, rows, cols], rz.at[d - 1, land, land_cols], p.zn(d)
+
+    def spans(self):
+        start, end = self.row0, self.row0 + self.rows
+        return slice(start, end), slice(start, start + self.half), slice(start + self.half, end)
 
     def start(self, *slots):
         for slot in slots:
@@ -228,48 +237,48 @@
 
     def s2(self):
         p = Place(self.inner)
-        rows = slice(0, self.rows)
-        r1 = self.slots[0]
+        r1, (land, _, _, cols) = self.slots[0], self.land
         self.arrive(0)
         for x, y in ((1 - p.x, 1 - p.y), (1 - p.x, p.y), (p.x, 1 - p.y), (p.x, p.y)):
-            self.add(x, y, rows, lambda z: r1[x, z, y, rows])
+            self.add(x, y, self.spans()[0], lambda z: r1[x, z, y, land, cols])
             if x is not p.x and y is not p.y:
                 self.start(1, 2)
 
     def s3(self):
         p = Place(self.inner)
-        half = self.half
-        cut, rest = slice(0, half), slice(half, self.rows)
+        _, upper, lower = self.spans()
+        _, land_a, land_b, cols = self.land
         ra, rb = self.slots[1:3]
         self.arrive(1)
-        self.add(1 - p.x, p.y, cut, lambda z: ra[z, cut])
+        self.add(1 - p.x, p.y, upper, lambda z: ra[z, land_a, cols])
         self.start(3)
         self.arrive(2)
-        self.add(p.x, 1 - p.y, rest, lambda z: rb[z, 0 : self.rows - half])
+        self.add(p.x, 1 - p.y, lower, lambda z: rb[z, land_b, cols])
         self.start(4)
 
     def s4(self):
         p = Place(self.inner)
-        rows = slice(0, self.rows)
+        land, _, _, cols = self.land
         rx, ry = self.slots[3:5]
         self.arrive(3, 4)
-        self.add(p.x, p.y, rows, lambda z: rx[z, rows], lambda z: ry[z, rows])
+        self.add(p.x, p.y, self.spans()[0], lambda z: rx[z, land, cols], lambda z: ry[z, land, cols])
         self.start(5, 6, 7)
 
     def s5(self):
         p = Place(self.inner)
-        rows = slice(0, self.rows)
+        land, _, _, cols = self.land
         rz = self.slots[5]
         self.arrive(5, 6, 7)
-        total = self.buf[p.x, p.c, p.z, p.y, rows, self.cols].astype(F32)
+        total = self.buf[p.x, p.c, p.z, p.y, self.spans()[0], self.cols].astype(F32)
         for d in range(3):
-            total = total + rz[d, rows].astype(F32)
+            total = total + rz[d, land, cols].astype(F32)
         self.out(total)
         self.left()
 
 
 class Total:
-    def __init__(self, inner, ref, got, send, recv):
+    def __init__(self, name, inner, ref, got, send, recv):
+        self.name = name
         self.inner, self.ref, self.got, self.send, self.recv = inner, ref, got, send, recv
 
     def copy(self, slot):
@@ -352,13 +361,16 @@
         c_ref[t, qs, 128:256] = jnp.where(low, outs[2], 0.0).astype(BF)
 
 
-def attend_back(t_ref, l_ref, kx_ref, k2_ref, c_ref, do_ref, sums, heads, t, length):
+def attend_back(t_ref, l_ref, kx_ref, k2_ref, kt_ref, c_ref, do_ref, sums, heads, t, length):
     lane = lanes()
     low = lane < 64
     dk_ref, dv_ref = sums
     odd = heads == (2,)
     if odd:
         roll_key(t_ref, k2_ref, t)
+        kt_ref[...] = k2_ref[...].T
+    else:
+        kt_ref[...] = t_ref[t, :, 128:256].T
     for ref in sums:
         ref[...] = jnp.zeros_like(ref)
     for i in range(length // BQ):
@@ -366,30 +378,37 @@
         width = (i + 1) * BQ - first
         qs, kr = slice(i * BQ, (i + 1) * BQ), slice(first, first + width)
         marks = l_ref[t, qs, :]
-        kx = kx_ref[kr, :]
-        minus = jnp.full((width, 128), -1.0, BF)
-        grad = None
+        side = slice(128, 256) if odd else slice(0, 128)
+        qs_all, dos, left, right = [], [], [], []
         for h in heads:
             q, k, v = head_parts(t_ref, k2_ref, t, h, qs, kr)
             keep = jnp.logical_not(low) if h == 1 else low
-            side = slice(128, 256) if odd else slice(0, 128)
             q = jnp.where(keep, q * BF(HD ** -0.5), BF(0))
             do = jnp.where(keep, do_ref[t, qs, side], BF(0))
-            km = jnp.where(keep, k, BF(0))
             dd = (do.astype(F32) * c_ref[t, qs, side].astype(F32)).astype(BF)
             mine = (lane < 8) | ((lane >= 8 + 16 * h) & (lane < 24 + 16 * h))
-            qe = jnp.concatenate([q, jnp.where(mine, marks, BF(0))], 1)
-            s = dot(jnp.concatenate([k, kx], 1), qe, NT)
-            dp = dot(jnp.concatenate([v, minus], 1), jnp.concatenate([do, dd], 1), NT)
+            qs_all.append(q)
+            dos.append(do)
+            left.append(jnp.concatenate([q, jnp.where(mine, marks, BF(0))], 1))
+            right.append(jnp.concatenate([do, dd], 1))
+        s_all = dot(jnp.concatenate([k, kx_ref[kr, :]], 1), jnp.concatenate(left, 0), NT)
+        minus = jnp.full((width, 128), -1.0, BF)
+        dp_all = dot(jnp.concatenate([v, minus], 1), jnp.concatenate(right, 0), NT)
+        ps, dss, grads = [], [], []
+        for n in range(len(heads)):
+            s = s_all[:, n * BQ : (n + 1) * BQ]
             edge = jnp.where(below(True), s[width - BQ :], BIG)
             s = edge if width == BQ else jnp.concatenate([s[: width - BQ], edge], 0)
             p = jnp.exp(s)
-            ds = (p * dp).astype(BF)
-            gq = dot(ds, km, TN)
-            grad = gq if grad is None else grad + gq
-            dv_ref[kr, :] += dot(p.astype(BF), do)
-            dk_ref[kr, :] += dot(ds, q)
-        grad = (grad * HD ** -0.5).astype(BF)
+            ds = (p * dp_all[:, n * BQ : (n + 1) * BQ]).astype(BF)
+            ps.append(p.astype(BF))
+            dss.append(ds)
+            grads.append(dot(kt_ref[64 * n : 64 * n + 64, kr], ds))
+        if odd:
+            grads.append(jnp.zeros((64, BQ), F32))
+        grad = (jnp.concatenate(grads, 0).T * HD ** -0.5).astype(BF)
+        dv_ref[kr, :] += dot(jnp.concatenate(ps, 1), jnp.concatenate(dos, 0))
+        dk_ref[kr, :] += dot(jnp.concatenate(dss, 1), jnp.concatenate(qs_all, 0))
         if odd:
             t_ref[t, qs, 384:512] = jnp.where(low, grad, t_ref[t, qs, 384:512])
         else:
@@ -420,16 +439,17 @@
 def kernel(
     inner, length,
     tok_in, cot_in, seg, valid, wq_in, wo_in, up_in, down_in, par_in,
-    lo_out, gt_out, gq_out, go_out, gup_out, gdown_out, *rest,
+    lo_out, gt_out, *rest,
 ):
-    small_outs = rest[: 1 if inner > 1 else 5]
+    big_outs = rest[0:5]
     (
-        bq, bo, bm0, bm1, bm2,
-        tok, cot, n1, tt, cc, ll, kx, k2, mid, n2, acc, gn, act, gu, val, par,
+        gq_out, go_out, gup_out, gdown_out, small_out,
+        bq, bo, bm0, bm1, bm2, gb,
+        tok, cot, n1, tt, cc, ll, kx, k2, kt, mid, n2, acc, gn, act, gu, val, par,
         dk, dv,
-        m_sets, ar, ar_got,
-        ag_send, ag_recv, rs_send, rs_recv, credit, ar_send, ar_recv, local_sem, own_sem,
-    ) = rest[len(small_outs) :]
+        m_sets, ar, ar_got, br, br_got, g1,
+        ag_send, ag_recv, rs_send, rs_recv, credit, ar_send, ar_recv, local_sem, own_sem, give_sem,
+    ) = rest[5:]
     width = tok.shape[1]
     bm = (bm0, bm1, bm2)
     blocks = [(bq, 0, 32), (bq, 32, 32), (bq, 64, 32), (bo, 0, 96)]
@@ -449,7 +469,9 @@
         return put
 
     def put_out(total):
-        go_out[...] = total.T[0 : 3 * HD]
+        go_out[0 : 2 * HD] = total[0:96].T
+        third = total[96:144].T
+        go_out[2 * HD : 3 * HD] = jnp.concatenate([third[0:64], third[64:128]], 1)
 
     def put_pair(total):
         gq_out[0, :, 0:128] = total[0:96, 0:128]
@@ -458,26 +480,38 @@
         gq_out[2, 48:96, 0:128] = total[96:144, 128:256]
 
     def put_odd(total):
-        gq_out[0, :, 128:192] = total[:, 0:64]
-        gq_out[1, :, 128:192] = total[:, 64:128]
-        gq_out[2, :, 128:192] = total[:, 128:192]
-
+        gq_out[0, 0:80, 128:192] = total[:, 0:64]
+        gq_out[1, 0:80, 128:192] = total[:, 64:128]
+
+    def put_rest(total):
+        gq_out[0, 80:96, 128:192] = total[0:16, 0:64]
+        gq_out[1, 80:96, 128:192] = total[0:16, 64:128]
+        gq_out[2, 0:48, 128:192] = total[16:64, 0:64]
+        gq_out[2, 48:96, 128:192] = total[16:64, 64:128]
+
+    grads = (gb, bm0, bm1)
     sets = [m_sets[0:6], m_sets[6:12], m_sets[12:18]]
+    start = (0, 0, 0, 0)
     plan = [
-        (bm0, 192, 0, 256, sets[0], put_mlp(0)), (bm1, 192, 0, 256, sets[1], put_mlp(1)),
-        (bm2, 192, 0, 256, sets[2], put_mlp(2)), (bo, 96, 0, 256, sets[0], put_out),
-        (bm0, 144, 0, 256, sets[1], put_pair), (bm1, 96, 0, 256, sets[2], put_odd),
+        (gb, (0, 192, 0, 256), sets[0], start, put_mlp(0)),
+        (bm0, (0, 192, 0, 256), sets[1], start, put_mlp(1)),
+        (bm1, (0, 192, 0, 256), sets[2], start, put_mlp(2)),
+        (bm2, (0, 144, 0, 128), sets[0], start, put_out),
+        (gb, (0, 144, 0, 256), sets[1], start, put_pair),
+        (bm2, (0, 80, 128, 128), sets[0], (0, 0, 0, 128), put_odd),
+        (bm2, (80, 64, 128, 128), sets[0], (80, 48, 32, 128), put_rest),
     ]
     scatters = [
         Scatter(
-            f"scatter{k}", inner, b, rows, col0, cols, slots,
-            rs_send.at[k], rs_recv.at[k], credit.at[min(k, 2)], out,
+            f"scatter{k}", inner, b, block, slots, place,
+            rs_send.at[k], rs_recv.at[k], credit.at[min(k, 1)], out,
         )
-        for k, (b, rows, col0, cols, slots, out) in enumerate(plan)
+        for k, (b, block, slots, place, out) in enumerate(plan)
     ]
-    m_sum, o_sum, qa_sum, qb_sum = scatters[0:3], scatters[3], scatters[4], scatters[5]
+    m_sum, o_sum, qa_sum, qb_sum, qc_sum = scatters[0:3], *scatters[3:7]
     q_in, o_in, m_in = gathers[0:3], gathers[3], gathers[4:10]
-    total = Total(inner, ar, ar_got, ar_send, ar_recv)
+    early = Total("early", inner, ar, ar_got, ar_send.at[0], ar_recv.at[0])
+    late = Total("late", inner, br, br_got, ar_send.at[1], ar_recv.at[1])
 
     def after(t, last, *steps):
         @pl.when(t == last)
@@ -490,6 +524,11 @@
 
     def weight(buf, t, r0, rows, columns):
         return buf[t // 2, t % 2, :, :, r0 : r0 + rows, columns].reshape(8 * rows, -1)
+
+    def fold(columns):
+        parts = columns.reshape(8, 96, 64)
+        halves = [parts[:, 48 * n : 48 * n + 48].reshape(8 * 48, 64) for n in range(2)]
+        return jnp.concatenate(halves, 1).astype(BF).reshape(4, 2, 48, 128)
 
     def cat(ref, s):
         return jnp.concatenate([ref[t, s, :] for t in range(4)], 1)
@@ -532,6 +571,8 @@
         val[...] = columns[:, 64:65]
         kx[...] = jnp.where(lanes() < 64, columns, 0.0).astype(BF)
         ar[0] = jnp.zeros_like(ar.at[0])
+        br[0] = jnp.zeros_like(br.at[0])
+        g1[...] = jnp.zeros_like(g1)
         count = jnp.sum(valid[...].astype(F32), axis=1, keepdims=True)
         ar[0, 7:8, 0:128] = jnp.broadcast_to(count, (1, 128))
         wide = jnp.concatenate([wo_in[...].astype(F32), jnp.zeros((64, 96), F32)], 0)
@@ -566,15 +607,14 @@
                 s = rows_of(i, 512)
                 tt[t, s, :] = dot(n1[s, :], w).astype(BF)
 
-            after(n, 0, m_in[1].s1)
-            after(n, 1, o_in.s3, m_in[1].s2, m_in[3].s1)
-            after(n, 2, o_in.s4)
-            after(n, 3, m_in[0].s4, m_in[2].s2, m_in[5].s1)
+            after(n, 1, m_in[1].s2, m_in[2].s1)
+            after(n, 2, m_in[0].s3)
+            after(n, 3, o_in.s4, m_in[2].s2, m_in[5].s1)
             attend(tt, ll, kx, k2, cc, t, length)
-            after(n, 0, *[g.s4 for g in q_in], *[g.near for g in q_in], m_in[0].s2, m_in[2].s1)
-            after(n, 1, m_in[0].s3, m_in[4].s1)
-            after(n, 2, *[g.far for g in q_in], m_in[1].s3)
-            after(n, 3, o_in.s5, m_in[3].s2, m_in[1].s4)
+            after(n, 0, *[g.s4 for g in q_in], *[g.near for g in q_in], m_in[0].s2)
+            after(n, 1, o_in.s3, m_in[3].s1)
+            after(n, 2, *[g.far for g in q_in], m_in[1].s3, m_in[4].s1)
+            after(n, 3, m_in[0].s4, m_in[3].s2, m_in[1].s4, o_in.s5)
 
     @phase
     def out_projection():
@@ -600,16 +640,22 @@
                 up = weight(b, t, 0, 96, slice(0, 256))
                 down = weight(b, t, 96, 96, slice(0, 256))
 
-                for i in range(length // 512):
-                    s = slice(512 * i, 512 * i + 512)
-                    v = dot(n2[s, :], up)
-                    ga = dot(cot[s, :], down)
+                def finish(s, v, ga):
                     v2 = v * v
                     th = jnp.tanh(v * (C0 + C1 * v2))
                     h = 0.5 + 0.5 * th
                     act[t, s, :] = (v * h).astype(BF)
                     slope = h + (0.5 * v) * (1.0 - th * th) * (C0 + (3.0 * C1) * v2)
                     gu[t, s, :] = (ga * slope).astype(BF)
+
+                waiting = None
+                for i in range(length // 128):
+                    s = slice(128 * i, 128 * i + 128)
+                    now = (s, dot(n2[s, :], up), dot(cot[s, :], down))
+                    if waiting is not None:
+                        finish(*waiting)
+                    waiting = now
+                finish(*waiting)
 
                 for k, step in enumerate(steps):
                     after(t, k, *step)
@@ -641,12 +687,11 @@
         sums()
 
     def mlp_weight_grads(j):
-        b = bm[j]
+        b = grads[j]
 
         @phase
         def weight_grads():
-            @pl.loop(0, 4)
-            def _(t):
+            for t in range(4):
                 gup = dot(n2[...], gu[t], TN).astype(BF)
                 b[t // 2, t % 2, :, :, 0:96, :] = gup.reshape(4, 2, 96, 256)
                 gdown = dot(cot[...], act[t], TN).astype(BF)
@@ -690,44 +735,57 @@
         def _(t):
             w = weight(bo, t, 0, 96, slice(0, 256))
             act[t] = dot(n2[...], w).astype(BF)
-            bo[t // 2, t % 2] = dot(n2[...], cc[t], TN).astype(BF).reshape(4, 2, 96, 256)
+            grad = dot(n2[...], cc[t], TN)
+            bm2[t // 2, t % 2, :, :, 0:96, 0:128] = grad[:, 0:128].astype(BF).reshape(4, 2, 96, 128)
+            bm2[t // 2, t % 2, :, :, 96:144, 0:128] = fold(grad[:, 128:192])
 
     @phase
     def pair_attention_back():
         @pl.loop(0, 4)
         def _(t):
-            attend_back(tt, ll, kx, k2, cc, act, (dk, dv), (0, 1), t, length)
-            after(t, 0, o_sum.s2, m_sum[2].s3)
-            after(t, 1, m_sum[1].s5, m_sum[1].give_credit, o_sum.s3)
-            after(t, 2, m_sum[2].s4)
-            after(t, 3, o_sum.s4)
+            attend_back(tt, ll, kx, k2, kt, cc, act, (dk, dv), (0, 1), t, length)
+            after(t, 0, o_sum.s2, m_sum[2].s3, early_take_0)
+            after(t, 1, o_sum.s3)
+            after(t, 2, m_sum[1].s5, m_sum[1].give_credit, early_take_1)
+            after(t, 3, m_sum[2].s4)
+
+    def early_take_0():
+        early.take(0)
+        early.run(1)
+
+    def early_take_1():
+        early.take(1)
+        early.left()
 
     @phase
     def pair_weight_grads():
-        @pl.loop(0, 4)
-        def _(t):
-            grad = dot(n1[...], tt[t, :, 0:384], TN).astype(BF)
-            x, c = t // 2, t % 2
-            bm0[x, c, :, :, 0:96, :] = grad[:, 0:256].reshape(4, 2, 96, 256)
-            third = grad[:, 256:384].reshape(4, 2, 96, 128)
-            bm0[x, c, :, :, 96:144, 0:128] = third[:, :, 0:48]
-            bm0[x, c, :, :, 96:144, 128:256] = third[:, :, 48:96]
+        @pl.loop(0, 2)
+        def _(x):
+            both = jnp.concatenate([tt[2 * x, :, 0:384], tt[2 * x + 1, :, 0:384]], 1)
+            grads = dot(n1[...], both, TN).astype(BF)
+            for c in range(2):
+                grad = grads[:, 384 * c : 384 * c + 384]
+                gb[x, c, :, :, 0:96, :] = grad[:, 0:256].reshape(4, 2, 96, 256)
+                third = grad[:, 256:384].reshape(4, 2, 96, 128)
+                gb[x, c, :, :, 96:144, 0:128] = third[:, :, 0:48]
+                gb[x, c, :, :, 96:144, 128:256] = third[:, :, 48:96]
 
     @phase
     def odd_weight_grads():
         @pl.loop(0, 4)
         def _(t):
-            grad = dot(n1[...], tt[t, :, 384:640], TN).astype(BF)
-            bm1[t // 2, t % 2, :, :, 0:96, :] = grad.reshape(4, 2, 96, 256)
+            grad = dot(n1[...], tt[t, :, 384:640], TN)
+            bm2[t // 2, t % 2, :, :, 0:96, 128:256] = grad[:, 0:128].astype(BF).reshape(4, 2, 96, 128)
+            bm2[t // 2, t % 2, :, :, 96:144, 128:256] = fold(grad[:, 128:192])
 
     @phase
     def odd_attention_back():
         @pl.loop(0, 4)
         def _(t):
-            attend_back(tt, ll, kx, k2, cc, act, (dk, dv), (2,), t, length)
-            after(t, 0, qa_sum.s2, o_sum.s5)
-            after(t, 1, m_sum[2].s5, m_sum[2].give_credit)
+            attend_back(tt, ll, kx, k2, kt, cc, act, (dk, dv), (2,), t, length)
+            after(t, 0, qa_sum.s2)
             after(t, 2, qa_sum.s3)
+            after(t, 3, m_sum[2].s5)
 
     def store_grad():
         return pltpu.make_async_copy(acc, gt_out, local_sem.at[4])
@@ -737,45 +795,50 @@
         @pl.loop(0, length // 256)
         def _(i):
             s = rows_of(i, 256)
-            grad = jnp.zeros((256, width), F32)
-            for t in range(4):
-                grad = grad + dot(tt[t, s, :], weight(bq, t, 0, 96, slice(0, 640)), NT)
+            w = jnp.concatenate([weight(bq, t, 0, 96, slice(0, 640)) for t in range(4)], 1)
+            grad = dot(cat(tt, s), w, NT)
             back, g_gain, g_bias = norm_back(tok[s, :].astype(F32), grad, par[64:65, :])
-            ar[0, 0:1, :] += g_gain
-            ar[0, 1:2, :] += g_bias
+            g1[0:1, :] += g_gain
+            g1[1:2, :] += g_bias
             acc[s, :] = mid[s, :] + back
-            after(i, 0, qb_sum.s2)
-            after(i, 1, qa_sum.s4)
-            after(i, 2, qb_sum.s3)
+            after(i, 0, qa_sum.s4, qb_sum.s2, qc_sum.s2)
+            after(i, 2, qb_sum.s3, qc_sum.s3)
 
         store_grad().start()
+        for k in range(width // 128):
+            for n in range(2):
+                br[0, 6 * n + k : 6 * n + k + 1, :] = g1[n : n + 1, 128 * k : 128 * k + 128]
 
     @phase
     def small_results():
-        sums = ar[2]
+        rows = [jnp.concatenate([br[2, 6 * n + k : 6 * n + k + 1, :] for k in range(6)], 1) for n in range(2)]
+        sums = jnp.concatenate(rows + [ar[2, 2:8, :]], 0)
         if inner > 1:
-            small_outs[0][...] = sums
+            small_out[...] = sums
             return
         share = width // 32
         owner = lax.axis_index("fsdp") * 4 + lax.axis_index("tp")
         moved = pltpu.roll(sums, width - owner * share, 1)
-        for k in range(4):
-            small_outs[k][...] = moved[k, 0:share]
         square = jnp.sum(sums[4:7], axis=1, keepdims=True) / (sums[7:8, 0:1] * width)
         rms = jnp.sqrt(jnp.broadcast_to(square, (3, 128)))
         lane = lanes()
         row = jnp.where(lane == 0, rms[0:1], jnp.where(lane == 1, rms[1:2], rms[2:3]))
-        small_outs[4][...] = row[0, 0:3]
+        small_out[0:4, :] = moved[0:4, 0:128]
+        small_out[4:8, :] = jnp.broadcast_to(row, (4, 128))
+
+    def give(k):
+        held = (gq_out, go_out, gup_out, gdown_out, small_out)[k]
+        return pltpu.make_async_copy(held, big_outs[k], give_sem.at[k])
 
     entry()
-    for g in q_in:
-        g.s1()
+    q_in[0].s1()
     document_marks()
-    own = own_copies()
-    for one in own:
+    for one in own_copies():
         one.wait()
+    q_in[1].s1()
     first_norm_statistics()
     q_in[0].s2()
+    q_in[2].s1()
     q_in[1].s2()
     q_in[0].s3()
     q_in[2].s2()
@@ -785,73 +848,86 @@
     q_in[2].s3()
     first_norm()
     o_in.s2()
+    m_in[1].s1()
     attention()
     out_projection()
     m_in[0].s5()
     m_in[1].s5()
 
-    mlp_hidden(0, (m_in[2].s3,), (m_in[4].s2,), (m_in[3].s3,))
-    mlp_sums(0, (m_in[2].s4, m_in[5].s2), (m_in[4].s3,), (m_in[3].s4,))
+    mlp_hidden(0, (m_in[2].s3,), (), (m_in[3].s3,))
+    m_in[4].s2()
+    mlp_weight_grads(0)
+    m_sum[0].s1()
+    m_in[2].s4()
+    m_in[5].s2()
+    mlp_sums(0, (), (m_in[3].s4,), (m_sum[0].s2,))
+    m_in[4].s3()
+    m_in[2].s5()
+    m_in[3].s5()
+
+    mlp_hidden(1, (), (m_in[5].s3,), (m_sum[0].s3,))
     m_in[0].s6()
     m_in[1].s6()
-    mlp_weight_grads(0)
-    m_in[5].s3()
-    m_sum[0].s1()
-    m_in[2].s5()
-    m_in[3].s5()
-
-    mlp_hidden(1, (m_in[4].s4,), (), (m_sum[0].s2,))
+    m_in[4].s4()
+    mlp_weight_grads(1)
+    m_sum[1].s1()
     m_in[5].s4()
-    mlp_sums(1)
-    m_sum[0].s3()
+    mlp_sums(1, (), (), (m_sum[1].s2,))
+    m_sum[0].s4()
+    m_in[4].s5()
+    m_in[5].s5()
+
+    mlp_hidden(2)
+    m_sum[1].s3()
     m_in[2].s6()
     m_in[3].s6()
-    m_in[4].s5()
-    m_in[5].s5()
-    mlp_weight_grads(1)
-    m_sum[1].s1()
-
-    mlp_hidden(2, (), (), (m_sum[1].s2,))
-    m_sum[0].s4()
-    mlp_sums(2)
-    m_sum[1].s3()
+    mlp_weight_grads(2)
+    m_sum[2].s1()
+    mlp_sums(2, (), (), (m_sum[2].s2, m_sum[0].s5, m_sum[0].give_credit))
     m_in[4].s6()
     m_in[5].s6()
-    mlp_weight_grads(2)
-    m_sum[2].s1()
 
     second_norm_back()
-    m_sum[2].s2()
-    m_sum[0].s5()
-    m_sum[0].give_credit()
+    m_sum[1].s4()
+    early.run(0)
     o_in.s6()
     out_projection_back()
-    m_sum[1].s4()
     m_sum[0].take_credit()
     o_sum.s1()
     pair_attention_back()
     pair_weight_grads()
     m_sum[1].take_credit()
     qa_sum.s1()
+    o_sum.s4()
     odd_attention_back()
     odd_weight_grads()
-    m_sum[2].take_credit()
     qb_sum.s1()
+    qc_sum.s1()
     for g in q_in:
         g.s6()
+    give(2).start()
+    give(3).start()
     first_norm_back()
-    total.run(0)
-    total.take(0)
-    total.run(1)
+    late.run(0)
+    o_sum.s5()
+    give(1).start()
     qb_sum.s4()
+    qc_sum.s4()
+    late.take(0)
+    late.run(1)
     qa_sum.s5()
-    total.take(1)
-    total.left()
+    late.take(1)
+    late.left()
     small_results()
+    give(4).start()
+    qb_sum.s5()
     for one in store_low():
         one.wait()
     store_grad().wait()
-    qb_sum.s5()
+    qc_sum.s5()
+    give(0).start()
+    for k in range(5):
+        give(k).wait()
 
 
 def scatter_slots(rows, columns):
@@ -868,8 +944,11 @@
 def layer(inner, tokens, cotangent, segments, valid, wq, wo, up, down, params):
     length, width = tokens.shape
     block = lambda rows, columns: pltpu.VMEM((2, 2, 4, 2, rows, columns), BF)
-    scratch = [
-        block(96, 640), block(96, 256), block(192, 256), block(192, 256), block(192, 256),
+    small = (8, width) if inner > 1 else (8, 128)
+    shapes = [(3, 96, 3 * HD), (3 * HD, 96), (96, width), (96, width), small]
+    scratch = [pltpu.VMEM(shape, F32) for shape in shapes]
+    scratch += [
+        block(96, 640), block(96, 256), block(192, 256), block(192, 256), block(192, 256), block(192, 256),
         pltpu.VMEM((length, width), BF),
         pltpu.VMEM((length, width), BF),
         pltpu.VMEM((length, width), BF),
@@ -878,6 +957,7 @@
         pltpu.VMEM((4, length, 128), BF),
         pltpu.VMEM((length, 128), BF),
         pltpu.VMEM((length, 128), BF),
+        pltpu.VMEM((128, length), BF),
         pltpu.VMEM((length, width), F32),
         pltpu.VMEM((length, width), BF),
         pltpu.VMEM((length, width), F32),
@@ -892,19 +972,21 @@
     scratch += [
         pltpu.VMEM((3, 8, width), F32),
         pltpu.VMEM((10, 8, width), F32),
+        pltpu.VMEM((3, 16, 128), F32),
+        pltpu.VMEM((10, 16, 128), F32),
+        pltpu.VMEM((8, width), F32),
         pltpu.SemaphoreType.DMA((10, 11)),
         pltpu.SemaphoreType.DMA((10, 11)),
-        pltpu.SemaphoreType.DMA((6, 8)),
-        pltpu.SemaphoreType.DMA((6, 8)),
-        pltpu.SemaphoreType.REGULAR((3, 6)),
-        pltpu.SemaphoreType.DMA((10,)),
-        pltpu.SemaphoreType.DMA((10,)),
+        pltpu.SemaphoreType.DMA((7, 8)),
+        pltpu.SemaphoreType.DMA((7, 8)),
+        pltpu.SemaphoreType.REGULAR((2, 6)),
+        pltpu.SemaphoreType.DMA((2, 10)),
+        pltpu.SemaphoreType.DMA((2, 10)),
         pltpu.SemaphoreType.DMA((5,)),
         pltpu.SemaphoreType.DMA((8,)),
+        pltpu.SemaphoreType.DMA((5,)),
     ]
     vmem, anywhere = pl.BlockSpec(memory_space=pltpu.VMEM), pl.BlockSpec(memory_space=pl.ANY)
-    small = [(8, width)] if inner > 1 else [(width // 32,)] * 4 + [(3,)]
-    shapes = [(3, 96, 3 * HD), (3 * HD, 96), (96, width), (96, width)] + small
     return pl.pallas_call(
         partial(kernel, inner, length),
         out_shape=[
@@ -913,7 +995,7 @@
         ]
         + [jax.ShapeDtypeStruct(shape, F32) for shape in shapes],
         in_specs=[anywhere, anywhere, vmem, vmem, vmem, vmem, anywhere, anywhere, vmem],
-        out_specs=[anywhere, anywhere] + [vmem] * len(shapes),
+        out_specs=[anywhere] * (2 + len(shapes)),
         scratch_shapes=scratch,
         compiler_params=pltpu.CompilerParams(
             collective_id=0, has_side_effects=True, vmem_limit_bytes=63 * 2**20
@@ -921,40 +1003,61 @@
     )(tokens, cotangent, segments, valid, wq, wo, up, down, params)
 
 
-def hand_over(arrays):
+def hand_over(arrays, share):
     count = len(arrays)
     pieces = []
     for k, a in enumerate(arrays):
         step = 256 if a.ndim == 2 and a.shape[0] % 256 == 0 else a.shape[0]
         pieces += [(k, start, step) for start in range(0, a.shape[0], step)]
+    small = [(share,)] * 4 + [(3,)] if share else []
+    shapes = [(a.shape, a.dtype) for a in arrays[: count - 1 if small else count]] + [(cut, F32) for cut in small]
+    whole = len(shapes) - len(small)
 
     def body(*refs):
-        came, went, held = refs[:count], refs[count : 2 * count], refs[2 * count : 3 * count]
-        sems = refs[-1]
-
-        def copy(n, into):
-            k, start, step = pieces[n]
-            part = (lambda ref: ref.at[pl.ds(start, step)]) if step < came[k].shape[0] else (lambda ref: ref)
-            if into:
-                return pltpu.make_async_copy(part(came[k]), part(held[k]), sems.at[0, n])
-            return pltpu.make_async_copy(part(held[k]), part(went[k]), sems.at[1, n])
-
+        came, went = refs[:count], refs[count : count + len(shapes)]
+        held = refs[count + len(shapes) : 2 * count + len(shapes)]
+        cuts, sems = refs[2 * count + len(shapes) : -1], refs[-1]
+
+        def part(ref, n):
+            _, start, step = pieces[n]
+            return ref.at[pl.ds(start, step)] if step < ref.shape[0] else ref
+
+        def fetch(n):
+            k = pieces[n][0]
+            return pltpu.make_async_copy(part(came[k], n), part(held[k], n), sems.at[0, n])
+
+        def put(n):
+            k = pieces[n][0]
+            return pltpu.make_async_copy(part(held[k], n), part(went[k], n), sems.at[1, n])
+
+        def put_cut(k):
+            return pltpu.make_async_copy(cuts[k], went[whole + k], sems.at[1, len(pieces) + k])
+
+        for n in reversed(range(len(pieces))):
+            fetch(n).start()
+        for n in reversed(range(len(pieces))):
+            fetch(n).wait()
+            if pieces[n][0] < whole:
+                put(n).start()
+                continue
+            for k, cut in enumerate(small):
+                cuts[k][...] = held[whole][k, 0 : cut[0]]
+                put_cut(k).start()
         for n in range(len(pieces)):
-            copy(n, True).start()
-        for n in range(len(pieces)):
-            copy(n, True).wait()
-            copy(n, False).start()
-        for n in range(len(pieces)):
-            copy(n, False).wait()
+            if pieces[n][0] < whole:
+                put(n).wait()
+        for k in range(len(small)):
+            put_cut(k).wait()
 
     anywhere = pl.BlockSpec(memory_space=pltpu.HBM)
     return pl.pallas_call(
         body,
-        out_shape=[jax.ShapeDtypeStruct(a.shape, a.dtype) for a in arrays],
+        out_shape=[jax.ShapeDtypeStruct(shape, dtype) for shape, dtype in shapes],
         in_specs=[anywhere] * count,
-        out_specs=[anywhere] * count,
+        out_specs=[anywhere] * len(shapes),
         scratch_shapes=[pltpu.VMEM(a.shape, a.dtype) for a in arrays]
-        + [pltpu.SemaphoreType.DMA((2, len(pieces)))],
+        + [pltpu.VMEM(cut, F32) for cut in small]
+        + [pltpu.SemaphoreType.DMA((2, len(pieces) + 5))],
         compiler_params=pltpu.CompilerParams(vmem_limit_bytes=63 * 2**20),
     )(*arrays)
 
@@ -984,7 +1087,7 @@
         inner, tokens, cotangent, segment_ids, valid.reshape(1, length),
         widen(w_qkv.transpose(1, 0, 2), 1), widen(w_out, 1), widen(w_up), widen(w_down.T), params,
     )
-    low, grad_tokens, gq, go, gup, gdown, *small = hand_over(results)
+    low, grad_tokens, gq, go, gup, gdown, *small = hand_over(results, width // 32 if inner == 1 else 0)
     if inner > 1:
         sums = lax.psum(small[0], "fsdp", axis_index_groups=groups)
         share = width // (holders * lax.axis_size("tp"))

time: 187 us -> 170 us (0.909)
  Pallas kernels: 184 us -> 168 us
    pallas_call x1, Pallas kernels: 179 us -> 163 us  [layer(): pl.pallas_call(partial(kernel, inner, length), out_shape=[jax.ShapeDtypeS...]
where the time goes in v4:
time: 170 us
  Pallas kernels  168 us (99%)
    pallas_call x1, Pallas kernels, layer(): pl.pallas_call(partial(kernel, inner, length), out_shape=[jax.ShapeDtypeS...  163 us
    pallas_call x1, Pallas kernels, hand_over(): pl.pallas_call(body, out_shape=[jax.ShapeDtypeStruct(shape, dtype) for sh...  5.12 us

profile of v4, /device:TPU:0, one launch (start us, length us, event | category | flops | bytes accessed | tf_op | source)
XLA Modules:
  0.0 170.0 jit_solution(5335796432566200627)
XLA Ops:
  0.6 1.3 maximum_convert_fusion.par_in
  1.9 162.7 %shard_map.203 = (bf16[1024,768]{1,0:T(8,128)(2,1)}, f32[1024,768]{1,0:T(8,128)}, f32[3,96,192]{2,1,0:T(8,128)}, f32[192,96]{1,0:T(8,128)}, f32[96,768]{1,0:T(8,...) custom-call(bf16[1024,768]{1,0:T(8,128)(2,1)} %tok_in.1, bf16[1024,768]{1,0:T(8,128)(2,1)} %cot_in.1, s32[4,1024]{1,0:T(4,128)} %seg.1, ...), custom_call_target="tpu_custom_call" | custom-call | tf_op jit(solution)/shard_map/pallas_call | solution.py:990
  164.7 5.1 %shard_map.204 = (bf16[1024,768]{1,0:T(8,128)(2,1)}, f32[1024,768]{1,0:T(8,128)}, f32[3,96,192]{2,1,0:T(8,128)}, f32[192,96]{1,0:T(8,128)}, f32[96,768]{1,0:T(8,...) custom-call(bf16[1024,768]{1,0:T(8,128)(2,1)} %get-tuple-element.29., ...), custom_call_target="tpu_custom_call" | custom-call | tf_op jit(solution)/shard_map/pallas_call | solution.py:1053

commit v5 on v4

--- a/solution.py
+++ b/solution.py
@@ -113,50 +113,66 @@
         yy = y if slot in (7, 8) else 1 - y
         return self.group(xx, c, yy), self.group(xx, 1 - c, yy), p.core()
 
+    SENT = (0, 0, 0, 1, 1, 2, 2, 1, 2, 2, 2)
+    CAME = (0, 0, 0, 1, 2, 3, 3, 4, 5, 4, 5)
+
     def start(self, *slots):
         for slot in slots:
             mine, _, dev = self.parts(slot)
-            remote(mine, mine, self.send.at[slot], self.recv.at[slot], dev).start()
-
-    def arrive(self, *slots):
-        for slot in slots:
-            _, theirs, dev = self.parts(slot)
-            remote(theirs, theirs, self.send.at[slot], self.recv.at[slot], dev).wait_recv()
-
-    def left(self, *slots):
-        for slot in slots:
-            mine, _, dev = self.parts(slot)
-            remote(mine, mine, self.send.at[slot], self.recv.at[slot], dev).wait_send()
+            remote(mine, mine, self.send.at[self.SENT[slot]], self.recv.at[self.CAME[slot]], dev).start()
+
+    def bytes_of(self, blocks):
+        rows = pl.ds(self.row0, self.rows)
+        if blocks == 3:
+            return self.buf.at[0, 0, 0:3, 0, rows]
+        if blocks == 4:
+            return self.buf.at[0, 0, :, 0, rows]
+        if blocks == 8:
+            return self.buf.at[0, 0, :, :, rows]
+        if blocks == 12:
+            return self.buf.at[:, :, 0:3, 0, rows]
+        return self.buf.at[0, :, :, :, rows]
+
+    def arrive(self, group):
+        ref = self.bytes_of((3, 4, 4, 4, 8, 8)[group])
+        dev = Place(self.inner).core()
+        remote(ref, ref, self.send.at[0], self.recv.at[group], dev).wait_recv()
+
+    def left(self):
+        for group, blocks in enumerate((3, 12, 16)):
+            ref = self.bytes_of(blocks)
+            dev = Place(self.inner).core()
+            remote(ref, ref, self.send.at[group], self.recv.at[0], dev).wait_send()
 
     def s1(self):
         self.start(0, 1, 2)
 
     def s2(self):
-        self.arrive(0, 1, 2)
+        self.arrive(0)
         self.start(3, 4, 7)
 
     def s3(self):
+        self.arrive(2)
+        self.start(6, 9)
+        self.arrive(1)
+        self.start(5, 8)
+
+    def s4(self):
+        self.arrive(3)
+        self.start(10)
+
+    def near(self):
         self.arrive(4)
-        self.start(6, 9)
-        self.arrive(3)
-        self.start(5, 8)
-
-    def s4(self):
-        self.arrive(5, 6)
-        self.start(10)
-
-    def near(self):
-        self.arrive(7, 9)
 
     def far(self):
-        self.arrive(8, 10)
+        self.arrive(5)
 
     def s5(self):
         self.near()
         self.far()
 
     def s6(self):
-        self.left(*range(11))
+        self.left()
 
 
 class Scatter:
@@ -198,20 +214,33 @@
         start, end = self.row0, self.row0 + self.rows
         return slice(start, end), slice(start, start + self.half), slice(start + self.half, end)
 
+    SENT = (0, 1, 1, 1, 1, 2, 2, 2)
+    CAME = (0, 1, 2, 3, 3, 4, 4, 4)
+
     def start(self, *slots):
         for slot in slots:
             src, dst, dev = self.parts(slot)
-            remote(src, dst, self.send.at[slot], self.recv.at[slot], dev).start()
-
-    def arrive(self, *slots):
-        for slot in slots:
-            _, dst, dev = self.parts(slot)
-            remote(dst, dst, self.send.at[slot], self.recv.at[slot], dev).wait_recv()
+            remote(src, dst, self.send.at[self.SENT[slot]], self.recv.at[self.CAME[slot]], dev).start()
+
+    def arrive(self, group):
+        land, _, _, cols = self.land
+        if group < 3:
+            ref = self.parts(group)[1]
+        elif group == 3:
+            ref = self.slots[0].at[0, :, :, land, cols]
+        else:
+            ref = self.slots[5].at[:, land, cols]
+        remote(ref, ref, self.send.at[0], self.recv.at[group], Place(self.inner).core()).wait_recv()
 
     def left(self):
-        for slot in range(8):
-            src, dst, dev = self.parts(slot)
-            remote(src, dst, self.send.at[slot], self.recv.at[slot], dev).wait_send()
+        rows, cols = self.spans()[0], self.cols
+        refs = (
+            self.buf.at[:, 0, :, :, rows, cols], self.buf.at[:, :, 0:3, 0, rows, cols],
+            self.buf.at[0, 0, 0:3, 0, rows, cols],
+        )
+        for group, ref in enumerate(refs):
+            dev = Place(self.inner).core()
+            remote(ref, ref, self.send.at[group], self.recv.at[0], dev).wait_send()
 
     def take_credit(self):
         for i in range(6):
@@ -260,7 +289,7 @@
         p = Place(self.inner)
         land, _, _, cols = self.land
         rx, ry = self.slots[3:5]
-        self.arrive(3, 4)
+        self.arrive(3)
         self.add(p.x, p.y, self.spans()[0], lambda z: rx[z, land, cols], lambda z: ry[z, land, cols])
         self.start(5, 6, 7)
 
@@ -268,7 +297,7 @@
         p = Place(self.inner)
         land, _, _, cols = self.land
         rz = self.slots[5]
-        self.arrive(5, 6, 7)
+        self.arrive(4)
         total = self.buf[p.x, p.c, p.z, p.y, self.spans()[0], self.cols].astype(F32)
         for d in range(3):
             total = total + rz[d, land, cols].astype(F32)
@@ -285,25 +314,30 @@
         p = Place(self.inner)
         dev = p.cube(slot + 1) if slot < 7 else p.zn(slot - 6)
         stage = 0 if slot < 7 else 1
-        return remote(self.ref.at[stage], self.got.at[slot], self.send.at[slot], self.recv.at[slot], dev)
+        return remote(self.ref.at[stage], self.got.at[slot], self.send.at[stage], self.recv.at[stage], dev)
 
     def slots(self, stage):
         return range(7) if stage == 0 else range(7, 10)
+
+    def all_of(self, stage):
+        span = self.slots(stage)
+        ref = self.got.at[span.start : span.stop]
+        return remote(ref, ref, self.send.at[stage], self.recv.at[stage], Place(self.inner).core())
 
     def run(self, stage):
         for slot in self.slots(stage):
             self.copy(slot).start()
 
     def take(self, stage):
+        self.all_of(stage).wait_recv()
         total = self.ref[stage]
         for slot in self.slots(stage):
-            self.copy(slot).wait_recv()
             total = total + self.got[slot]
         self.ref[stage + 1] = total
 
     def left(self):
-        for slot in range(10):
-            self.copy(slot).wait_send()
+        for stage in range(2):
+            self.all_of(stage).wait_send()
 
 
 def head_parts(t_ref, k2_ref, t, h, qs, kr):
@@ -438,7 +472,7 @@
 
 def kernel(
     inner, length,
-    tok_in, cot_in, seg, valid, wq_in, wo_in, up_in, down_in, par_in,
+    tok_in, cot_in, seg, valid, wq_in, wo_in, up_in, down_in, par_a, par_b, par_c, par_d,
     lo_out, gt_out, *rest,
 ):
     big_outs = rest[0:5]
@@ -447,7 +481,7 @@
         bq, bo, bm0, bm1, bm2, gb,
         tok, cot, n1, tt, cc, ll, kx, k2, kt, mid, n2, acc, gn, act, gu, val, par,
         dk, dv,
-        m_sets, ar, ar_got, br, br_got, g1,
+        m_sets, o_set, ar, ar_got, br, br_got, g1,
         ag_send, ag_recv, rs_send, rs_recv, credit, ar_send, ar_recv, local_sem, own_sem, give_sem,
     ) = rest[5:]
     width = tok.shape[1]
@@ -496,15 +530,15 @@
         (gb, (0, 192, 0, 256), sets[0], start, put_mlp(0)),
         (bm0, (0, 192, 0, 256), sets[1], start, put_mlp(1)),
         (bm1, (0, 192, 0, 256), sets[2], start, put_mlp(2)),
-        (bm2, (0, 144, 0, 128), sets[0], start, put_out),
-        (gb, (0, 144, 0, 256), sets[1], start, put_pair),
-        (bm2, (0, 80, 128, 128), sets[0], (0, 0, 0, 128), put_odd),
-        (bm2, (80, 64, 128, 128), sets[0], (80, 48, 32, 128), put_rest),
+        (bm2, (0, 144, 0, 128), o_set, start, put_out),
+        (gb, (0, 144, 0, 256), sets[0], start, put_pair),
+        (bm2, (0, 80, 128, 128), o_set, (0, 0, 0, 128), put_odd),
+        (bm2, (80, 64, 128, 128), o_set, (80, 48, 32, 128), put_rest),
     ]
     scatters = [
         Scatter(
             f"scatter{k}", inner, b, block, slots, place,
-            rs_send.at[k], rs_recv.at[k], credit.at[min(k, 1)], out,
+            rs_send.at[k], rs_recv.at[k], credit.at[0], out,
         )
         for k, (b, block, slots, place, out) in enumerate(plan)
     ]
@@ -552,7 +586,7 @@
             bq[(*mine, slice(None), slice(128 * n, 128 * n + 128))] = one[:, 0:128]
         odd = [one[:, 128:192].astype(F32) for one in (q, k, v)]
         bq[(*mine, slice(None), slice(384, 512))] = jnp.concatenate(odd[0:2], 1).astype(BF)
-        params = jnp.concatenate([par_in[...], jnp.zeros((124, 96), F32)], 0).T[:, 0:64]
+        params = jnp.concatenate([one[...].astype(F32) for one in (par_a, par_b, par_c, par_d)] + [jnp.zeros((124, 96), F32)], 0).T[:, 0:64]
         bq[(*mine, slice(None), slice(512, 640))] = jnp.concatenate([odd[2], params], 1).astype(BF)
         met(inner)
 
@@ -608,13 +642,12 @@
                 tt[t, s, :] = dot(n1[s, :], w).astype(BF)
 
             after(n, 1, m_in[1].s2, m_in[2].s1)
-            after(n, 2, m_in[0].s3)
-            after(n, 3, o_in.s4, m_in[2].s2, m_in[5].s1)
+            after(n, 3, m_in[1].s3, m_in[2].s2, m_in[5].s1)
             attend(tt, ll, kx, k2, cc, t, length)
             after(n, 0, *[g.s4 for g in q_in], *[g.near for g in q_in], m_in[0].s2)
             after(n, 1, o_in.s3, m_in[3].s1)
-            after(n, 2, *[g.far for g in q_in], m_in[1].s3, m_in[4].s1)
-            after(n, 3, m_in[0].s4, m_in[3].s2, m_in[1].s4, o_in.s5)
+            after(n, 2, m_in[0].s3, *[g.far for g in q_in], m_in[4].s1)
+            after(n, 3, o_in.s4, m_in[3].s2, m_in[0].s4, o_in.s5)
 
     @phase
     def out_projection():
@@ -744,9 +777,8 @@
         @pl.loop(0, 4)
         def _(t):
             attend_back(tt, ll, kx, k2, kt, cc, act, (dk, dv), (0, 1), t, length)
-            after(t, 0, o_sum.s2, m_sum[2].s3, early_take_0)
-            after(t, 1, o_sum.s3)
-            after(t, 2, m_sum[1].s5, m_sum[1].give_credit, early_take_1)
+            after(t, 0, m_sum[2].s3, m_sum[1].s4)
+            after(t, 1, o_sum.s2, early_take_0)
             after(t, 3, m_sum[2].s4)
 
     def early_take_0():
@@ -783,9 +815,10 @@
         @pl.loop(0, 4)
         def _(t):
             attend_back(tt, ll, kx, k2, kt, cc, act, (dk, dv), (2,), t, length)
-            after(t, 0, qa_sum.s2)
+            after(t, 0, qa_sum.s2, early_take_1)
+            after(t, 1, m_sum[1].s5)
             after(t, 2, qa_sum.s3)
-            after(t, 3, m_sum[2].s5)
+            after(t, 3, o_sum.s4)
 
     def store_grad():
         return pltpu.make_async_copy(acc, gt_out, local_sem.at[4])
@@ -797,12 +830,13 @@
             s = rows_of(i, 256)
             w = jnp.concatenate([weight(bq, t, 0, 96, slice(0, 640)) for t in range(4)], 1)
             grad = dot(cat(tt, s), w, NT)
+            after(i, 2, qb_sum.s3, qc_sum.s3)
             back, g_gain, g_bias = norm_back(tok[s, :].astype(F32), grad, par[64:65, :])
             g1[0:1, :] += g_gain
             g1[1:2, :] += g_bias
             acc[s, :] = mid[s, :] + back
-            after(i, 0, qa_sum.s4, qb_sum.s2, qc_sum.s2)
-            after(i, 2, qb_sum.s3, qc_sum.s3)
+            after(i, 0, qb_sum.s2, qc_sum.s2)
+            after(i, 1, qa_sum.s4)
 
         store_grad().start()
         for k in range(width // 128):
@@ -851,58 +885,59 @@
     m_in[1].s1()
     attention()
     out_projection()
+    m_in[1].s4()
     m_in[0].s5()
     m_in[1].s5()
 
-    mlp_hidden(0, (m_in[2].s3,), (), (m_in[3].s3,))
+    mlp_hidden(0, (), (m_in[2].s3,), (), (m_in[3].s3,))
     m_in[4].s2()
     mlp_weight_grads(0)
     m_sum[0].s1()
     m_in[2].s4()
     m_in[5].s2()
-    mlp_sums(0, (), (m_in[3].s4,), (m_sum[0].s2,))
-    m_in[4].s3()
+    mlp_sums(0, (), (), (m_in[3].s4,))
+    m_sum[0].s2()
     m_in[2].s5()
     m_in[3].s5()
 
-    mlp_hidden(1, (), (m_in[5].s3,), (m_sum[0].s3,))
+    mlp_hidden(1, (), (m_in[4].s3,), (), (m_in[5].s3,))
     m_in[0].s6()
     m_in[1].s6()
-    m_in[4].s4()
     mlp_weight_grads(1)
     m_sum[1].s1()
-    m_in[5].s4()
-    mlp_sums(1, (), (), (m_sum[1].s2,))
-    m_sum[0].s4()
+    mlp_sums(1, (m_sum[0].s3,), (m_in[4].s4,), (), (m_in[5].s4,))
+    m_sum[1].s2()
     m_in[4].s5()
     m_in[5].s5()
 
     mlp_hidden(2)
-    m_sum[1].s3()
     m_in[2].s6()
     m_in[3].s6()
     mlp_weight_grads(2)
     m_sum[2].s1()
-    mlp_sums(2, (), (), (m_sum[2].s2, m_sum[0].s5, m_sum[0].give_credit))
+    m_sum[0].s4()
+    mlp_sums(2, (), (m_sum[1].s3,))
+    m_sum[2].s2()
     m_in[4].s6()
     m_in[5].s6()
 
     second_norm_back()
-    m_sum[1].s4()
     early.run(0)
     o_in.s6()
     out_projection_back()
-    m_sum[0].take_credit()
     o_sum.s1()
+    m_sum[0].s5()
+    m_sum[0].give_credit()
     pair_attention_back()
     pair_weight_grads()
-    m_sum[1].take_credit()
+    o_sum.s3()
+    m_sum[0].take_credit()
     qa_sum.s1()
-    o_sum.s4()
     odd_attention_back()
     odd_weight_grads()
     qb_sum.s1()
     qc_sum.s1()
+    m_sum[2].s5()
     for g in q_in:
         g.s6()
     give(2).start()
@@ -941,7 +976,7 @@
     ]
 
 
-def layer(inner, tokens, cotangent, segments, valid, wq, wo, up, down, params):
+def layer(inner, tokens, cotangent, segments, valid, wq, wo, up, down, *params):
     length, width = tokens.shape
     block = lambda rows, columns: pltpu.VMEM((2, 2, 4, 2, rows, columns), BF)
     small = (8, width) if inner > 1 else (8, 128)
@@ -968,20 +1003,20 @@
         pltpu.VMEM((128, width), F32),
     ]
     scratch += [pltpu.VMEM((length, 128), F32)] * 2
-    scratch += [scatter_slots(192, 256) * 3]
+    scratch += [scatter_slots(192, 256) * 3, scatter_slots(144, 256)]
     scratch += [
         pltpu.VMEM((3, 8, width), F32),
         pltpu.VMEM((10, 8, width), F32),
         pltpu.VMEM((3, 16, 128), F32),
         pltpu.VMEM((10, 16, 128), F32),
         pltpu.VMEM((8, width), F32),
-        pltpu.SemaphoreType.DMA((10, 11)),
-        pltpu.SemaphoreType.DMA((10, 11)),
-        pltpu.SemaphoreType.DMA((7, 8)),
-        pltpu.SemaphoreType.DMA((7, 8)),
-        pltpu.SemaphoreType.REGULAR((2, 6)),
-        pltpu.SemaphoreType.DMA((2, 10)),
-        pltpu.SemaphoreType.DMA((2, 10)),
+        pltpu.SemaphoreType.DMA((10, 3)),
+        pltpu.SemaphoreType.DMA((10, 6)),
+        pltpu.SemaphoreType.DMA((7, 3)),
+        pltpu.SemaphoreType.DMA((7, 5)),
+        pltpu.SemaphoreType.REGULAR((1, 6)),
+        pltpu.SemaphoreType.DMA((2, 2)),
+        pltpu.SemaphoreType.DMA((2, 2)),
         pltpu.SemaphoreType.DMA((5,)),
         pltpu.SemaphoreType.DMA((8,)),
         pltpu.SemaphoreType.DMA((5,)),
@@ -994,13 +1029,13 @@
             jax.ShapeDtypeStruct((length, width), F32),
         ]
         + [jax.ShapeDtypeStruct(shape, F32) for shape in shapes],
-        in_specs=[anywhere, anywhere, vmem, vmem, vmem, vmem, anywhere, anywhere, vmem],
+        in_specs=[anywhere, anywhere, vmem, vmem, vmem, vmem, anywhere, anywhere] + [vmem] * 4,
         out_specs=[anywhere] * (2 + len(shapes)),
         scratch_shapes=scratch,
         compiler_params=pltpu.CompilerParams(
             collective_id=0, has_side_effects=True, vmem_limit_bytes=63 * 2**20
         ),
-    )(tokens, cotangent, segments, valid, wq, wo, up, down, params)
+    )(tokens, cotangent, segments, valid, wq, wo, up, down, *params)
 
 
 def hand_over(arrays, share):
@@ -1082,10 +1117,10 @@
             block, "fsdp", scatter_dimension=axis, axis_index_groups=groups, tiled=True
         )
 
-    params = widen(jnp.stack([ln1_gain, ln1_bias, ln2_gain, ln2_bias]), 1).astype(F32)
+    params = [widen(one.reshape(1, -1), 1) for one in (ln1_gain, ln1_bias, ln2_gain, ln2_bias)]
     results = layer(
         inner, tokens, cotangent, segment_ids, valid.reshape(1, length),
-        widen(w_qkv.transpose(1, 0, 2), 1), widen(w_out, 1), widen(w_up), widen(w_down.T), params,
+        widen(w_qkv.transpose(1, 0, 2), 1), widen(w_out, 1), widen(w_up), widen(w_down.T), *params,
     )
     low, grad_tokens, gq, go, gup, gdown, *small = hand_over(results, width // 32 if inner == 1 else 0)
     if inner > 1:

time: 170 us -> 161 us (0.947)
  Pallas kernels: 168 us -> 160 us
    pallas_call x1, Pallas kernels: 163 us -> 155 us  [layer(): pl.pallas_call(partial(kernel, inner, length), out_shape=[jax.ShapeDtypeS...]
where the time goes in v5:
time: 161 us
  Pallas kernels  160 us (99%)
    pallas_call x1, Pallas kernels, layer(): pl.pallas_call(partial(kernel, inner, length), out_shape=[jax.ShapeDtypeS...  155 us
    pallas_call x1, Pallas kernels, hand_over(): pl.pallas_call(body, out_shape=[jax.ShapeDtypeStruct(shape, dtype) for sh...  5.12 us

profile of v5, /device:TPU:0, one launch (start us, length us, event | category | flops | bytes accessed | tf_op | source)
XLA Modules:
  0.0 161.0 jit_solution(12310465729401790624)
XLA Ops:
  0.6 155.0 %shard_map.203 = (bf16[1024,768]{1,0:T(8,128)(2,1)}, f32[1024,768]{1,0:T(8,128)}, f32[3,96,192]{2,1,0:T(8,128)}, f32[192,96]{1,0:T(8,128)}, f32[96,768]{1,0:T(8,...) custom-call(bf16[1024,768]{1,0:T(8,128)(2,1)} %tok_in.1, bf16[1024,768]{1,0:T(8,128)(2,1)} %cot_in.1, s32[4,1024]{1,0:T(4,128)} %seg.1, ...), custom_call_target="tpu_custom_call" | custom-call | tf_op jit(solution)/shard_map/pallas_call | solution.py:1025
  155.7 5.1 %shard_map.204 = (bf16[1024,768]{1,0:T(8,128)(2,1)}, f32[1024,768]{1,0:T(8,128)}, f32[3,96,192]{2,1,0:T(8,128)}, f32[192,96]{1,0:T(8,128)}, f32[96,768]{1,0:T(8,...) custom-call(bf16[1024,768]{1,0:T(8,128)(2,1)} %get-tuple-element.29., ...), custom_call_target="tpu_custom_call" | custom-call | tf_op jit(solution)/shard_map/pallas_call | solution.py:1088

commit v6 on v5

--- a/solution.py
+++ b/solution.py
@@ -64,6 +64,10 @@
     def zn(self, d):
         return self.device((self.z + d) % 4, self.y, self.x, self.c)
 
+    def reach(self, k):
+        upper = self.z // 2
+        return (3 - k) * (1 - upper) + (1 + k) * upper
+
     def zp(self, d):
         return self.device((self.z - d + 4) % 4, self.y, self.x, self.c)
 
@@ -91,16 +95,16 @@
     def group(self, x, c, y, half=None):
         start, size = self.row0, self.rows
         if half is not None:
-            size = self.rows // 2
-            start = self.row0 + half * size
+            cut = (size // 2 + 15) // 16 * 16
+            start, size = (start + cut, size - cut) if half else (start, cut)
         return self.buf.at[x, c, :, y, pl.ds(start, size)]
 
     def parts(self, slot):
         p = Place(self.inner)
         x, c, z, y = p.x, p.c, p.z, p.y
         if slot < 3:
-            d = slot + 1
-            return self.own(x, c, z, y), self.own(x, c, (z - d + 4) % 4, y), p.zn(d)
+            mine = self.own(x, c, z, y)
+            return mine, mine, p.zn(p.reach(slot))
         if slot == 3:
             return self.group(x, c, y), self.group(1 - x, c, y), p.xn()
         if slot == 4:
@@ -207,7 +211,7 @@
             return buf.at[1 - x, c, :, y, rows, cols], rx.at[:, land, land_cols], p.xn()
         if slot == 4:
             return buf.at[x, c, :, 1 - y, rows, cols], ry.at[:, land, land_cols], p.yn()
-        d = slot - 4
+        d = p.reach(slot - 5)
         return buf.at[x, c, (z + d) % 4, y, rows, cols], rz.at[d - 1, land, land_cols], p.zn(d)
 
     def spans(self):
@@ -259,9 +263,11 @@
 
         @pl.loop(0, 4)
         def _(z):
-            total = self.buf[x, c, z, y, rows, self.cols].astype(F32)
+            total = self.buf[x, c, z, y, rows, self.cols]
+            if len(others) > 1:
+                total = total.astype(F32)
             for other in others:
-                total = total + other(z).astype(F32)
+                total = total + other(z).astype(total.dtype)
             self.buf[x, c, z, y, rows, self.cols] = total.astype(BF)
 
     def s2(self):
@@ -354,9 +360,9 @@
     k2_ref[...] = pltpu.roll(t_ref[t, :, 384:512].astype(F32), 64, 1).astype(BF)
 
 
-def below(transposed):
-    r = lax.broadcasted_iota(jnp.int32, (BQ, BQ), 0)
-    c = lax.broadcasted_iota(jnp.int32, (BQ, BQ), 1)
+def below(transposed, size=BQ):
+    r = lax.broadcasted_iota(jnp.int32, (size, size), 0)
+    c = lax.broadcasted_iota(jnp.int32, (size, size), 1)
     return r <= c if transposed else r >= c
 
 
@@ -400,6 +406,7 @@
     low = lane < 64
     dk_ref, dv_ref = sums
     odd = heads == (2,)
+    size = BQ
     if odd:
         roll_key(t_ref, k2_ref, t)
         kt_ref[...] = k2_ref[...].T
@@ -407,10 +414,10 @@
         kt_ref[...] = t_ref[t, :, 128:256].T
     for ref in sums:
         ref[...] = jnp.zeros_like(ref)
-    for i in range(length // BQ):
-        first = max(0, i * BQ - length // 2)
-        width = (i + 1) * BQ - first
-        qs, kr = slice(i * BQ, (i + 1) * BQ), slice(first, first + width)
+    for i in range(length // size):
+        first = max(0, i * size - length // 2)
+        width = (i + 1) * size - first
+        qs, kr = slice(i * size, (i + 1) * size), slice(first, first + width)
         marks = l_ref[t, qs, :]
         side = slice(128, 256) if odd else slice(0, 128)
         qs_all, dos, left, right = [], [], [], []
@@ -430,16 +437,16 @@
         dp_all = dot(jnp.concatenate([v, minus], 1), jnp.concatenate(right, 0), NT)
         ps, dss, grads = [], [], []
         for n in range(len(heads)):
-            s = s_all[:, n * BQ : (n + 1) * BQ]
-            edge = jnp.where(below(True), s[width - BQ :], BIG)
-            s = edge if width == BQ else jnp.concatenate([s[: width - BQ], edge], 0)
+            s = s_all[:, n * size : (n + 1) * size]
+            edge = jnp.where(below(True, size), s[width - size :], BIG)
+            s = edge if width == size else jnp.concatenate([s[: width - size], edge], 0)
             p = jnp.exp(s)
-            ds = (p * dp_all[:, n * BQ : (n + 1) * BQ]).astype(BF)
+            ds = (p * dp_all[:, n * size : (n + 1) * size]).astype(BF)
             ps.append(p.astype(BF))
             dss.append(ds)
             grads.append(dot(kt_ref[64 * n : 64 * n + 64, kr], ds))
         if odd:
-            grads.append(jnp.zeros((64, BQ), F32))
+            grads.append(jnp.zeros((64, size), F32))
         grad = (jnp.concatenate(grads, 0).T * HD ** -0.5).astype(BF)
         dv_ref[kr, :] += dot(jnp.concatenate(ps, 1), jnp.concatenate(dos, 0))
         dk_ref[kr, :] += dot(jnp.concatenate(dss, 1), jnp.concatenate(qs_all, 0))
@@ -479,14 +486,14 @@
     (
         gq_out, go_out, gup_out, gdown_out, small_out,
         bq, bo, bm0, bm1, bm2, gb,
-        tok, cot, n1, tt, cc, ll, kx, k2, kt, mid, n2, acc, gn, act, gu, val, par,
+        tok, cot, n1, tt, cc, ll, kx, k2, kt, wo, mid, n2, acc, gn, act, gu, val, par,
         dk, dv,
         m_sets, o_set, ar, ar_got, br, br_got, g1,
         ag_send, ag_recv, rs_send, rs_recv, credit, ar_send, ar_recv, local_sem, own_sem, give_sem,
     ) = rest[5:]
     width = tok.shape[1]
     bm = (bm0, bm1, bm2)
-    blocks = [(bq, 0, 32), (bq, 32, 32), (bq, 64, 32), (bo, 0, 96)]
+    blocks = [(bq, 0, 32), (bq, 32, 32), (bq, 64, 32), (bo, 0, 144)]
     blocks += [(b, r0, 96) for b in bm for r0 in (0, 96)]
     gathers = [
         Gather(f"gather{k}", inner, b, r0, rows, ag_send.at[k], ag_recv.at[k])
@@ -508,10 +515,14 @@
         go_out[2 * HD : 3 * HD] = jnp.concatenate([third[0:64], third[64:128]], 1)
 
     def put_pair(total):
-        gq_out[0, :, 0:128] = total[0:96, 0:128]
-        gq_out[1, :, 0:128] = total[0:96, 128:256]
-        gq_out[2, 0:48, 0:128] = total[96:144, 0:128]
-        gq_out[2, 48:96, 0:128] = total[96:144, 128:256]
+        gq_out[0, 0:80, 0:128] = total[:, 0:128]
+        gq_out[1, 0:80, 0:128] = total[:, 128:256]
+
+    def put_pair_rest(total):
+        gq_out[0, 80:96, 0:128] = total[0:16, 0:128]
+        gq_out[1, 80:96, 0:128] = total[0:16, 128:256]
+        gq_out[2, 0:48, 0:128] = total[16:64, 0:128]
+        gq_out[2, 48:96, 0:128] = total[16:64, 128:256]
 
     def put_odd(total):
         gq_out[0, 0:80, 128:192] = total[:, 0:64]
@@ -531,7 +542,8 @@
         (bm0, (0, 192, 0, 256), sets[1], start, put_mlp(1)),
         (bm1, (0, 192, 0, 256), sets[2], start, put_mlp(2)),
         (bm2, (0, 144, 0, 128), o_set, start, put_out),
-        (gb, (0, 144, 0, 256), sets[0], start, put_pair),
+        (gb, (0, 80, 0, 256), sets[0], start, put_pair),
+        (gb, (80, 64, 0, 256), sets[0], (80, 48, 32, 0), put_pair_rest),
         (bm2, (0, 80, 128, 128), o_set, (0, 0, 0, 128), put_odd),
         (bm2, (80, 64, 128, 128), o_set, (80, 48, 32, 128), put_rest),
     ]
@@ -542,7 +554,7 @@
         )
         for k, (b, block, slots, place, out) in enumerate(plan)
     ]
-    m_sum, o_sum, qa_sum, qb_sum, qc_sum = scatters[0:3], *scatters[3:7]
+    m_sum, o_sum, qa_sum, qd_sum, qb_sum, qc_sum = scatters[0:3], *scatters[3:8]
     q_in, o_in, m_in = gathers[0:3], gathers[3], gathers[4:10]
     early = Total("early", inner, ar, ar_got, ar_send.at[0], ar_recv.at[0])
     late = Total("late", inner, br, br_got, ar_send.at[1], ar_recv.at[1])
@@ -609,8 +621,10 @@
         g1[...] = jnp.zeros_like(g1)
         count = jnp.sum(valid[...].astype(F32), axis=1, keepdims=True)
         ar[0, 7:8, 0:128] = jnp.broadcast_to(count, (1, 128))
-        wide = jnp.concatenate([wo_in[...].astype(F32), jnp.zeros((64, 96), F32)], 0)
-        bo[mine] = wide.T.astype(BF)
+        wide = jnp.concatenate([wo_in[...].astype(F32), jnp.zeros((64, 96), F32)], 0).T
+        third = wide[:, 128:192]
+        bo[(*mine, slice(0, 96))] = wide[:, 0:128].astype(BF)
+        bo[(*mine, slice(96, 144))] = jnp.concatenate([third[0:48], third[48:96]], 1).astype(BF)
 
     @phase
     def first_norm_statistics():
@@ -649,14 +663,22 @@
             after(n, 2, m_in[0].s3, *[g.far for g in q_in], m_in[4].s1)
             after(n, 3, o_in.s4, m_in[3].s2, m_in[0].s4, o_in.s5)
 
+    def out_weight(t):
+        return jnp.concatenate([weight(bo, t, 0, 96, slice(0, 128)), wo[t]], 1)
+
     @phase
     def out_projection():
+        for t in range(4):
+            third = bo[t // 2, t % 2, :, :, 96:144, :].reshape(8, 48, 128)
+            turned = pltpu.roll(third.astype(F32).reshape(8 * 48, 128), 64, 1).astype(BF)
+            wo[t] = jnp.concatenate([third, turned.reshape(8, 48, 128)], 1).reshape(width, 128)
+
         @pl.loop(0, length // 256)
         def _(i):
             s = rows_of(i, 256)
             branch = jnp.zeros((256, width), F32)
             for t in range(4):
-                branch = branch + dot(cc[t, s, :], weight(bo, t, 0, 96, slice(0, 256)), NT)
+                branch = branch + dot(cc[t, s, :], out_weight(t), NT)
             v = tok[s, :].astype(F32) + branch
             mid[s, :] = v
             ar[0, 5:6, :] += jnp.sum(val[s, :] * (branch * branch), 0, keepdims=True)
@@ -703,9 +725,9 @@
 
         @phase
         def sums():
-            @pl.loop(0, length // 256)
+            @pl.loop(0, length // 512)
             def _(i):
-                s = rows_of(i, 256)
+                s = rows_of(i, 512)
                 one = dot(cat(act, s), wcat(96), NT)
                 two = dot(cat(gu, s), wcat(0), NT)
                 if j == 0:
@@ -719,7 +741,7 @@
 
         sums()
 
-    def mlp_weight_grads(j):
+    def mlp_weight_grads(j, *steps):
         b = grads[j]
 
         @phase
@@ -729,6 +751,8 @@
                 b[t // 2, t % 2, :, :, 0:96, :] = gup.reshape(4, 2, 96, 256)
                 gdown = dot(cot[...], act[t], TN).astype(BF)
                 b[t // 2, t % 2, :, :, 96:192, :] = gdown.reshape(4, 2, 96, 256)
+                for step in steps[t : t + 1]:
+                    step()
 
         weight_grads()
 
@@ -766,8 +790,7 @@
     def out_projection_back():
         @pl.loop(0, 4)
         def _(t):
-            w = weight(bo, t, 0, 96, slice(0, 256))
-            act[t] = dot(n2[...], w).astype(BF)
+            act[t] = dot(n2[...], out_weight(t)).astype(BF)
             grad = dot(n2[...], cc[t], TN)
             bm2[t // 2, t % 2, :, :, 0:96, 0:128] = grad[:, 0:128].astype(BF).reshape(4, 2, 96, 128)
             bm2[t // 2, t % 2, :, :, 96:144, 0:128] = fold(grad[:, 128:192])
@@ -777,9 +800,8 @@
         @pl.loop(0, 4)
         def _(t):
             attend_back(tt, ll, kx, k2, kt, cc, act, (dk, dv), (0, 1), t, length)
-            after(t, 0, m_sum[2].s3, m_sum[1].s4)
-            after(t, 1, o_sum.s2, early_take_0)
-            after(t, 3, m_sum[2].s4)
+            after(t, 0, o_sum.s2)
+            after(t, 1, m_sum[1].s4)
 
     def early_take_0():
         early.take(0)
@@ -815,10 +837,10 @@
         @pl.loop(0, 4)
         def _(t):
             attend_back(tt, ll, kx, k2, kt, cc, act, (dk, dv), (2,), t, length)
-            after(t, 0, qa_sum.s2, early_take_1)
-            after(t, 1, m_sum[1].s5)
-            after(t, 2, qa_sum.s3)
-            after(t, 3, o_sum.s4)
+            after(t, 0, qa_sum.s2)
+            after(t, 1, qd_sum.s2, m_sum[1].s5, early_take_0)
+            after(t, 2, qa_sum.s3, o_sum.s4)
+            after(t, 3, qd_sum.s3)
 
     def store_grad():
         return pltpu.make_async_copy(acc, gt_out, local_sem.at[4])
@@ -835,8 +857,8 @@
             g1[0:1, :] += g_gain
             g1[1:2, :] += g_bias
             acc[s, :] = mid[s, :] + back
-            after(i, 0, qb_sum.s2, qc_sum.s2)
-            after(i, 1, qa_sum.s4)
+            after(i, 0, qb_sum.s2, qc_sum.s2, qa_sum.s4)
+            after(i, 1, qd_sum.s4)
 
         store_grad().start()
         for k in range(width // 128):
@@ -895,17 +917,17 @@
     m_sum[0].s1()
     m_in[2].s4()
     m_in[5].s2()
-    mlp_sums(0, (), (), (m_in[3].s4,))
+    mlp_sums(0, (m_in[3].s4,))
     m_sum[0].s2()
     m_in[2].s5()
     m_in[3].s5()
 
-    mlp_hidden(1, (), (m_in[4].s3,), (), (m_in[5].s3,))
+    mlp_hidden(1, (), (m_in[4].s3,))
     m_in[0].s6()
     m_in[1].s6()
-    mlp_weight_grads(1)
+    mlp_weight_grads(1, lambda: None, m_in[5].s3)
     m_sum[1].s1()
-    mlp_sums(1, (m_sum[0].s3,), (m_in[4].s4,), (), (m_in[5].s4,))
+    mlp_sums(1, (m_sum[0].s3,), (m_in[4].s4, m_in[5].s4))
     m_sum[1].s2()
     m_in[4].s5()
     m_in[5].s5()
@@ -916,8 +938,9 @@
     mlp_weight_grads(2)
     m_sum[2].s1()
     m_sum[0].s4()
-    mlp_sums(2, (), (m_sum[1].s3,))
+    mlp_sums(2)
     m_sum[2].s2()
+    m_sum[1].s3()
     m_in[4].s6()
     m_in[5].s6()
 
@@ -926,13 +949,16 @@
     o_in.s6()
     out_projection_back()
     o_sum.s1()
+    m_sum[2].s3()
     m_sum[0].s5()
     m_sum[0].give_credit()
     pair_attention_back()
     pair_weight_grads()
+    m_sum[2].s4()
     o_sum.s3()
     m_sum[0].take_credit()
     qa_sum.s1()
+    qd_sum.s1()
     odd_attention_back()
     odd_weight_grads()
     qb_sum.s1()
@@ -944,6 +970,7 @@
     give(3).start()
     first_norm_back()
     late.run(0)
+    early_take_1()
     o_sum.s5()
     give(1).start()
     qb_sum.s4()
@@ -951,6 +978,7 @@
     late.take(0)
     late.run(1)
     qa_sum.s5()
+    qd_sum.s5()
     late.take(1)
     late.left()
     small_results()
@@ -983,7 +1011,7 @@
     shapes = [(3, 96, 3 * HD), (3 * HD, 96), (96, width), (96, width), small]
     scratch = [pltpu.VMEM(shape, F32) for shape in shapes]
     scratch += [
-        block(96, 640), block(96, 256), block(192, 256), block(192, 256), block(192, 256), block(192, 256),
+        block(96, 640), block(144, 128), block(192, 256), block(192, 256), block(192, 256), block(192, 256),
         pltpu.VMEM((length, width), BF),
         pltpu.VMEM((length, width), BF),
         pltpu.VMEM((length, width), BF),
@@ -993,6 +1021,7 @@
         pltpu.VMEM((length, 128), BF),
         pltpu.VMEM((length, 128), BF),
         pltpu.VMEM((128, length), BF),
+        pltpu.VMEM((4, width, 128), BF),
         pltpu.VMEM((length, width), F32),
         pltpu.VMEM((length, width), BF),
         pltpu.VMEM((length, width), F32),
@@ -1012,8 +1041,8 @@
         pltpu.VMEM((8, width), F32),
         pltpu.SemaphoreType.DMA((10, 3)),
         pltpu.SemaphoreType.DMA((10, 6)),
-        pltpu.SemaphoreType.DMA((7, 3)),
-        pltpu.SemaphoreType.DMA((7, 5)),
+        pltpu.SemaphoreType.DMA((8, 3)),
+        pltpu.SemaphoreType.DMA((8, 5)),
         pltpu.SemaphoreType.REGULAR((1, 6)),
         pltpu.SemaphoreType.DMA((2, 2)),
         pltpu.SemaphoreType.DMA((2, 2)),

time: 161 us -> 159 us (0.988)
  Pallas kernels: 160 us -> 158 us
    pallas_call x1, Pallas kernels: 155 us -> 153 us  [layer(): pl.pallas_call(partial(kernel, inner, length), out_shape=[jax.ShapeDtypeS...]
where the time goes in v6:
time: 159 us; the launch traced here: 158 us
  Pallas kernels  158 us (99%)
    pallas_call x1, Pallas kernels, layer(): pl.pallas_call(partial(kernel, inner, length), out_shape=[jax.ShapeDtypeS...  153 us
    pallas_call x1, Pallas kernels, hand_over(): pl.pallas_call(body, out_shape=[jax.ShapeDtypeStruct(shape, dtype) for sh...  5.12 us

profile of v6, /device:TPU:0, one launch (start us, length us, event | category | flops | bytes accessed | tf_op | source)
XLA Modules:
  0.0 158.5 jit_solution(1597559500754395130)
XLA Ops:
  0.6 152.5 %shard_map.203 = (bf16[1024,768]{1,0:T(8,128)(2,1)}, f32[1024,768]{1,0:T(8,128)}, f32[3,96,192]{2,1,0:T(8,128)}, f32[192,96]{1,0:T(8,128)}, f32[96,768]{1,0:T(8,...) custom-call(bf16[1024,768]{1,0:T(8,128)(2,1)} %tok_in.1, bf16[1024,768]{1,0:T(8,128)(2,1)} %cot_in.1, s32[4,1024]{1,0:T(4,128)} %seg.1, ...), custom_call_target="tpu_custom_call" | custom-call | tf_op jit(solution)/shard_map/pallas_call | solution.py:1054
  153.2 5.1 %shard_map.204 = (bf16[1024,768]{1,0:T(8,128)(2,1)}, f32[1024,768]{1,0:T(8,128)}, f32[3,96,192]{2,1,0:T(8,128)}, f32[192,96]{1,0:T(8,128)}, f32[96,768]{1,0:T(8,...) custom-call(bf16[1024,768]{1,0:T(8,128)(2,1)} %get-tuple-element.29., ...), custom_call_target="tpu_custom_call" | custom-call | tf_op jit(solution)/shard_map/pallas_call | solution.py:1117

commit v7 on v6

--- a/solution.py
+++ b/solution.py
@@ -467,11 +467,11 @@
     mean = jnp.mean(v, axis=-1, keepdims=True)
     center = v - mean
     scale = lax.rsqrt(jnp.mean(center * center, axis=-1, keepdims=True) + EPS)
-    return center * scale, scale
-
-
-def norm_back(v, q, gain):
-    n, scale = stats(v)
+    return center * scale, mean, scale
+
+
+def norm_back(v, mean, scale, q, gain):
+    n = (v - mean) * scale
     e = q * gain
     back = scale * (e - jnp.mean(e, -1, keepdims=True) - n * jnp.mean(e * n, -1, keepdims=True))
     return back, jnp.sum(q * n, 0, keepdims=True), jnp.sum(q, 0, keepdims=True)
@@ -486,7 +486,7 @@
     (
         gq_out, go_out, gup_out, gdown_out, small_out,
         bq, bo, bm0, bm1, bm2, gb,
-        tok, cot, n1, tt, cc, ll, kx, k2, kt, wo, mid, n2, acc, gn, act, gu, val, par,
+        tok, cot, n1, tt, cc, ll, kx, k2, kt, wo, mid, n2, acc, gn, act, gu, val, kept, par,
         dk, dv,
         m_sets, o_set, ar, ar_got, br, br_got, g1,
         ag_send, ag_recv, rs_send, rs_recv, credit, ar_send, ar_recv, local_sem, own_sem, give_sem,
@@ -631,7 +631,10 @@
         @pl.loop(0, length // 256)
         def _(i):
             s = rows_of(i, 256)
-            mid[s, :] = stats(tok[s, :].astype(F32))[0]
+            n, mean, scale = stats(tok[s, :].astype(F32))
+            mid[s, :] = n
+            kept[s, 0:1] = mean
+            kept[s, 1:2] = scale
 
     @phase
     def first_norm():
@@ -682,7 +685,9 @@
             v = tok[s, :].astype(F32) + branch
             mid[s, :] = v
             ar[0, 5:6, :] += jnp.sum(val[s, :] * (branch * branch), 0, keepdims=True)
-            n, _ = stats(v)
+            n, mean, scale = stats(v)
+            kept[s, 2:3] = mean
+            kept[s, 3:4] = scale
             n2[s, :] = (n * par[66:67, :] + par[67:68, :]).astype(BF)
 
     def mlp_hidden(j, *steps):
@@ -776,7 +781,7 @@
             low_out = out.astype(BF)
             for k in range(width // 256):
                 gu[k, s, :] = low_out[:, 256 * k : 256 * k + 256]
-            back, g_gain, g_bias = norm_back(v, gn[s, :], par[66:67, :])
+            back, g_gain, g_bias = norm_back(v, kept[s, 2:3], kept[s, 3:4], gn[s, :], par[66:67, :])
             ar[0, 2:3, :] += g_gain
             ar[0, 3:4, :] += g_bias
             grad = cot[s, :].astype(F32) + back
@@ -837,10 +842,10 @@
         @pl.loop(0, 4)
         def _(t):
             attend_back(tt, ll, kx, k2, kt, cc, act, (dk, dv), (2,), t, length)
-            after(t, 0, qa_sum.s2)
+            after(t, 0, qa_sum.s2, o_sum.s3)
             after(t, 1, qd_sum.s2, m_sum[1].s5, early_take_0)
-            after(t, 2, qa_sum.s3, o_sum.s4)
-            after(t, 3, qd_sum.s3)
+            after(t, 2, qa_sum.s3)
+            after(t, 3, o_sum.s4)
 
     def store_grad():
         return pltpu.make_async_copy(acc, gt_out, local_sem.at[4])
@@ -853,12 +858,12 @@
             w = jnp.concatenate([weight(bq, t, 0, 96, slice(0, 640)) for t in range(4)], 1)
             grad = dot(cat(tt, s), w, NT)
             after(i, 2, qb_sum.s3, qc_sum.s3)
-            back, g_gain, g_bias = norm_back(tok[s, :].astype(F32), grad, par[64:65, :])
+            back, g_gain, g_bias = norm_back(tok[s, :].astype(F32), kept[s, 0:1], kept[s, 1:2], grad, par[64:65, :])
             g1[0:1, :] += g_gain
             g1[1:2, :] += g_bias
             acc[s, :] = mid[s, :] + back
             after(i, 0, qb_sum.s2, qc_sum.s2, qa_sum.s4)
-            after(i, 1, qd_sum.s4)
+            after(i, 2, qd_sum.s4)
 
         store_grad().start()
         for k in range(width // 128):
@@ -955,7 +960,6 @@
     pair_attention_back()
     pair_weight_grads()
     m_sum[2].s4()
-    o_sum.s3()
     m_sum[0].take_credit()
     qa_sum.s1()
     qd_sum.s1()
@@ -963,6 +967,7 @@
     odd_weight_grads()
     qb_sum.s1()
     qc_sum.s1()
+    qd_sum.s3()
     m_sum[2].s5()
     for g in q_in:
         g.s6()
@@ -1029,6 +1034,7 @@
         pltpu.VMEM((4, length, 256), BF),
         pltpu.VMEM((4, length, 256), BF),
         pltpu.VMEM((length, 1), F32),
+        pltpu.VMEM((length, 4), F32),
         pltpu.VMEM((128, width), F32),
     ]
     scratch += [pltpu.VMEM((length, 128), F32)] * 2

time: 159 us -> 157 us (0.987)
  Pallas kernels: 158 us -> 156 us
where the time goes in v7:
time: 157 us
  Pallas kernels  156 us (99%)
    pallas_call x1, Pallas kernels, layer(): pl.pallas_call(partial(kernel, inner, length), out_shape=[jax.ShapeDtypeS...  151 us
    pallas_call x1, Pallas kernels, hand_over(): pl.pallas_call(body, out_shape=[jax.ShapeDtypeStruct(shape, dtype) for sh...  5.12 us

profile of v7, /device:TPU:0, one launch (start us, length us, event | category | flops | bytes accessed | tf_op | source)
XLA Modules:
  0.0 157.3 jit_solution(17629270440486110294)
XLA Ops:
  0.6 151.3 %shard_map.203 = (bf16[1024,768]{1,0:T(8,128)(2,1)}, f32[1024,768]{1,0:T(8,128)}, f32[3,96,192]{2,1,0:T(8,128)}, f32[192,96]{1,0:T(8,128)}, f32[96,768]{1,0:T(8,...) custom-call(bf16[1024,768]{1,0:T(8,128)(2,1)} %tok_in.1, bf16[1024,768]{1,0:T(8,128)(2,1)} %cot_in.1, s32[4,1024]{1,0:T(4,128)} %seg.1, ...), custom_call_target="tpu_custom_call" | custom-call | tf_op jit(solution)/shard_map/pallas_call | solution.py:1060
  152.0 5.1 %shard_map.204 = (bf16[1024,768]{1,0:T(8,128)(2,1)}, f32[1024,768]{1,0:T(8,128)}, f32[3,96,192]{2,1,0:T(8,128)}, f32[192,96]{1,0:T(8,128)}, f32[96,768]{1,0:T(8,...) custom-call(bf16[1024,768]{1,0:T(8,128)(2,1)} %get-tuple-element.29., ...), custom_call_target="tpu_custom_call" | custom-call | tf_op jit(solution)/shard_map/pallas_call | solution.py:1123

commit v8 on v7

--- a/solution.py
+++ b/solution.py
@@ -653,10 +653,7 @@
             t = 2 * x + c
             w = bq[x, c].reshape(width, 640)
 
-            @pl.loop(0, length // 512)
-            def _(i):
-                s = rows_of(i, 512)
-                tt[t, s, :] = dot(n1[s, :], w).astype(BF)
+            tt[t] = dot(n1[...], w).astype(BF)
 
             after(n, 1, m_in[1].s2, m_in[2].s1)
             after(n, 3, m_in[1].s3, m_in[2].s2, m_in[5].s1)
@@ -842,7 +839,7 @@
         @pl.loop(0, 4)
         def _(t):
             attend_back(tt, ll, kx, k2, kt, cc, act, (dk, dv), (2,), t, length)
-            after(t, 0, qa_sum.s2, o_sum.s3)
+            after(t, 0, qa_sum.s2, o_sum.s3, m_sum[2].s4)
             after(t, 1, qd_sum.s2, m_sum[1].s5, early_take_0)
             after(t, 2, qa_sum.s3)
             after(t, 3, o_sum.s4)
@@ -959,7 +956,6 @@
     m_sum[0].give_credit()
     pair_attention_back()
     pair_weight_grads()
-    m_sum[2].s4()
     m_sum[0].take_credit()
     qa_sum.s1()
     qd_sum.s1()

time: 157 us -> 162 us (1.032)
  Pallas kernels: 156 us -> 161 us
    pallas_call x1, Pallas kernels: 151 us -> 155 us  [layer(): pl.pallas_call(partial(kernel, inner, length), out_shape=[jax.ShapeDtypeS...]
where the time goes in v8:
time: 162 us; the launch traced here: 161 us
  Pallas kernels  161 us (99%)
    pallas_call x1, Pallas kernels, layer(): pl.pallas_call(partial(kernel, inner, length), out_shape=[jax.ShapeDtypeS...  155 us
    pallas_call x1, Pallas kernels, hand_over(): pl.pallas_call(body, out_shape=[jax.ShapeDtypeStruct(shape, dtype) for sh...  5.12 us

profile of v8, /device:TPU:0, one launch (start us, length us, event | category | flops | bytes accessed | tf_op | source)
XLA Modules:
  0.0 161.3 jit_solution(9734323064793824409)
XLA Ops:
  0.6 155.4 %shard_map.203 = (bf16[1024,768]{1,0:T(8,128)(2,1)}, f32[1024,768]{1,0:T(8,128)}, f32[3,96,192]{2,1,0:T(8,128)}, f32[192,96]{1,0:T(8,128)}, f32[96,768]{1,0:T(8,...) custom-call(bf16[1024,768]{1,0:T(8,128)(2,1)} %tok_in.1, bf16[1024,768]{1,0:T(8,128)(2,1)} %cot_in.1, s32[4,1024]{1,0:T(4,128)} %seg.1, ...), custom_call_target="tpu_custom_call" | custom-call | tf_op jit(solution)/shard_map/pallas_call | solution.py:1056
  156.0 5.1 %shard_map.204 = (bf16[1024,768]{1,0:T(8,128)(2,1)}, f32[1024,768]{1,0:T(8,128)}, f32[3,96,192]{2,1,0:T(8,128)}, f32[192,96]{1,0:T(8,128)}, f32[96,768]{1,0:T(8,...) custom-call(bf16[1024,768]{1,0:T(8,128)(2,1)} %get-tuple-element.29., ...), custom_call_target="tpu_custom_call" | custom-call | tf_op jit(solution)/shard_map/pallas_call | solution.py:1119
